TPU v7x, 32 devices: a whole 2x2x4 slice. The times are simulated.
32 devices in a mesh: rep: 8 (over z, core), fsdp: 4 (over y, x).
Axes of the slice: x: 2, y: 2, z: 4, core: 2. Of those that a mesh axis runs over, the one named last changes fastest.
Arguments:
- tokens: bfloat16 [8192, 1536], P(('rep', 'fsdp')), may hold values from -6 to 6
- segment_ids: int32 [32, 256], P(('rep', 'fsdp')), may hold values from 0 to 3, never falling along the last dimension, each value on 1 to 128 neighbouring positions
- cotangent: bfloat16 [8192, 1536], P(('rep', 'fsdp')), may hold values from -6 to 6
- norm_gain: bfloat16 [1536], P('fsdp'), may hold values from 0.5 to 1.5
- in_weight: bfloat16 [1536, 6448], P('fsdp'), may hold values from -0.15625 to 0.15625
- conv_weight: bfloat16 [4, 3328], P(None, 'fsdp'), may hold values from -3 to 3
- conv_bias: bfloat16 [3328], P('fsdp'), may hold values from -0.5 to 0.5
- step_bias: bfloat16 [48], replicated, may hold values from -6 to -2
- rate_log: bfloat16 [48], replicated, may hold values from 0 to 2.5
- skip_gain: bfloat16 [48], replicated, may hold values from 0.5 to 2
- gate_gain: bfloat16 [3072], P('fsdp'), may hold values from 0.5 to 1.5
- out_weight: bfloat16 [3072, 1536], P('fsdp'), may hold values from -0.109375 to 0.109375
Outputs:
- output: bfloat16 [8192, 1536], P(('rep', 'fsdp'))
- tokens_grad: bfloat16 [8192, 1536], P(('rep', 'fsdp'))
- grad_norm: float32 [1536], P('fsdp')
- grad_inproj: float32 [1536, 6448], P('fsdp')
- grad_kernel: float32 [4, 3328], P(None, 'fsdp')
- grad_convbias: float32 [3328], P('fsdp')
- grad_step: float32 [48], replicated
- grad_rate: float32 [48], replicated
- grad_skip: float32 [48], replicated
- grad_gate: float32 [3072], P('fsdp')
- grad_outproj: float32 [3072, 1536], P('fsdp')
Inputs may be any that keep to these rules, and one draw needn't show every extreme that they name: `segment_ids`: in each row the ids never fall; each of the 4 ids covers 1 to 128 consecutive slots, and some id covers exactly 128.
All inputs are finite; a program needn't handle non-finite values.
Results may differ from a plain program's by a relative error of at most 0.0072.
Values may be sent and summed in bfloat16 or wider, within the bound.
No kernel may reach another device: no remote copies, remote signals or barrier semaphores. Data moves between devices by JAX's collectives and lax.ppermute only.
A program may use at most 256 MiB of HBM per device.

v0:
```python
from functools import partial

import jax
import jax.numpy as jnp
from jax import lax
from jax.experimental import pallas as pl
from jax.experimental.pallas import tpu as pltpu
from jax.sharding import PartitionSpec as P


HEADS = 48
HEADDIM = 64
KERNEL = 4
LANES = 128
EPSILON = 1e-05
BF = jnp.bfloat16
F32 = jnp.float32

NN = (((1,), (0,)), ((), ()))
NT = (((1,), (1,)), ((), ()))
TN = (((0,), (0,)), ((), ()))


def mm(a, b, dims):
    return lax.dot_general(a, b, dims, preferred_element_type=F32)


def halves(x):
    top = x.astype(BF)
    return top, (x - top.astype(F32)).astype(BF)


def mm_fine(a, b, dims):
    a_top, a_low = halves(a)
    b_top, b_low = halves(b)
    return mm(a_top, b_top, dims) + (mm(a_top, b_low, dims) + mm(a_low, b_top, dims))


def mm_ones(ones, x, dims):
    top, low = halves(x)
    rest = (x - top.astype(F32) - low.astype(F32)).astype(BF)
    parts = mm(ones, jnp.concatenate([top, low, rest], axis=1), dims)
    lanes = x.shape[1]
    return parts[:, :lanes] + (parts[:, lanes : 2 * lanes] + parts[:, 2 * lanes :])


def sigmoid(v):
    return 0.5 * jnp.tanh(0.5 * v) + 0.5


def silu_parts(v):
    gate = sigmoid(v)
    return v * gate, gate * (1.0 + v * (1.0 - gate))


def call(kernel, out_shape, flops, moved, mib=None, **kw):
    grant = (mib or 4 * lax.axis_size("fsdp")) * 1024 * 1024

    def run(*operands):
        return pl.pallas_call(
            kernel,
            out_shape=out_shape,
            cost_estimate=pl.CostEstimate(flops=flops, bytes_accessed=moved, transcendentals=0),
            compiler_params=pltpu.CompilerParams(vmem_limit_bytes=grant),
            **kw,
        )(*operands)

    return run


VM = pl.BlockSpec(memory_space=pltpu.VMEM)
HBM = pl.BlockSpec(memory_space=pl.ANY)


def pack_kernel(groups, *refs):
    place_ref, weight_ref, gain_ref, taps_ref, shift_ref, seg_ref = refs[:6]
    sends = refs[6 : 5 + groups]
    small_ref, sems = refs[5 + groups :]
    member, quarter = place_ref[0], place_ref[2]
    inner, share, edge, part, tail = quarter_sizes(sends[0].shape[0], weight_ref.shape[0], groups)
    copies = []
    for k in range(1, groups):
        peer = jnp.bitwise_xor(member, k)
        for i in range(2):
            source = pl.multiple_of(i * (edge // 2) + peer * inner + quarter * share, 16)
            copies.append(
                pltpu.make_async_copy(
                    weight_ref.at[pl.ds(source, share), :],
                    sends[k - 1].at[pl.ds(i * share, share), :],
                    sems.at[2 * k - 2 + i],
                )
            )
    for copy in copies:
        copy.start()
    for q in range(4):
        count = max(0, min(part, tail - q * part))

        @pl.when(quarter == q)
        def _():
            more = [
                pltpu.make_async_copy(
                    weight_ref.at[pl.ds(edge + q * part, count), :],
                    sends[k - 1].at[pl.ds(2 * share, count), :],
                    sems.at[2 * groups - 3 + k],
                )
                for k in range(1, groups)
                if count > 0
            ]
            for copy in more:
                copy.start()
            if count < part:
                for k in range(1, groups):
                    sends[k - 1][2 * share + count :, :] = jnp.zeros((part - count, weight_ref.shape[1]), BF)
            for copy in more:
                copy.wait()

    small_ref[...] = jnp.zeros_like(small_ref)
    small_ref[0:1, : gain_ref.shape[1]] = gain_ref[...].astype(F32)
    small_ref[1 : 1 + KERNEL, : taps_ref.shape[1]] = taps_ref[...].astype(F32)
    small_ref[1 + KERNEL : 2 + KERNEL, : shift_ref.shape[1]] = shift_ref[...].astype(F32)
    small_ref[2 + KERNEL : 3 + KERNEL, : seg_ref.shape[1]] = seg_ref[...].astype(F32)
    for copy in copies:
        copy.wait()


def copy_kernel(source_ref, target_ref):
    target_ref[...] = source_ref[...]


def quarter_sizes(sent, columns, groups):
    full = HEADS * HEADDIM
    inner = full // groups
    return inner, inner // 4, 2 * full, sent - inner // 2, columns - 2 * full


def inproj_kernel(groups, aligned, *refs):
    tokens = refs[:groups]
    gain_ref, place_ref, own_ref = refs[groups : groups + 3]
    given = refs[groups + 3 : -7]
    normed_ref, proj_ref, weight_out_ref, token_ref, weight_ref, sems, token_sems = refs[-7:]
    member, quarter = place_ref[0], place_ref[2]
    model = gain_ref.shape[1]
    rows = model // groups
    span = tokens[0].shape[0]
    loads = [pltpu.make_async_copy(tokens[r], token_ref.at[r], token_sems.at[r]) for r in range(groups)]
    for load in loads:
        load.start()
    copies = []
    if aligned:
        sent = given[0].shape[0] // (groups - 1)
        inner, share, edge, part, tail = quarter_sizes(sent, own_ref.shape[0], groups)
        for i, (source, count) in enumerate(
            ((member * inner, inner), (edge // 2 + member * inner, inner), (edge, tail))
        ):
            copies.append(
                pltpu.make_async_copy(
                    own_ref.at[pl.ds(pl.multiple_of(source, 16), count), :],
                    weight_ref.at[pl.ds(i * inner, count), pl.ds(0, rows)],
                    sems.at[i],
                )
            )
        for n, piece in enumerate(given):
            whose = jnp.bitwise_xor(quarter, n)
            for k in range(1, groups):
                for i, count in enumerate((share, share, part)):
                    target = pl.multiple_of(i * inner + whose * count, 16)
                    copies.append(
                        pltpu.make_async_copy(
                            piece.at[pl.ds((k - 1) * sent + i * share, count), :],
                            weight_ref.at[pl.ds(target, count), pl.ds(k * rows, rows)],
                            sems.at[len(copies)],
                        )
                    )
    else:
        copies.append(pltpu.make_async_copy(own_ref, weight_ref, sems.at[0]))
    for copy in copies:
        copy.start()
    if aligned and part * 4 > tail:
        weight_ref[2 * inner + tail :, 0:rows] = jnp.zeros((4 * part - tail, rows), BF)
    for r in range(groups):
        loads[r].wait()
        blocks = [token_ref[r, :, lane_block(aligned, member, k, rows)].astype(F32) for k in range(groups)]
        total = jnp.sum(blocks[0] * blocks[0], axis=-1, keepdims=True)
        for x in blocks[1:]:
            total = total + jnp.sum(x * x, axis=-1, keepdims=True)
        factor = lax.rsqrt(total / model + EPSILON)
        for k in range(groups):
            at = slice(k * rows, (k + 1) * rows)
            normed_ref[r * span : (r + 1) * span, at] = (blocks[k] * factor * gain_ref[:, at]).astype(BF)
    for copy in copies:
        copy.wait()
    keep = pltpu.make_async_copy(weight_ref, weight_out_ref, sems.at[0])
    keep.start()
    width = 384
    total = weight_ref.shape[0] // width

    def column(n, carry):
        at = pl.multiple_of(n * width, LANES)
        for r in range(groups):
            proj_ref[r * span : (r + 1) * span, pl.ds(at, width)] = mm(
                normed_ref[r * span : (r + 1) * span, :], weight_ref[pl.ds(at, width), :], NT
            )
        return carry

    lax.fori_loop(0, total, column, 0)
    keep.wait()


def lane_block(aligned, member, k, rows):
    if aligned:
        return pl.ds(pl.multiple_of(jnp.bitwise_xor(member, k) * rows, LANES), rows)
    return slice(k * rows, (k + 1) * rows)


def conv_forward(x, masks, taps, shift):
    total = shift + taps[KERNEL - 1] * x
    for s in range(1, KERNEL):
        total = total + taps[KERNEL - 1 - s] * (pltpu.roll(x, s, 0) * masks[s - 1])
    return total


def conv_backward(grad, x, masks, taps):
    span = x.shape[0]
    back = taps[KERNEL - 1] * grad
    tap_grads = [None] * KERNEL
    tap_grads[KERNEL - 1] = jnp.sum(grad * x, axis=0, keepdims=True)
    for s in range(1, KERNEL):
        part = grad * masks[s - 1]
        back = back + taps[KERNEL - 1 - s] * pltpu.roll(part, span - s, 0)
        tap_grads[KERNEL - 1 - s] = jnp.sum(part * pltpu.roll(x, s, 0), axis=0, keepdims=True)
    return back, tap_grads


def wide(column, count):
    return jnp.concatenate([column] * (count // LANES), axis=1)


def segment_masks(seg_ref):
    span = seg_ref.shape[-1]
    row = seg_ref[0:1, :]
    column = jnp.broadcast_to(row, (LANES, span)).T
    token = lax.broadcasted_iota(jnp.int32, (span, LANES), 0)
    masks = []
    for s in range(1, KERNEL):
        same = (pltpu.roll(column, s, 0) == column) & (token >= s)
        masks.append(jnp.where(same, 1.0, 0.0))
    return masks, wide(column, span), row


def ordered(span):
    i = lax.broadcasted_iota(jnp.int32, (span, span), 0)
    j = lax.broadcasted_iota(jnp.int32, (span, span), 1)
    return i >= j, i <= j


def row_setup(shared_ref, seg_ref, taps_ref, head_ref, member, per, affinity_ref, kept):
    mask_ref, afft_ref, step_ref, run_ref, runt_ref, raw_ref, act_ref, sum_ref = kept
    masks, column, row = segment_masks(seg_ref)
    after, _ = ordered(row.shape[1])
    for s in range(KERNEL - 1):
        mask_ref[:, s * LANES : (s + 1) * LANES] = masks[s]
    outs = []
    for c in range(2):
        at = slice(c * LANES, (c + 1) * LANES)
        taps = [taps_ref[k : k + 1, at] for k in range(KERNEL)]
        total = conv_forward(shared_ref[:, at], masks, taps, taps_ref[KERNEL : KERNEL + 1, at])
        active = total * sigmoid(total)
        outs.append(active)
        sum_ref[:, at] = total
        act_ref[:, at] = active
    affinity = jnp.where(after & (column == row), mm_fine(outs[1], outs[0], NT), 0.0)
    affinity_ref[...] = affinity
    afft_ref[...] = affinity.T
    raw = pltpu.roll(shared_ref[:, 2 * LANES :], lax.rem(LANES - member * per, LANES), 1)
    raw = raw + head_ref[0:1, :]
    step = jnp.maximum(raw, 0.0) + jnp.log1p(jnp.exp(-jnp.abs(raw)))
    run = mm_ones(jnp.where(after, 1.0, 0.0).astype(BF), -head_ref[1:2, :] * step, NN)
    raw_ref[...] = raw
    step_ref[...] = step
    run_ref[...] = run
    runt_ref[...] = run.T


def pair_columns(pair, run_ref, runt_ref, step_ref):
    back = lax.rem(LANES - 2 * pair, LANES)
    runs = pltpu.roll(run_ref[...], back, 1)
    steps = pltpu.roll(step_ref[...], back, 1)
    lane = lax.broadcasted_iota(jnp.int32, runs.shape, 1)
    low = lane < HEADDIM
    stepx = jnp.where(low, steps[:, 0:1], steps[:, 1:2])
    columns = [runs[:, e : e + 1] for e in range(2)]
    rows = [runt_ref[pl.ds(2 * pair + e, 1), :] for e in range(2)]
    return columns, rows, stepx, low, lane


def forward_kernel(
    per,
    place_ref,
    z_ref,
    v_ref,
    shared_ref,
    seg_ref,
    taps_s_ref,
    taps_v_ref,
    head_ref,
    scanned_ref,
    total_ref,
    gated_ref,
    square_ref,
    mask_ref,
    afft_ref,
    step_ref,
    run_ref,
    runt_ref,
    raw_ref,
    act_ref,
    sum_ref,
    affinity_ref,
    square_sum_ref,
):
    pair = pl.program_id(1)

    @pl.when(pair == 0)
    def _():
        kept = (mask_ref, afft_ref, step_ref, run_ref, runt_ref, raw_ref, act_ref, sum_ref)
        row_setup(shared_ref, seg_ref, taps_s_ref, head_ref, place_ref[0], per, affinity_ref, kept)
        square_sum_ref[...] = jnp.zeros_like(square_sum_ref)

    masks = [mask_ref[:, s * LANES : (s + 1) * LANES] for s in range(KERNEL - 1)]
    taps = [taps_v_ref[k : k + 1, :] for k in range(KERNEL)]
    total = conv_forward(v_ref[...], masks, taps, taps_v_ref[KERNEL : KERNEL + 1, :])
    total_ref[...] = total
    values = total * sigmoid(total)
    columns, rows, stepx, low, _ = pair_columns(pair, run_ref, runt_ref, step_ref)
    fed = (stepx * values).astype(BF)
    skipped = taps_v_ref[KERNEL + 1 : KERNEL + 2, :] * values
    cut = fed.shape[0] // 2
    for n in range(2):
        at = slice(n * cut, (n + 1) * cut)
        seen = (n + 1) * cut
        affinity = affinity_ref[at, :seen]
        parts = []
        for e in range(2):
            decay = jnp.exp(jnp.minimum(columns[e][at] - rows[e][:, :seen], 0.0))
            parts.append(mm((decay * affinity).astype(BF), fed[:seen], NN))
        scanned = jnp.where(low[at], parts[0], parts[1]) + skipped[at]
        z = z_ref[at, :]
        g = scanned * (z * sigmoid(z))
        scanned_ref[at, :] = scanned
        gated_ref[at, :] = (g * taps_v_ref[KERNEL + 2 : KERNEL + 3, :]).astype(BF)
        square_sum_ref[at, :] = square_sum_ref[at, :] + g * g

    @pl.when(pair == pl.num_programs(1) - 1)
    def _():
        row = jnp.sum(square_sum_ref[...].T, axis=0, keepdims=True)
        square_ref[...] = jnp.broadcast_to(row, square_ref.shape)


def mixgrad_kernel(groups, *refs):
    cots = refs[:groups]
    out_w_ref, gated_ref, square_ref, dm_ref, sums_ref = refs[groups:]
    span = cots[0].shape[0]
    width = 384 if out_w_ref.shape[0] % 384 == 0 else LANES

    def column(n, carry):
        cols = pl.ds(pl.multiple_of(n * width, LANES), width)
        weight = out_w_ref[cols, :]
        for r in range(groups):
            dm_ref[r * span : (r + 1) * span, cols] = mm(cots[r][...], weight, NT)
        return carry

    lax.fori_loop(0, out_w_ref.shape[0] // width, column, 0)
    for r in range(groups):
        at = slice(r * span, (r + 1) * span)
        prod = dm_ref[at, :] * gated_ref[at, :].astype(F32)
        part = prod[:, :LANES]
        for c in range(1, prod.shape[1] // LANES):
            part = part + prod[:, c * LANES : (c + 1) * LANES]
        row = jnp.sum(part.T, axis=0, keepdims=True)
        sub = lax.broadcasted_iota(jnp.int32, (8, span), 0)
        sums_ref[8 * r : 8 * r + 8, :] = jnp.where(sub == 0, square_ref[8 * r : 8 * r + 8, :], row)


def outproj_kernel(groups, gated_ref, out_w_ref, *outs):
    span, model = outs[0].shape
    width = 384 if model % 384 == 0 else LANES

    def column(n, carry):
        cols = pl.ds(pl.multiple_of(n * width, LANES), width)
        weight = out_w_ref[:, cols]
        for r in range(groups):
            outs[r][:, cols] = mm(gated_ref[r * span : (r + 1) * span, :], weight, NN).astype(outs[r].dtype)
        return carry

    lax.fori_loop(0, model // width, column, 0)


def gate_scales(parts, width):
    total = parts[0]
    for part in parts[1:]:
        total = total + part
    square, cross = total[0:1, :], total[1:2, :]
    factor = lax.rsqrt(square / width + EPSILON)
    bend = factor * factor * factor * (cross / width)
    span = total.shape[1]
    return (
        jnp.broadcast_to(factor, (LANES, span)).T,
        jnp.broadcast_to(bend, (LANES, span)).T,
    )


def gatebwd_kernel(groups, width, *refs):
    sums = refs[:groups]
    z_ref, scanned_ref, dm_ref, gain_ref, gz_ref, ds_ref, mixed_ref, gate_ref = refs[groups:]
    r = pl.program_id(0)
    factor, bend = gate_scales([s[...] for s in sums], width)

    @pl.when(r == 0)
    def _():
        gate_ref[...] = jnp.zeros_like(gate_ref)

    for c in range(z_ref.shape[1] // LANES):
        at = slice(c * LANES, (c + 1) * LANES)
        gain = gain_ref[0:1, at]
        sz, dsz = silu_parts(z_ref[:, at])
        scanned = scanned_ref[:, at]
        dm = dm_ref[:, at]
        g = scanned * sz
        scaled = g * factor
        dg = factor * (dm * gain) - g * bend
        mixed_ref[:, at] = (scaled * gain).astype(BF)
        gz_ref[:, at] = (dg * scanned * dsz).astype(BF)
        ds_ref[:, at] = dg * sz
        gate_ref[0:1, at] += jnp.sum(dm * scaled, axis=0, keepdims=True)


def backward_kernel(per, first, last, carried, *refs):
    (ds_ref, v_ref, total_in_ref, scanned_ref, mask_ref, afft_ref, step_ref, run_ref, runt_ref, taps_v_ref) = refs[:10]
    refs = refs[10:]
    if carried:
        carry, refs = refs[:3], refs[3:]
    if last:
        (shared_ref, raw_ref, act_ref, sum_ref, seg_ref, taps_s_ref, head_ref, place_ref) = refs[:8]
        gv_ref, vsum_ref, gs_ref, ssum_ref, daff_ref, dstep_ref, drun_ref = refs[8:]
    else:
        gv_ref, vsum_ref, daff_ref, dstep_ref, drun_ref = refs
    row, pair = pl.program_id(0), pl.program_id(1)
    head_pair = pair + first

    @pl.when((row == 0) & (pair == 0))
    def _():
        vsum_ref[...] = jnp.zeros_like(vsum_ref)
        if last:
            ssum_ref[...] = jnp.zeros_like(ssum_ref)

    @pl.when(pair == 0)
    def _():
        for n, target in enumerate((daff_ref, dstep_ref, drun_ref)):
            target[...] = carry[n][...] if carried else jnp.zeros_like(target)

    masks = [mask_ref[:, s * LANES : (s + 1) * LANES] for s in range(KERNEL - 1)]
    taps = [taps_v_ref[k : k + 1, :] for k in range(KERNEL)]
    skip = taps_v_ref[KERNEL + 1 : KERNEL + 2, :]
    values, dvalues = silu_parts(total_in_ref[...])
    columns, rows, stepx, low, lane = pair_columns(head_pair, run_ref, runt_ref, step_ref)
    ds = ds_ref[...]
    dsb = ds.astype(BF)
    fed = (stepx * values).astype(BF)
    zero = jnp.zeros_like(dsb)
    chosen = [jnp.where(low, dsb, zero), jnp.where(low, zero, dsb)]
    cut = fed.shape[0] // 2
    backs = []
    for n in range(2):
        at = slice(n * cut, (n + 1) * cut)
        begin = n * cut
        affinity = afft_ref[at, begin:]
        daff = daff_ref[at, begin:]
        parts = []
        for e in range(2):
            decay = jnp.exp(jnp.minimum(rows[e][:, begin:] - columns[e][at], 0.0))
            parts.append(mm((decay * affinity).astype(BF), dsb[begin:], NN))
            daff = daff + mm(fed[at], chosen[e][begin:], NT) * decay
        daff_ref[at, begin:] = daff
        backs.append(jnp.where(low[at], parts[0], parts[1]))
    back = jnp.concatenate(backs, axis=0)
    inner = scanned_ref[...] - skip * values
    direct = back * values
    moved = dsb.astype(F32) * inner - fed.astype(F32) * back
    dstep, drun = dstep_ref[...], drun_ref[...]
    for e in range(2):
        half = low if e == 0 else ~low
        spot = lane == 2 * head_pair + e
        dstep = dstep + jnp.where(spot, jnp.sum(jnp.where(half, direct, 0.0), axis=1, keepdims=True), 0.0)
        drun = drun + jnp.where(spot, jnp.sum(jnp.where(half, moved, 0.0), axis=1, keepdims=True), 0.0)
    dstep_ref[...] = dstep
    drun_ref[...] = drun
    dtotal = (stepx * back + skip * ds) * dvalues
    dx, tap_grads = conv_backward(dtotal, v_ref[...], masks, taps)
    gv_ref[...] = dx.astype(BF)
    sums = tap_grads + [
        jnp.sum(dtotal, axis=0, keepdims=True),
        jnp.sum(ds * values, axis=0, keepdims=True),
        jnp.zeros((2, LANES), F32),
    ]
    at = pl.ds(pl.multiple_of(pair * LANES, LANES), LANES)
    vsum_ref[:, at] = vsum_ref[:, at] + jnp.concatenate(sums, axis=0)
    if not last:
        return

    @pl.when(pair == pl.num_programs(1) - 1)
    def _():
        _, column, seg_row = segment_masks(seg_ref)
        _, before = ordered(seg_row.shape[1])
        allowed = before & (column == seg_row)
        full = jnp.where(allowed, daff_ref[...], 0.0)
        keys, queries = act_ref[:, :LANES], act_ref[:, LANES:]
        dkeys = mm_fine(full, queries, NN)
        dqueries = mm_fine(full, keys, TN)
        for c, dside in enumerate((dkeys, dqueries)):
            lanes = slice(c * LANES, (c + 1) * LANES)
            taps_c = [taps_s_ref[k : k + 1, lanes] for k in range(KERNEL)]
            dsum = dside * silu_parts(sum_ref[:, lanes])[1]
            dside_x, taps_g = conv_backward(dsum, shared_ref[:, lanes], masks, taps_c)
            gs_ref[:, lanes] = dside_x.astype(BF)
            more = taps_g + [jnp.sum(dsum, axis=0, keepdims=True), jnp.zeros((3, LANES), F32)]
            ssum_ref[:, lanes] = ssum_ref[:, lanes] + jnp.concatenate(more, axis=0)
        ddecay = mm_ones(jnp.where(before, 1.0, 0.0).astype(BF), drun_ref[...], NN)
        rate = -head_ref[1:2, :]
        draw = (dstep_ref[...] + ddecay * rate) * jax.nn.sigmoid(raw_ref[...])
        draw = draw * head_ref[2:3, :]
        gs_ref[:, 2 * LANES :] = pltpu.roll(draw, place_ref[0] * per, 1).astype(BF)
        heads = [
            jnp.sum(draw, axis=0, keepdims=True),
            jnp.sum(ddecay * (rate * step_ref[...]), axis=0, keepdims=True) * head_ref[2:3, :],
            jnp.zeros((6, LANES), F32),
        ]
        ssum_ref[:, 2 * LANES :] = ssum_ref[:, 2 * LANES :] + jnp.concatenate(heads, axis=0)


def weightgrad_kernel(lefts, rights, parts, *refs):
    place_ref = refs[0]
    left_refs = refs[1 : 1 + lefts]
    right_refs = refs[1 + lefts : 1 + lefts + rights]
    given_ref, kept_ref, stage_ref, sems = refs[1 + lefts + rights :]
    core = place_ref[1]
    model = stage_ref.shape[1]
    width = 384 if model % 384 == 0 else LANES

    def column(n, carry):
        cols = pl.ds(pl.multiple_of(n * width, LANES), width)
        right = jnp.concatenate([ref[:, cols] for ref in right_refs], axis=0)
        row = 0
        for ref in left_refs:
            rows = ref.shape[1]
            stage_ref[row : row + rows, cols] = mm(ref[...], right, TN).astype(BF)
            row += rows
        return carry

    lax.fori_loop(0, model // width, column, 0)
    copies = []
    for target, whose in ((given_ref, 1 - core), (kept_ref, core)):
        row = done = 0
        for half in parts:
            copies.append(
                pltpu.make_async_copy(
                    stage_ref.at[pl.ds(pl.multiple_of(row + whose * half, 16), half), :],
                    target.at[pl.ds(done, half), :],
                    sems.at[len(copies)],
                )
            )
            copies[-1].start()
            row += 2 * half
            done += half
    for copy in copies:
        copy.wait()


def weightgrad(place, lefts, rights, parts):
    rows, model = 2 * sum(parts), rights[0].shape[1]
    tokens = lefts[0].shape[0]
    half = jax.ShapeDtypeStruct((rows // 2, model), BF)
    return call(
        partial(weightgrad_kernel, len(lefts), len(rights), parts),
        (half, half),
        2 * tokens * rows * model,
        2 * tokens * (rows + model) + 2 * rows * model,
        in_specs=[pl.BlockSpec(memory_space=pltpu.SMEM)] + [VM] * (len(lefts) + len(rights)),
        out_specs=(HBM, HBM),
        scratch_shapes=[pltpu.VMEM((rows, model), BF), pltpu.SemaphoreType.DMA((2 * len(parts),))],
    )(place, *lefts, *rights)


def normgrad_kernel(groups, *refs):
    parts, weight_ref, outs = refs[: -groups - 1], refs[-groups - 1], refs[-groups:]
    span = outs[0].shape[0]
    model = weight_ref.shape[1]
    width = 384 if model % 384 == 0 else LANES

    def column(n, carry):
        cols = pl.ds(pl.multiple_of(n * width, LANES), width)
        weight = weight_ref[:, cols]
        for r in range(groups):
            at = slice(r * span, (r + 1) * span)
            terms = jnp.concatenate([part[at, :] for part in parts], axis=1)
            outs[r][:, cols] = mm(terms, weight, NN).astype(outs[r].dtype)
        return carry

    lax.fori_loop(0, model // width, column, 0)


def final_kernel(groups, aligned, width, *refs):
    outs = refs[:groups]
    grads = refs[groups : 2 * groups]
    sums = refs[2 * groups : 3 * groups]
    place_ref, tokens_ref, normal_ref, cot_ref, gain_ref, output_ref, tgrad_ref, gnorm_ref = refs[3 * groups :]
    member = place_ref[0]
    model = gain_ref.shape[1]
    rows = model // groups
    factor = gate_scales([s[...] for s in sums], width)[0]
    total = outs[0][...].astype(F32)
    for part in outs[1:]:
        total = total + part[...].astype(F32)
    output_ref[...] = (tokens_ref[...].astype(F32) + total * factor[:, 0:1]).astype(BF)
    xs, gained, square, cross = [], [], 0.0, 0.0
    for b in range(groups):
        at = slice(b * rows, (b + 1) * rows)
        grad = grads[0][:, at].astype(F32)
        for k in range(1, groups):
            grad = grad + grads[k][:, (b ^ k) * rows : ((b ^ k) + 1) * rows].astype(F32)
        x = normal_ref[:, lane_block(aligned, member, b, rows)].astype(F32)
        more = grad * gain_ref[:, at]
        square = square + jnp.sum(x * x, axis=-1, keepdims=True)
        cross = cross + jnp.sum(more * x, axis=-1, keepdims=True)
        xs.append((x, grad))
        gained.append(more)
    scale = lax.rsqrt(square / model + EPSILON)
    bend = scale * scale * scale * (cross / model)
    for b in range(groups):
        at = slice(b * rows, (b + 1) * rows)
        x, grad = xs[b]
        lanes = lane_block(aligned, member, b, rows)
        tgrad_ref[:, lanes] = (cot_ref[:, lanes].astype(F32) + (gained[b] * scale - x * bend)).astype(BF)
        gnorm_ref[0:1, at] = jnp.sum(grad * (x * scale), axis=0, keepdims=True)


def place_kernel(pieces, groups, *refs):
    place_ref = refs[0]
    count = len(pieces)
    sources = refs[1 : 1 + 2 * count]
    out_ref, stage_ref, sems = refs[-3:]
    member, core = place_ref[0], place_ref[1]
    copies = []
    row = 0
    later = []
    for n, (segments, stride, shared) in enumerate(pieces):
        each = sum(half for half, _ in segments)
        for which in range(2):
            whose = core if which == 0 else 1 - core
            source = sources[2 * n + which]
            for k in range(groups):
                stage_ref[row : row + each, :] = source[k * each : (k + 1) * each, :].astype(F32)
                for half, offset in segments:
                    target = offset + jnp.bitwise_xor(member, k) * stride + whose * half
                    copy = pltpu.make_async_copy(
                        stage_ref.at[pl.ds(row, half), :],
                        out_ref.at[pl.ds(pl.multiple_of(target, 8), half), :],
                        sems.at[len(copies)],
                    )
                    copy.start()
                    copies.append(copy)
                    row += half
            if shared:
                part = source.shape[0] - groups * each
                begin, tail = shared
                stage_ref[row : row + part, :] = source[groups * each :, :].astype(F32)
                later.append((whose, row, begin, part, tail, len(copies) + len(later) + which))
                row += part
    for whose, row, begin, part, tail, sem in later:
        for c, size in ((0, part), (1, tail - part)):

            @pl.when(whose == c)
            def _():
                copy = pltpu.make_async_copy(
                    stage_ref.at[pl.ds(row, size), :], out_ref.at[pl.ds(begin + c * part, size), :], sems.at[sem]
                )
                copy.start()
                copy.wait()

    for copy in copies:
        copy.wait()


def place_rows(place, groups, shape, pieces, values, onto=None):
    rows = sum(v.shape[0] for v in values)
    given = [] if onto is None else [onto]
    return call(
        partial(place_kernel, pieces, groups),
        jax.ShapeDtypeStruct(shape, F32),
        rows * shape[1],
        6 * rows * shape[1],
        in_specs=[pl.BlockSpec(memory_space=pltpu.SMEM)] + [VM] * len(values) + [HBM] * len(given),
        out_specs=HBM,
        scratch_shapes=[
            pltpu.VMEM((rows, shape[1]), F32),
            pltpu.SemaphoreType.DMA((4 * len(pieces) * (groups + 2),)),
        ],
        input_output_aliases={1 + len(values): 0} if given else {},
    )(place, *values, *given)


def swap(value, axis, step):
    size = lax.axis_size(axis)
    return lax.ppermute(value, axis, [(i, i ^ step) for i in range(size)])


def rounded_sum(a, b):
    return (a.astype(F32) + b.astype(F32)).astype(BF)


def line_sum(value):
    size = lax.axis_size("rep")
    bits = size.bit_length() - 1
    last = bits - 2 if bits >= 3 else bits
    for b in range(1, last):
        value = rounded_sum(value, swap(value, "rep", 1 << b))
    if bits < 3:
        return value
    low = size // 4
    where = lax.axis_index("rep") // low
    inward = [(low * a + i, low * b + i) for a, b in ((0, 1), (3, 2)) for i in range(low)]
    middle = [(low * a + i, low * b + i) for a, b in ((1, 2), (2, 1)) for i in range(low)]
    outward = [(low * a + i, low * b + i) for a, b in ((1, 0), (2, 3)) for i in range(low)]
    got = lax.ppermute(value, "rep", inward)
    value = rounded_sum(value, got)
    got = lax.ppermute(value, "rep", middle)
    value = rounded_sum(value, got)
    back = lax.ppermute(value, "rep", outward)
    return jnp.where((where == 0) | (where == 3), back, value)


def all_sum(value):
    for axis in ("fsdp", "rep"):
        size = lax.axis_size(axis)
        step = 1
        while step < size:
            if step * 4 <= size:
                near, far, both = (swap(value, axis, step * m) for m in (1, 2, 3))
                value = (value + near) + (far + both)
                step *= 4
            else:
                value = value + swap(value, axis, step)
                step *= 2
    return value


def to_owners(total, groups):
    rows = total.shape[1] // groups
    blocks = [total[:, k * rows : (k + 1) * rows] for k in range(groups)]
    return [blocks[0]] + [swap(blocks[k], "fsdp", k) for k in range(1, groups)]


def core_sum(halves_):
    given, kept = halves_
    got = swap(given, "rep", 1)
    return rounded_sum(kept, got)


def body(
    tokens,
    segment_ids,
    cotangent,
    norm_gain,
    in_weight,
    conv_weight,
    conv_bias,
    step_bias,
    rate_log,
    skip_gain,
    gate_gain,
    out_weight,
):
    groups = lax.axis_size("fsdp")
    member = lax.axis_index("fsdp")
    core = lax.axis_index("rep") % 2
    span, model = tokens.shape
    per = HEADS // groups
    inner = per * HEADDIM
    full = inner * groups
    conv = conv_bias.shape[0] * groups
    tail = in_weight.shape[1] - 2 * full
    padded = -(-tail // 384) * 384
    width = 2 * inner + padded
    pairs = per // 2
    whole = groups * span
    quarter = lax.axis_index("rep") % 4
    place = jnp.stack([member, core, quarter]).astype(jnp.int32)

    rows = in_weight.shape[0]
    aligned = rows % LANES == 0
    cols = conv // groups
    smem = pl.BlockSpec(memory_space=pltpu.SMEM)
    weight_t = in_weight.T

    xs = [tokens] + [swap(tokens, "fsdp", k) for k in range(1, groups)]
    small_width = -(-max(rows, cols, span) // LANES) * LANES
    packed = call(
        partial(pack_kernel, groups),
        tuple(jax.ShapeDtypeStruct((width // 4, rows), BF) for _ in range(1, groups))
        + (jax.ShapeDtypeStruct((8, small_width), F32),),
        1,
        4 * width * rows * groups,
        in_specs=[smem, HBM] + [VM] * 4,
        out_specs=(VM,) * groups,
        scratch_shapes=[pltpu.SemaphoreType.DMA((3 * groups,))],
    )(place, weight_t, norm_gain.reshape(1, -1), conv_weight, conv_bias.reshape(1, -1), segment_ids)
    near = [swap(packed[k - 1], "fsdp", k) for k in range(1, groups)]
    own_small = call(
        copy_kernel, jax.ShapeDtypeStruct(packed[-1].shape, F32), 1, 1, in_specs=[VM], out_specs=VM
    )(packed[-1])
    small = [own_small] + [swap(packed[-1], "fsdp", k) for k in range(1, groups)]
    near = jnp.concatenate(near, axis=0)
    across = swap(near, "rep", 2)
    given = [near, swap(near, "rep", 1), across, swap(across, "rep", 1)]
    late, _ = lax.optimization_barrier((cotangent, (near, xs[-1])))
    cots = [cotangent] + [swap(late, "fsdp", k) for k in range(1, groups)]

    gain_x = jnp.concatenate([t[0:1, :rows] for t in small], axis=1)
    order = jnp.arange(groups) ^ member
    table = jnp.take(jnp.stack(small), order, axis=0)
    taps_full = jnp.swapaxes(table[:, 1 : 2 + KERNEL, :cols], 0, 1).reshape(KERNEL + 1, conv)
    own_heads = lambda v: lax.dynamic_slice_in_dim(v.astype(F32), member * per, per, 0)
    taps_v = jnp.concatenate(
        [
            lax.dynamic_slice_in_dim(taps_full, member * inner, inner, 1),
            jnp.repeat(own_heads(skip_gain), HEADDIM).reshape(1, inner),
            gate_gain.astype(F32).reshape(1, inner),
            jnp.zeros((1, inner), F32),
        ],
        axis=0,
    )
    taps_s = jnp.concatenate([taps_full[:, full:], jnp.zeros((3, conv - full), F32)], axis=0)
    spread = lambda v: jnp.pad(v, (0, LANES - per)).reshape(1, LANES)
    heads = jnp.concatenate(
        [
            spread(own_heads(step_bias)),
            spread(jnp.exp(own_heads(rate_log))),
            spread(jnp.ones((per,), F32)),
            jnp.zeros((5, LANES), F32),
        ],
        axis=0,
    )
    segs = jnp.concatenate(
        [jnp.broadcast_to(s[2 + KERNEL : 3 + KERNEL, :span], (8, span)) for s in small], axis=0
    )

    def in_peer_order(value):
        if aligned:
            return value
        return jnp.take(value.reshape(value.shape[0], groups, rows), order, axis=1).reshape(value.shape)

    if aligned:
        sources = [weight_t] + given
    else:
        ranked = jnp.take(jnp.stack(given), jnp.arange(4) ^ quarter, axis=0)
        mine = jnp.concatenate(
            [
                lax.dynamic_slice_in_dim(weight_t, member * inner, inner, 0),
                lax.dynamic_slice_in_dim(weight_t, full + member * inner, inner, 0),
                jnp.pad(weight_t[2 * full :], ((0, padded - tail), (0, 0))),
            ],
            axis=0,
        )
        sent, share = width // 4, inner // 4

        def block(k):
            own = ranked[:, (k - 1) * sent : k * sent]
            pieces = (own[:, :share], own[:, share : 2 * share], own[:, 2 * share :])
            return jnp.concatenate([piece.reshape(-1, rows) for piece in pieces], axis=0)

        sources = [jnp.concatenate([mine] + [block(k) for k in range(1, groups)], axis=1)]
    sems = pltpu.SemaphoreType.DMA((12 * groups,))
    normed, projected, weight = call(
        partial(inproj_kernel, groups, aligned),
        (
            jax.ShapeDtypeStruct((whole, model), BF),
            jax.ShapeDtypeStruct((whole, width), F32),
            jax.ShapeDtypeStruct((width, model), BF),
        ),
        2 * whole * model * width,
        4 * whole * width + 4 * model * width + 4 * whole * model,
        mib=6 * groups,
        in_specs=[HBM] * groups + [VM, smem] + [HBM] * len(sources),
        out_specs=(VM, VM, HBM),
        scratch_shapes=[
            pltpu.VMEM((groups, span, model), BF),
            pltpu.VMEM((width, model), BF),
            sems,
            pltpu.SemaphoreType.DMA((groups,)),
        ],
    )(*[in_peer_order(x) for x in xs], gain_x, place, *sources)

    tile = lambda col: pl.BlockSpec((span, LANES), lambda r, p: (r, col + p))
    per_row = lambda cols_, col: pl.BlockSpec((span, cols_), lambda r, p: (r, col))
    fixed = lambda shape: pl.BlockSpec(shape, lambda r, p: (0, 0))
    pair_cols = pl.BlockSpec((8, LANES), lambda r, p: (0, p))
    seg_spec = pl.BlockSpec((8, span), lambda r, p: (r, 0))
    shared_spec = per_row(padded, 2 * inner // padded)
    scan_flops = 4 * whole * span * inner
    side = lambda w: jax.ShapeDtypeStruct((whole, w), F32)
    flipped_spec = pl.BlockSpec((LANES, span), lambda r, p: (r, 0))
    kept_shapes = (
        side((KERNEL - 1) * LANES),
        side(span),
        side(LANES),
        side(LANES),
        jax.ShapeDtypeStruct((groups * LANES, span), F32),
        side(LANES),
        side(2 * LANES),
        side(2 * LANES),
    )
    kept_specs = (
        per_row((KERNEL - 1) * LANES, 0),
        per_row(span, 0),
        per_row(LANES, 0),
        per_row(LANES, 0),
        flipped_spec,
        per_row(LANES, 0),
        per_row(2 * LANES, 0),
        per_row(2 * LANES, 0),
    )
    scanned, totals, gated, squares, *kept = call(
        partial(forward_kernel, per),
        (
            side(inner),
            side(inner),
            jax.ShapeDtypeStruct((whole, inner), BF),
            jax.ShapeDtypeStruct((8 * groups, span), F32),
        )
        + kept_shapes,
        8 * scan_flops,
        20 * whole * inner,
        mib=12,
        grid=(groups, pairs),
        in_specs=[
            smem,
            tile(0),
            tile(pairs),
            shared_spec,
            seg_spec,
            fixed((8, conv - full)),
            pair_cols,
            fixed((8, LANES)),
        ],
        out_specs=(tile(0), tile(0), tile(0), seg_spec) + kept_specs,
        scratch_shapes=[pltpu.VMEM((span, span), F32), pltpu.VMEM((span, LANES), F32)],
    )(place, projected, projected, projected, segs, taps_s, taps_v, heads)

    proj_flops = 2 * whole * inner * model
    dm, sums = call(
        partial(mixgrad_kernel, groups),
        (jax.ShapeDtypeStruct((whole, inner), F32), jax.ShapeDtypeStruct((8 * groups, span), F32)),
        proj_flops,
        2 * whole * model + 6 * whole * inner + 2 * inner * model,
        in_specs=[VM] * (groups + 3),
        out_specs=(VM, VM),
    )(*cots, out_weight, gated, squares)
    sums_all = [sums] + [swap(sums, "fsdp", k) for k in range(1, groups)]

    outs = call(
        partial(outproj_kernel, groups),
        tuple(jax.ShapeDtypeStruct((span, model), BF if k else F32) for k in range(groups)),
        proj_flops,
        2 * whole * model + 2 * whole * inner + 2 * inner * model,
        in_specs=[VM, VM],
        out_specs=(VM,) * groups,
    )(gated, out_weight)
    outs = [outs[0]] + [swap(outs[k], "fsdp", k) for k in range(1, groups)]

    row_spec = lambda cols_, col=0: pl.BlockSpec((span, cols_), lambda r: (r, col))
    gz, ds, mixed, gate_sum = call(
        partial(gatebwd_kernel, groups, float(full)),
        (
            jax.ShapeDtypeStruct((whole, inner), BF),
            jax.ShapeDtypeStruct((whole, inner), F32),
            jax.ShapeDtypeStruct((whole, inner), BF),
            jax.ShapeDtypeStruct((8, inner), F32),
        ),
        20 * whole * inner,
        20 * whole * inner,
        mib=16,
        grid=(groups,),
        in_specs=[
            pl.BlockSpec((8, span), (lambda k: lambda r: (jnp.bitwise_xor(r, k), 0))(k)) for k in range(groups)
        ]
        + [row_spec(inner), row_spec(inner), row_spec(inner), pl.BlockSpec((8, inner), lambda r: (0, 0))],
        out_specs=(
            row_spec(inner),
            row_spec(inner),
            row_spec(inner),
            pl.BlockSpec((8, inner), lambda r: (0, 0)),
        ),
    )(*sums_all, projected, scanned, dm, jnp.broadcast_to(gate_gain.astype(F32).reshape(1, inner), (8, inner)))

    z_sum = core_sum(weightgrad(place, [gz], [normed], (inner // 2,)))
    o_sum = core_sum(weightgrad(place, [mixed], cots, (inner // 2,)))
    out_part = line_sum(o_sum)
    z_part = line_sum(jnp.concatenate(to_owners(z_sum, groups), axis=0))

    third = pairs // 3
    cuts = (0, third, 2 * third, pairs)
    split = cuts[2]
    carry_shapes = (side(span), side(LANES), side(LANES))
    carry_specs = (per_row(span, 0), per_row(LANES, 0), per_row(LANES, 0))

    def backward(n, carry):
        first, count, last = cuts[n], cuts[n + 1] - cuts[n], n == 2
        cols_ = count * LANES
        outs_ = (jax.ShapeDtypeStruct((whole, cols_), BF), jax.ShapeDtypeStruct((8, cols_), F32))
        specs_ = (tile(0), fixed((8, cols_)))
        scratch, more, more_specs = [], [], []
        if last:
            outs_ += (jax.ShapeDtypeStruct((whole, padded), BF), jax.ShapeDtypeStruct((8, padded), F32))
            specs_ += (per_row(padded, 0), fixed((8, padded)))
            scratch = [
                pltpu.VMEM((span, span), F32),
                pltpu.VMEM((span, LANES), F32),
                pltpu.VMEM((span, LANES), F32),
            ]
            more = [projected, kept[5], kept[6], kept[7], segs, taps_s, heads, place]
            more_specs = [shared_spec, kept_specs[5], kept_specs[6], kept_specs[7], seg_spec]
            more_specs += [fixed((8, conv - full)), fixed((8, LANES)), smem]
        else:
            outs_ += carry_shapes
            specs_ += carry_specs
        return call(
            partial(backward_kernel, per, first, last, len(carry) > 0),
            outs_,
            16 * scan_flops * count // pairs,
            24 * whole * cols_,
            mib=48 if last else 12,
            grid=(groups, count),
            in_specs=[tile(first), tile(pairs + first), tile(first), tile(first)]
            + list(kept_specs[:5])
            + [pl.BlockSpec((8, LANES), lambda r, p: (0, first + p))]
            + (list(carry_specs) if carry else [])
            + more_specs,
            out_specs=specs_,
            scratch_shapes=scratch,
        )(ds, projected, totals, scanned, *kept[:5], taps_v, *carry, *more)

    gva, vsum1, *handed = backward(0, ())
    gvb, vsum2, *handed = backward(1, handed)
    v1_sum = core_sum(weightgrad(place, [gva, gvb], [normed], (third * HEADDIM, third * HEADDIM)))
    gv2, vsum3, gs, ssum = backward(2, handed)
    vsum = jnp.concatenate([vsum1, vsum2, vsum3], axis=1)

    backs = call(
        partial(normgrad_kernel, groups),
        tuple(jax.ShapeDtypeStruct((span, model), BF if k else F32) for k in range(groups)),
        2 * whole * width * model,
        2 * whole * model + 2 * whole * width + 2 * width * model,
        in_specs=[VM] * 6,
        out_specs=(VM,) * groups,
    )(gz, gva, gvb, gv2, gs, weight)
    backs = [backs[0]] + [swap(backs[k], "fsdp", k) for k in range(1, groups)]

    v1_part = line_sum(jnp.concatenate(to_owners(v1_sum, groups), axis=0))
    deep = (pairs - split) * HEADDIM
    s_sum = core_sum(weightgrad(place, [gv2, gs], [normed], (deep, padded // 2)))
    terms = to_owners(s_sum, groups)
    shared_sum = terms[0][deep:].astype(F32)
    for term in terms[1:]:
        shared_sum = shared_sum + term[deep:].astype(F32)
    s_part = line_sum(jnp.concatenate([t[:deep] for t in terms] + [shared_sum.astype(BF)], axis=0))

    whole_spec = lambda shape: pl.BlockSpec(shape, lambda i: (0,) * len(shape))
    output, tokens_grad, norm_sum = call(
        partial(final_kernel, groups, aligned, float(full)),
        (
            jax.ShapeDtypeStruct((span, model), BF),
            jax.ShapeDtypeStruct((span, model), BF),
            jax.ShapeDtypeStruct((8, model), F32),
        ),
        30 * span * model,
        24 * span * model,
        grid=(1,),
        in_specs=[whole_spec((span, model))] * (2 * groups)
        + [pl.BlockSpec((8, span), (lambda k: lambda i: (k, 0))(k)) for k in range(groups)]
        + [smem]
        + [whole_spec((span, model))] * 3
        + [whole_spec((1, model))],
        out_specs=(whole_spec((span, model)), whole_spec((span, model)), whole_spec((8, model))),
    )(*outs, *backs, *sums_all, place, tokens, in_peer_order(tokens), in_peer_order(cotangent), gain_x)
    tokens_grad = in_peer_order(tokens_grad)
    norm_sum = jnp.take(norm_sum[0].reshape(groups, rows), order, axis=0).reshape(1, model)

    def returned(part):
        return [part, swap(part, "rep", 1)]

    grad_outproj = place_rows(
        place, 1, out_weight.shape, ((((inner // 2, 0),), 0, None),), returned(out_part)
    )
    early = returned(z_part) + returned(v1_part)
    gin = place_rows(
        place,
        groups,
        weight_t.shape,
        (
            (((inner // 2, 0),), inner, None),
            (((third * HEADDIM, full), (third * HEADDIM, full + third * 2 * HEADDIM)), inner, None),
        ),
        early,
    )
    grad_inproj = place_rows(
        place,
        groups,
        weight_t.shape,
        ((((deep, full + split * 2 * HEADDIM),), inner, (2 * full, tail)),),
        returned(s_part),
        gin,
    ).T

    own_cols = lambda v: lax.dynamic_update_slice_in_dim(
        jnp.zeros((v.shape[0], full), F32), v, member * inner, 1
    )
    own_spot = lambda v: lax.dynamic_update_slice_in_dim(jnp.zeros((HEADS,), F32), v, member * per, 0)
    taps_grad = jnp.concatenate([own_cols(vsum[: KERNEL + 1]), ssum[: KERNEL + 1, : conv - full]], axis=1)
    head_grads = [
        own_spot(ssum[0, 2 * LANES : 2 * LANES + per]),
        own_spot(ssum[1, 2 * LANES : 2 * LANES + per]),
        own_spot(vsum[KERNEL + 1].reshape(per, HEADDIM).sum(axis=1)),
    ]
    flat = jnp.concatenate(
        [norm_sum[0], taps_grad.reshape(-1), own_cols(gate_sum[:1]).reshape(-1)] + head_grads
    )
    length = flat.shape[0]
    flat = jnp.pad(flat, (0, -length % 1024)).reshape(-1, LANES)
    flat = all_sum(flat).reshape(-1)
    at = 0
    grad_norm = lax.dynamic_slice_in_dim(flat, member * rows, rows, 0)
    at += model
    taps_all = flat[at : at + (KERNEL + 1) * conv].reshape(KERNEL + 1, conv)
    taps_own = lax.dynamic_slice_in_dim(taps_all, member * cols, cols, 1)
    at += (KERNEL + 1) * conv
    grad_gate = lax.dynamic_slice_in_dim(flat, at + member * inner, inner, 0)
    at += full
    return (
        output,
        tokens_grad,
        grad_norm,
        grad_inproj,
        taps_own[:KERNEL],
        taps_own[KERNEL],
        flat[at : at + HEADS],
        flat[at + HEADS : at + 2 * HEADS],
        flat[at + 2 * HEADS : at + 3 * HEADS],
        grad_gate,
        grad_outproj,
    )


def solution(mesh):
    rows = P(("rep", "fsdp"), None)
    in_specs = (
        rows,
        rows,
        rows,
        P("fsdp"),
        P("fsdp", None),
        P(None, "fsdp"),
        P("fsdp"),
        P(),
        P(),
        P(),
        P("fsdp"),
        P("fsdp", None),
    )
    out_specs = (
        rows,
        rows,
        P("fsdp"),
        P("fsdp", None),
        P(None, "fsdp"),
        P("fsdp"),
        P(),
        P(),
        P(),
        P("fsdp"),
        P("fsdp", None),
    )

    return jax.shard_map(body, mesh=mesh, in_specs=in_specs, out_specs=out_specs, check_vma=False)
```

profile of v0, /device:TPU:0, one launch (start us, length us, event | category | flops | bytes accessed | tf_op | source)
XLA Modules:
  0.0 466.8 jit_solution(13975063170113630174)
XLA Ops:
  2.1 2.4 copy-done.7
  5.9 2.1 shard_map.203
  8.1 3.0 collective-permute-start.6
  11.1 1.5 collective-permute-start.7
  12.6 7.9 %collective-permute-done.6 = bf16[480,384]{1,0:T(8,128)(2,1)S(1)} collective-permute-done((bf16[480,384]{1,0:T(8,128)(2,1)S(1)}, bf16[480,384]{1,0:T(8,128)(2,1)S(1)}, u32[]{:S(2)}, u32[]{:S(2)}) %collective-permute-start.6) | collective-permute-done | bytes 368672 | tf_op jit(solution)/shard_map/ppermute | solution.py:713
  20.6 8.5 %collective-permute-done.7 = bf16[480,384]{1,0:T(8,128)(2,1)S(1)} collective-permute-done((bf16[480,384]{1,0:T(8,128)(2,1)S(1)}, bf16[480,384]{1,0:T(8,128)(2,1)S(1)}, u32[]{:S(2)}, u32[]{:S(2)}) %collective-permute-start.7) | collective-permute-done | bytes 368672 | tf_op jit(solution)/shard_map/ppermute | solution.py:713
  29.2 1.4 collective-permute-start.10
  30.6 1.5 collective-permute-start.5
  34.5 19.8 %collective-permute-done.10.refs_9_ = bf16[1440,384]{1,0:T(8,128)(2,1)S(1)} collective-permute-done((bf16[1440,384]{1,0:T(8,128)(2,1)S(1)}, bf16[1440,384]{1,0:T(8,128)(2,1)S(1)}, u32[]{:S(2)}, u32[]{:S(2)}) %collective-permute-start.10) | collective-permute-done | bytes 1105952 | tf_op jit(solution)/shard_map/ppermute | solution.py:713
  55.7 1.4 collective-permute-start
  57.7 1.5 collective-permute-start.2
  61.6 31.1 %collective-permute-done.2.refs_3_ = bf16[256,1536]{1,0:T(8,128)(2,1)} collective-permute-done((bf16[256,1536]{1,0:T(8,128)(2,1)S(1)}, bf16[256,1536]{1,0:T(8,128)(2,1)}, u32[]{:S(2)}, u32[]{:S(2)}) %collective-permute-start.2) | collective-permute-done | bytes 786464 | tf_op jit(solution)/shard_map/ppermute | solution.py:713
  92.7 1.5 collective-permute-start.15
  96.2 2.4 copy-done.8
  98.6 13.1 %shard_map.205 = (bf16[1024,1536]{1,0:T(8,128)(2,1)S(1)}, f32[1024,1920]{1,0:T(8,128)S(1)}, bf16[1920,1536]{1,0:T(8,128)(2,1)S(1)}) custom-call(bf16[256,1536]{1,0:T(8,128)(2,1)S(1)} %copy-done.15, bf16[256,1536]{1,0:T(8,128)(2,1)} %collective-permute-done.refs_1_, bf16[256,1536]{1,0:T(8,128)(2,1)} %collective-permute-done.1.refs_2_, ...), custom_call_target="tpu_custom_call" | custom-call | flops 6039797760 | bytes 25952256 | tf_op jit(solution)/shard_map/pallas_call | solution.py:60
  111.7 1.8 copy-done.62
  113.5 19.8 %shard_map.206 = (f32[1024,768]{1,0:T(8,128)S(1)}, f32[1024,768]{1,0:T(8,128)S(1)}, bf16[1024,768]{1,0:T(8,128)(2,1)S(1)}, f32[32,256]{1,0:T(8,128)S(1)}, f32[10...) custom-call(s32[3]{0:T(128)S(1)} %pad_add_fusion.refs_0_.refs_5_.pla, ...), custom_call_target="tpu_custom_call" | custom-call | flops 6442450944 | bytes 15728640 | tf_op jit(solution)/shard_map/pallas_call | solution.py:60
  135.5 5.7 %shard_map.208 = (f32[1024,768]{1,0:T(8,128)S(1)}, f32[32,256]{1,0:T(8,128)S(1)}) custom-call(bf16[256,1536]{1,0:T(8,128)(2,1)} %refs_2_.1, bf16[256,1536]{1,0:T(8,128)(2,1)S(1)} %collective-permute-done.15.refs_1_.refs_3_, bf16[256,1536]{1,0:T(8,128)(2,1)S(1)} %collective-permute-done.16.refs_2_.refs_4_, ...), custom_call_target="tpu_custom_call" | custom-call | flops 2415919104 | bytes 10223616 | tf_op jit(solution)/shard_map/pallas_call | solution.py:60
  143.9 1.5 collective-permute-start.18
  145.3 1.4 collective-permute-start.19
  147.4 4.9 %shard_map.207 = (f32[256,1536]{1,0:T(8,128)S(1)}, bf16[256,1536]{1,0:T(8,128)(2,1)}, bf16[256,1536]{1,0:T(8,128)(2,1)}, bf16[256,1536]{1,0:T(8,128)(2,1)}) custom-call(bf16[1024,768]{1,0:T(8,128)(2,1)S(1)} %get-tuple-element.75.gated_ref.refs_5_, bf16[768,1536]{1,0:T(8,128)(2,1)S(1)} %copy-done.38), custom_call_target="tpu_custom_call" | custom-call | flops 2415919104 | bytes 7077888 | tf_op jit(solution)/shard_map/pallas_call | solution.py:60
  152.3 1.5 collective-permute-start.12
  153.8 1.4 collective-permute-start.13
  155.9 3.6 shard_map.209
  159.6 7.0 %shard_map.210 = (bf16[1024,256]{1,0:T(8,128)(2,1)S(1)}, f32[8,256]{1,0:T(8,128)S(1)}, f32[1024,256]{1,0:T(8,128)S(1)}, f32[1024,128]{1,0:T(8,128)S(1)}, f32[1024,128]{1,0:T(8,128)S(1)}) custom-call(f32[1024,768]{1,0:T(8,128)S(1)} %get-tuple-element.86.refs_0_, f32[1024,1920]{1,0:T(8,128)S(1)} %get-tuple-element.74.z_ref.v_ref.shared_ref.refs_4_.refs_1_.refs_13_, ...), custom_call_target="tpu_custom_call" | custom-call | flops 4294967296 | bytes 6291456 | tf_op jit(solution)/shard_map/pallas_call | solution.py:60
  166.8 7.2 %shard_map.211 = (bf16[1024,256]{1,0:T(8,128)(2,1)S(1)}, f32[8,256]{1,0:T(8,128)S(1)}, f32[1024,256]{1,0:T(8,128)S(1)}, f32[1024,128]{1,0:T(8,128)S(1)}, f32[1024,128]{1,0:T(8,128)S(1)}) custom-call(f32[1024,768]{1,0:T(8,128)S(1)} %get-tuple-element.86.refs_0_, f32[1024,1920]{1,0:T(8,128)S(1)} %get-tuple-element.74.z_ref.v_ref.shared_ref.refs_4_.refs_1_.refs_13_, ...), custom_call_target="tpu_custom_call" | custom-call | flops 4294967296 | bytes 6291456 | tf_op jit(solution)/shard_map/pallas_call | solution.py:60
  180.2 12.9 %shard_map.212 = (bf16[1024,256]{1,0:T(8,128)(2,1)S(1)}, f32[8,256]{1,0:T(8,128)S(1)}, bf16[1024,384]{1,0:T(8,128)(2,1)S(1)}, f32[8,384]{1,0:T(8,128)S(1)}) custom-call(f32[1024,768]{1,0:T(8,128)} %copy-done.3, f32[1024,1920]{1,0:T(8,128)} %copy-done, f32[1024,768]{1,0:T(8,128)} %copy-done.2, f32[1024,768]{1,0:T(8,128)} %copy-done.1, f32[1024,384]{1,0:T(8,128)} %copy-done.4, ...), custom_call_target="tpu_custom_call" | custom-call | flops 4294967296 | bytes 6291456 | tf_op jit(solution)/shard_map/pallas_call | solution.py:60
  193.1 3.1 copy-done.65
  196.2 9.6 %shard_map.213 = (f32[256,1536]{1,0:T(8,128)S(1)}, bf16[256,1536]{1,0:T(8,128)(2,1)}, bf16[256,1536]{1,0:T(8,128)(2,1)}, bf16[256,1536]{1,0:T(8,128)(2,1)S(1)}) custom-call(bf16[1024,768]{1,0:T(8,128)(2,1)S(1)} %copy-done.42, bf16[1024,256]{1,0:T(8,128)(2,1)S(1)} %copy-done.55, bf16[1024,256]{1,0:T(8,128)(2,1)S(1)} %copy-done.58, ...), custom_call_target="tpu_custom_call" | custom-call | flops 6039797760 | bytes 12976128 | tf_op jit(solution)/shard_map/pallas_call | solution.py:60
  206.7 1.5 collective-permute-start.21
  208.2 1.4 collective-permute-start.22
  214.7 1.9 copy-done.63
  216.6 5.1 %shard_map.215 = (bf16[320,1536]{1,0:T(8,128)(2,1)}, bf16[320,1536]{1,0:T(8,128)(2,1)S(1)}) custom-call(s32[3]{0:T(128)S(1)} %pad_add_fusion.refs_0_.refs_5_.place_ref.refs_20_.refs_12_, bf16[1024,256]{1,0:T(8,128)(2,1)S(1)} %copy-done.61, bf16[1024,384]{1,0:T(8,128)(2,1)S(1)} %copy-done.53, bf16[1024,1536]{1,0:T(8,128)(2,1)S(1)} %copy-done.63), custom_call_target="tpu_custom_call" | custom-call | flops 2013265920 | bytes 6422528 | tf_op jit(solution)/shard_map/pallas_call | solution.py:60
  223.5 4.6 shard_map.217
  228.1 5.6 %shard_map.216 = (bf16[384,1536]{1,0:T(8,128)(2,1)}, bf16[384,1536]{1,0:T(8,128)(2,1)S(1)}) custom-call(s32[3]{0:T(128)S(1)} %pad_add_fusion.refs_0_.refs_5_.place_ref.refs_20_.refs_12_, bf16[1024,768]{1,0:T(8,128)(2,1)S(1)} %copy-done.43, bf16[1024,1536]{1,0:T(8,128)(2,1)S(1)} %copy-done.63), custom_call_target="tpu_custom_call" | custom-call | flops 2415919104 | bytes 7077888 | tf_op jit(solution)/shard_map/pallas_call | solution.py:60
  235.2 6.4 %shard_map.220 = (bf16[384,1536]{1,0:T(8,128)(2,1)}, bf16[384,1536]{1,0:T(8,128)(2,1)S(1)}) custom-call(s32[3]{0:T(128)S(1)} %pad_add_fusion.refs_0_.refs_5_.place_ref.refs_20_.refs_12_, bf16[1024,768]{1,0:T(8,128)(2,1)S(1)} %copy-done.40, bf16[256,1536]{1,0:T(8,128)(2,1)} %refs_2_.1, bf16[256,1536]{1,0:T(8,128)(2,1)S(1)} %copy-done.45, ...), custom_call_target="tpu_custom_call" | custom-call | flops 2415919104 | bytes 7077888 | tf_op jit(solution)/shard_map/pallas_call | solution.py:60
  243.7 5.1 %shard_map.214 = (bf16[256,1536]{1,0:T(8,128)(2,1)}, bf16[256,1536]{1,0:T(8,128)(2,1)}, f32[8,1536]{1,0:T(8,128)S(1)}) custom-call(f32[256,1536]{1,0:T(8,128)S(1)} %copy-done.18, bf16[256,1536]{1,0:T(8,128)(2,1)} %collective-permute-done.12.refs_1_, bf16[256,1536]{1,0:T(8,128)(2,1)} %collective-permute-done.13.refs_2_, ...), custom_call_target="tpu_custom_call" | custom-call | flops 11796480 | bytes 9437184 | tf_op jit(solution)/shard_map/pallas_call | solution.py:60
  249.6 1.4 add_convert_fusion.9
  251.9 2.3 collective-permute-start.50
  255.5 1.4 add_convert_fusion.6
  257.1 1.6 collective-permute-start.32
  258.6 1.6 add_convert_fusion.2
  260.2 3.1 collective-permute-start.56
  263.3 1.5 add_convert_fusion.5
  265.0 1.9 collective-permute-start.42
  268.7 1.5 collective-permute-done.32
  270.7 5.8 %collective-permute-done.42 = bf16[384,384]{1,0:T(8,128)(2,1)S(1)} collective-permute-done((bf16[384,384]{1,0:T(8,128)(2,1)S(1)}, bf16[384,384]{1,0:T(8,128)(2,1)S(1)}, u32[]{:S(2)}, u32[]{:S(2)}) %collective-permute-start.42) | collective-permute-done | bytes 294944 | tf_op jit(solution)/shard_map/ppermute | solution.py:713
  276.4 2.3 collective-permute-start.34
  278.8 4.1 collective-permute-done.41
  282.8 1.6 collective-permute-start.51
  284.5 1.8 collective-permute-start.43
  286.3 5.1 %collective-permute-done.33 = bf16[320,384]{1,0:T(8,128)(2,1)S(1)} collective-permute-done((bf16[320,384]{1,0:T(8,128)(2,1)S(1)}, bf16[320,384]{1,0:T(8,128)(2,1)S(1)}, u32[]{:S(2)}, u32[]{:S(2)}) %collective-permute-start.33) | collective-permute-done | bytes 245792 | tf_op jit(solution)/shard_map/ppermute | solution.py:713
  292.6 5.9 %collective-permute-start.35 = (bf16[704,384]{1,0:T(8,128)(2,1)S(1)}, bf16[704,384]{1,0:T(8,128)(2,1)S(1)}, u32[]{:S(2)}, u32[]{:S(2)}) collective-permute-start(bf16[704,384]{1,0:T(8,128)(2,1)S(1)} %fusion), channel_id=1, source_target_pairs={{0,8},{4,12},{24,16},{28,20},{1,9},{5,13},{25,17},{29,21},{2,10},{... | collective-permute-start | bytes 1622024 | tf_op jit(solution)/shard_map/ppermute | solution.py:733
  298.5 33.2 %collective-permute-done.43 = bf16[1536,384]{1,0:T(8,128)(2,1)S(1)} collective-permute-done((bf16[1536,384]{1,0:T(8,128)(2,1)S(1)}, bf16[1536,384]{1,0:T(8,128)(2,1)S(1)}, u32[]{:S(2)}, u32[]{:S(2)}) %collective-permute-start.43) | collective-permute-done | bytes 1179680 | tf_op jit(solution)/shard_map/ppermute | solution.py:733
  332.8 1.4 collective-permute-start.25
  335.7 5.7 %collective-permute-done.35 = bf16[704,384]{1,0:T(8,128)(2,1)S(1)} collective-permute-done((bf16[704,384]{1,0:T(8,128)(2,1)S(1)}, bf16[704,384]{1,0:T(8,128)(2,1)S(1)}, u32[]{:S(2)}, u32[]{:S(2)}) %collective-permute-start.35) | collective-permute-done | bytes 540704 | tf_op jit(solution)/shard_map/ppermute | solution.py:733
  347.7 20.8 %collective-permute-start.28 = (f32[168,128]{1,0:T(8,128)S(1)}, f32[168,128]{1,0:T(8,128)S(1)}, u32[]{:S(2)}, u32[]{:S(2)}) collective-permute-start(f32[168,128]{1,0:T(8,128)S(1)} %add_add_fusion.1), channel_id=1, source_target_pairs={{0,8},{4,12},{8,0},{12,4},{16,24},{20,28},{24,16},{28,20},{1,9},{5... | collective-permute-start | bytes 258056 | tf_op jit(solution)/shard_map/ppermute | solution.py:713
  370.2 23.2 %collective-permute-done.58 = bf16[384,1536]{1,0:T(8,128)(2,1)S(1)} collective-permute-done((bf16[384,1536]{1,0:T(8,128)(2,1)S(1)}, bf16[384,1536]{1,0:T(8,128)(2,1)S(1)}, u32[]{:S(2)}, u32[]{:S(2)}) %collective-permute-start.58) | collective-permute-done | bytes 1179680 | tf_op jit(solution)/shard_map/ppermute | solution.py:737
  394.8 23.8 %collective-permute-done.45 = bf16[1536,384]{1,0:T(8,128)(2,1)S(1)} collective-permute-done((bf16[1536,384]{1,0:T(8,128)(2,1)S(1)}, bf16[1536,384]{1,0:T(8,128)(2,1)S(1)}, u32[]{:S(2)}, u32[]{:S(2)}) %collective-permute-start.45) | collective-permute-done | bytes 1179680 | tf_op jit(solution)/shard_map/ppermute | solution.py:737
  418.8 22.2 %collective-permute-done.53 = bf16[1024,384]{1,0:T(8,128)(2,1)S(1)} collective-permute-done((bf16[1024,384]{1,0:T(8,128)(2,1)S(1)}, bf16[1024,384]{1,0:T(8,128)(2,1)S(1)}, u32[]{:S(2)}, u32[]{:S(2)}) %collective-permute-start.53) | collective-permute-done | bytes 786464 | tf_op jit(solution)/shard_map/ppermute | solution.py:737
  444.5 6.6 %collective-permute-done.30 = f32[168,128]{1,0:T(8,128)S(1)} collective-permute-done((f32[168,128]{1,0:T(8,128)S(1)}, f32[168,128]{1,0:T(8,128)S(1)}, u32[]{:S(2)}, u32[]{:S(2)}) %collective-permute-start.30) | collective-permute-done | bytes 86048 | tf_op jit(solution)/shard_map/ppermute | solution.py:713
  454.4 3.7 shard_map.221
  458.1 5.1 %shard_map.218.refs_3_ = f32[6448,384]{1,0:T(8,128)} custom-call(s32[3]{0:T(128)S(1)} %pad_add_fusion.refs_0_.refs_5_.place_ref.refs_20_.refs_12_, bf16[1536,384]{1,0:T(8,128)(2,1)S(1)} %broadcast_select_fusion.1.refs_1_, bf16[1536,384]{1,0:T(8,128)(2,1)} %collective-permute-done.46.refs_2_, bf16[1024,384]{1,0:T(8,128)(2,1)S(1)} %broadcast_select_fusion.2.refs_3_, ...), custom_call_target="tpu_custom_call" | custom-call | flops 1966080 | bytes 11796480 | tf_op jit(solution)/shard_map/pallas_call | solution.py:60
  463.2 3.4 shard_map.219
  (359 shorter events, 60.6 us)
Async XLA Ops:
  8.0 46.8 %copy-start.73 = (bf16[768]{0:T(1024)(128)(2,1)S(1)}, bf16[768]{0:T(1024)(128)(2,1)}, u32[]{:S(2)}) copy-start(bf16[768]{0:T(1024)(128)(2,1)} %param.22) | copy-start | bytes 4612
  8.1 47.6 %copy-start.15 = (bf16[256,1536]{1,0:T(8,128)(2,1)S(1)}, bf16[256,1536]{1,0:T(8,128)(2,1)}, u32[]{:S(2)}) copy-start(bf16[256,1536]{1,0:T(8,128)(2,1)} %refs_14_.1) | copy-start | bytes 2359300
  8.1 12.5 %collective-permute-start.6 = (bf16[480,384]{1,0:T(8,128)(2,1)S(1)}, bf16[480,384]{1,0:T(8,128)(2,1)S(1)}, u32[]{:S(2)}, u32[]{:S(2)}) collective-permute-start(bf16[480,384]{1,0:T(8,128)(2,1)S(1)} %get-tuple-element.71), channel_id=1, source_target_pairs={{0,1},{1,0},{2,3},{3,2},{4,5},{5,4},{6,7},{7,6},{8,9},{9,8},{10,11... | collective-permute-start | bytes 1105928 | tf_op jit(solution)/shard_map/ppermute | solution.py:713
  11.1 17.9 %collective-permute-start.7 = (bf16[480,384]{1,0:T(8,128)(2,1)S(1)}, bf16[480,384]{1,0:T(8,128)(2,1)S(1)}, u32[]{:S(2)}, u32[]{:S(2)}) collective-permute-start(bf16[480,384]{1,0:T(8,128)(2,1)S(1)} %get-tuple-element.72), channel_id=1, source_target_pairs={{0,2},{1,3},{2,0},{3,1},{4,6},{5,7},{6,4},{7,5},{8,10},{9,11},{10,... | collective-permute-start | bytes 1105928 | tf_op jit(solution)/shard_map/ppermute | solution.py:713
  12.6 16.5 %collective-permute-start.8 = (bf16[480,384]{1,0:T(8,128)(2,1)S(1)}, bf16[480,384]{1,0:T(8,128)(2,1)S(1)}, u32[]{:S(2)}, u32[]{:S(2)}) collective-permute-start(bf16[480,384]{1,0:T(8,128)(2,1)S(1)} %get-tuple-element.73), channel_id=1, source_target_pairs={{0,3},{1,2},{2,1},{3,0},{4,7},{5,6},{6,5},{7,4},{8,11},{9,10},{10,... | collective-permute-start | bytes 1105928 | tf_op jit(solution)/shard_map/ppermute | solution.py:713
  29.2 25.1 %collective-permute-start.10 = (bf16[1440,384]{1,0:T(8,128)(2,1)S(1)}, bf16[1440,384]{1,0:T(8,128)(2,1)S(1)}, u32[]{:S(2)}, u32[]{:S(2)}) collective-permute-start(bf16[1440,384]{1,0:T(8,128)(2,1)S(1)} %constant_dynamic-update-slice_fusion.refs_7_), channel_id=1, source_target_pairs={{0,8},{4,12},{8,0},{12,4},{16,24},{20,28},{24,16},{28,20},{1,9},{5... | collective-permute-start | bytes 3317768 | tf_op jit(solution)/shard_map/ppermute | solution.py:713
  30.6 25.1 %collective-permute-start.5 = (f32[8,896]{1,0:T(8,128)S(1)}, f32[8,896]{1,0:T(8,128)S(1)}, u32[]{:S(2)}, u32[]{:S(2)}) collective-permute-start(f32[8,896]{1,0:T(8,128)S(1)} %get-tuple-element.70.source_ref), channel_id=1, source_target_pairs={{0,3},{1,2},{2,1},{3,0},{4,7},{5,6},{6,5},{7,4},{8,11},{9,10},{10,... | collective-permute-start | bytes 86024 | tf_op jit(solution)/shard_map/ppermute | solution.py:713
  32.1 25.0 %collective-permute-start.4 = (f32[8,896]{1,0:T(8,128)S(1)}, f32[8,896]{1,0:T(8,128)S(1)}, u32[]{:S(2)}, u32[]{:S(2)}) collective-permute-start(f32[8,896]{1,0:T(8,128)S(1)} %get-tuple-element.70.source_ref), channel_id=1, source_target_pairs={{0,2},{1,3},{2,0},{3,1},{4,6},{5,7},{6,4},{7,5},{8,10},{9,11},{10,... | collective-permute-start | bytes 86024 | tf_op jit(solution)/shard_map/ppermute | solution.py:713
  33.2 24.5 %collective-permute-start.3 = (f32[8,896]{1,0:T(8,128)S(1)}, f32[8,896]{1,0:T(8,128)S(1)}, u32[]{:S(2)}, u32[]{:S(2)}) collective-permute-start(f32[8,896]{1,0:T(8,128)S(1)} %get-tuple-element.70.source_ref), channel_id=1, source_target_pairs={{0,1},{1,0},{2,3},{3,2},{4,5},{5,4},{6,7},{7,6},{8,9},{9,8},{10,11... | collective-permute-start | bytes 86024 | tf_op jit(solution)/shard_map/ppermute | solution.py:713
  34.5 61.7 %collective-permute-start.9 = (bf16[1440,384]{1,0:T(8,128)(2,1)S(1)}, bf16[1440,384]{1,0:T(8,128)(2,1)}, u32[]{:S(2)}, u32[]{:S(2)}) collective-permute-start(bf16[1440,384]{1,0:T(8,128)(2,1)S(1)} %constant_dynamic-update-slice_fusion.refs_7_), channel_id=1, source_target_pairs={{0,4},{4,0},{8,12},{12,8},{16,20},{20,16},{24,28},{28,24},{1,5},{5... | collective-permute-start | bytes 3317768 | tf_op jit(solution)/shard_map/ppermute | solution.py:713
  54.2 41.9 %collective-permute-start.11 = (bf16[1440,384]{1,0:T(8,128)(2,1)S(1)}, bf16[1440,384]{1,0:T(8,128)(2,1)}, u32[]{:S(2)}, u32[]{:S(2)}) collective-permute-start(bf16[1440,384]{1,0:T(8,128)(2,1)S(1)} %collective-permute-done.10.refs_9_), channel_id=1, source_target_pairs={{0,4},{4,0},{8,12},{12,8},{16,20},{20,16},{24,28},{28,24},{1,5},{5... | collective-permute-start | bytes 3317768 | tf_op jit(solution)/shard_map/ppermute | solution.py:713
  55.7 38.4 %collective-permute-start = (bf16[256,1536]{1,0:T(8,128)(2,1)S(1)}, bf16[256,1536]{1,0:T(8,128)(2,1)}, u32[]{:S(2)}, u32[]{:S(2)}) collective-permute-start(bf16[256,1536]{1,0:T(8,128)(2,1)S(1)} %copy-done.15), channel_id=1, source_target_pairs={{0,1},{1,0},{2,3},{3,2},{4,5},{5,4},{6,7},{7,6},{8,9},{9,8},{10,11... | collective-permute-start | bytes 2359304 | tf_op jit(solution)/shard_map/ppermute | solution.py:713
  57.1 38.4 %collective-permute-start.1 = (bf16[256,1536]{1,0:T(8,128)(2,1)S(1)}, bf16[256,1536]{1,0:T(8,128)(2,1)}, u32[]{:S(2)}, u32[]{:S(2)}) collective-permute-start(bf16[256,1536]{1,0:T(8,128)(2,1)S(1)} %copy-done.15), channel_id=1, source_target_pairs={{0,2},{1,3},{2,0},{3,1},{4,6},{5,7},{6,4},{7,5},{8,10},{9,11},{10,... | collective-permute-start | bytes 2359304 | tf_op jit(solution)/shard_map/ppermute | solution.py:713
  57.7 35.0 %collective-permute-start.2 = (bf16[256,1536]{1,0:T(8,128)(2,1)S(1)}, bf16[256,1536]{1,0:T(8,128)(2,1)}, u32[]{:S(2)}, u32[]{:S(2)}) collective-permute-start(bf16[256,1536]{1,0:T(8,128)(2,1)S(1)} %copy-done.15), channel_id=1, source_target_pairs={{0,3},{1,2},{2,1},{3,0},{4,7},{5,6},{6,5},{7,4},{8,11},{9,10},{10,... | collective-permute-start | bytes 2359304 | tf_op jit(solution)/shard_map/ppermute | solution.py:713
  92.7 42.8 %collective-permute-start.15 = (bf16[256,1536]{1,0:T(8,128)(2,1)}, bf16[256,1536]{1,0:T(8,128)(2,1)S(1)}, u32[]{:S(2)}, u32[]{:S(2)}) collective-permute-start(bf16[256,1536]{1,0:T(8,128)(2,1)} %refs_2_.1), channel_id=1, source_target_pairs={{0,1},{1,0},{2,3},{3,2},{4,5},{5,4},{6,7},{7,6},{8,9},{9,8},{10,11... | collective-permute-start | bytes 2359304 | tf_op jit(solution)/shard_map/ppermute | solution.py:713
  94.1 41.3 %collective-permute-start.16 = (bf16[256,1536]{1,0:T(8,128)(2,1)}, bf16[256,1536]{1,0:T(8,128)(2,1)S(1)}, u32[]{:S(2)}, u32[]{:S(2)}) collective-permute-start(bf16[256,1536]{1,0:T(8,128)(2,1)} %refs_2_.1), channel_id=1, source_target_pairs={{0,2},{1,3},{2,0},{3,1},{4,6},{5,7},{6,4},{7,5},{8,10},{9,11},{10,... | collective-permute-start | bytes 2359304 | tf_op jit(solution)/shard_map/ppermute | solution.py:713
  95.5 40.0 %collective-permute-start.17 = (bf16[256,1536]{1,0:T(8,128)(2,1)}, bf16[256,1536]{1,0:T(8,128)(2,1)S(1)}, u32[]{:S(2)}, u32[]{:S(2)}) collective-permute-start(bf16[256,1536]{1,0:T(8,128)(2,1)} %refs_2_.1), channel_id=1, source_target_pairs={{0,3},{1,2},{2,1},{3,0},{4,7},{5,6},{6,5},{7,4},{8,11},{9,10},{10,... | collective-permute-start | bytes 2359304 | tf_op jit(solution)/shard_map/ppermute | solution.py:713
  113.5 53.2 %copy-start = (f32[1024,1920]{1,0:T(8,128)}, f32[1024,1920]{1,0:T(8,128)S(1)}, u32[]{:S(2)}) copy-start(f32[1024,1920]{1,0:T(8,128)S(1)} %get-tuple-element.74.z_ref.v_ref.shared_ref.refs_4_.refs_1_.refs_13_) | copy-start | bytes 23592964
  143.9 11.3 %collective-permute-start.18 = (f32[32,256]{1,0:T(8,128)S(1)}, f32[32,256]{1,0:T(8,128)S(1)}, u32[]{:S(2)}, u32[]{:S(2)}) collective-permute-start(f32[32,256]{1,0:T(8,128)S(1)} %get-tuple-element.82.refs_0_.refs_8_), channel_id=1, source_target_pairs={{0,1},{1,0},{2,3},{3,2},{4,5},{5,4},{6,7},{7,6},{8,9},{9,8},{10,11... | collective-permute-start | bytes 98312 | tf_op jit(solution)/shard_map/ppermute | solution.py:713
  145.3 10.5 %collective-permute-start.19 = (f32[32,256]{1,0:T(8,128)S(1)}, f32[32,256]{1,0:T(8,128)S(1)}, u32[]{:S(2)}, u32[]{:S(2)}) collective-permute-start(f32[32,256]{1,0:T(8,128)S(1)} %get-tuple-element.82.refs_0_.refs_8_), channel_id=1, source_target_pairs={{0,2},{1,3},{2,0},{3,1},{4,6},{5,7},{6,4},{7,5},{8,10},{9,11},{10,... | collective-permute-start | bytes 98312 | tf_op jit(solution)/shard_map/ppermute | solution.py:713
  146.7 9.1 %collective-permute-start.20 = (f32[32,256]{1,0:T(8,128)S(1)}, f32[32,256]{1,0:T(8,128)S(1)}, u32[]{:S(2)}, u32[]{:S(2)}) collective-permute-start(f32[32,256]{1,0:T(8,128)S(1)} %get-tuple-element.82.refs_0_.refs_8_), channel_id=1, source_target_pairs={{0,3},{1,2},{2,1},{3,0},{4,7},{5,6},{6,5},{7,4},{8,11},{9,10},{10,... | collective-permute-start | bytes 98312 | tf_op jit(solution)/shard_map/ppermute | solution.py:713
  152.3 70.5 %collective-permute-start.12 = (bf16[256,1536]{1,0:T(8,128)(2,1)}, bf16[256,1536]{1,0:T(8,128)(2,1)}, u32[]{:S(2)}, u32[]{:S(2)}) collective-permute-start(bf16[256,1536]{1,0:T(8,128)(2,1)} %get-tuple-element.77), channel_id=1, source_target_pairs={{0,1},{1,0},{2,3},{3,2},{4,5},{5,4},{6,7},{7,6},{8,9},{9,8},{10,11... | collective-permute-start | bytes 2359304 | tf_op jit(solution)/shard_map/ppermute | solution.py:713
  153.8 80.0 %collective-permute-start.13 = (bf16[256,1536]{1,0:T(8,128)(2,1)}, bf16[256,1536]{1,0:T(8,128)(2,1)}, u32[]{:S(2)}, u32[]{:S(2)}) collective-permute-start(bf16[256,1536]{1,0:T(8,128)(2,1)} %get-tuple-element.78), channel_id=1, source_target_pairs={{0,2},{1,3},{2,0},{3,1},{4,6},{5,7},{6,4},{7,5},{8,10},{9,11},{10,... | collective-permute-start | bytes 2359304 | tf_op jit(solution)/shard_map/ppermute | solution.py:713
  155.2 87.5 %collective-permute-start.14 = (bf16[256,1536]{1,0:T(8,128)(2,1)}, bf16[256,1536]{1,0:T(8,128)(2,1)}, u32[]{:S(2)}, u32[]{:S(2)}) collective-permute-start(bf16[256,1536]{1,0:T(8,128)(2,1)} %get-tuple-element.79), channel_id=1, source_target_pairs={{0,3},{1,2},{2,1},{3,0},{4,7},{5,6},{6,5},{7,4},{8,11},{9,10},{10,... | collective-permute-start | bytes 2359304 | tf_op jit(solution)/shard_map/ppermute | solution.py:713
  206.7 36.4 %collective-permute-start.21 = (bf16[256,1536]{1,0:T(8,128)(2,1)}, bf16[256,1536]{1,0:T(8,128)(2,1)}, u32[]{:S(2)}, u32[]{:S(2)}) collective-permute-start(bf16[256,1536]{1,0:T(8,128)(2,1)} %get-tuple-element.108), channel_id=1, source_target_pairs={{0,1},{1,0},{2,3},{3,2},{4,5},{5,4},{6,7},{7,6},{8,9},{9,8},{10,11... | collective-permute-start | bytes 2359304 | tf_op jit(solution)/shard_map/ppermute | solution.py:713
  208.2 35.0 %collective-permute-start.22 = (bf16[256,1536]{1,0:T(8,128)(2,1)}, bf16[256,1536]{1,0:T(8,128)(2,1)}, u32[]{:S(2)}, u32[]{:S(2)}) collective-permute-start(bf16[256,1536]{1,0:T(8,128)(2,1)} %get-tuple-element.109), channel_id=1, source_target_pairs={{0,2},{1,3},{2,0},{3,1},{4,6},{5,7},{6,4},{7,5},{8,10},{9,11},{10,... | collective-permute-start | bytes 2359304 | tf_op jit(solution)/shard_map/ppermute | solution.py:713
  222.8 20.8 %collective-permute-start.23 = (bf16[256,1536]{1,0:T(8,128)(2,1)S(1)}, bf16[256,1536]{1,0:T(8,128)(2,1)S(1)}, u32[]{:S(2)}, u32[]{:S(2)}) collective-permute-start(bf16[256,1536]{1,0:T(8,128)(2,1)S(1)} %copy-done.51), channel_id=1, source_target_pairs={{0,3},{1,2},{2,1},{3,0},{4,7},{5,6},{6,5},{7,4},{8,11},{9,10},{10,... | collective-permute-start | bytes 2359304 | tf_op jit(solution)/shard_map/ppermute | solution.py:713
  233.8 15.8 %collective-permute-start.47 = (bf16[256,1536]{1,0:T(8,128)(2,1)}, bf16[256,1536]{1,0:T(8,128)(2,1)}, u32[]{:S(2)}, u32[]{:S(2)}) collective-permute-start(bf16[256,1536]{1,0:T(8,128)(2,1)} %get-tuple-element.125), channel_id=1, source_target_pairs={{0,4},{4,0},{8,12},{12,8},{16,20},{20,16},{24,28},{28,24},{1,5},{5... | collective-permute-start | bytes 2359304 | tf_op jit(solution)/shard_map/ppermute | solution.py:713
  242.6 12.3 %collective-permute-start.31 = (bf16[320,1536]{1,0:T(8,128)(2,1)}, bf16[320,1536]{1,0:T(8,128)(2,1)}, u32[]{:S(2)}, u32[]{:S(2)}) collective-permute-start(bf16[320,1536]{1,0:T(8,128)(2,1)} %get-tuple-element.121), channel_id=1, source_target_pairs={{0,4},{4,0},{8,12},{12,8},{16,20},{20,16},{24,28},{28,24},{1,5},{5... | collective-permute-start | bytes 2949128 | tf_op jit(solution)/shard_map/ppermute | solution.py:713
  243.1 17.1 %collective-permute-start.39 = (bf16[384,1536]{1,0:T(8,128)(2,1)}, bf16[384,1536]{1,0:T(8,128)(2,1)}, u32[]{:S(2)}, u32[]{:S(2)}) collective-permute-start(bf16[384,1536]{1,0:T(8,128)(2,1)} %get-tuple-element.123), channel_id=1, source_target_pairs={{0,4},{4,0},{8,12},{12,8},{16,20},{20,16},{24,28},{28,24},{1,5},{5... | collective-permute-start | bytes 3538952 | tf_op jit(solution)/shard_map/ppermute | solution.py:713
  243.2 13.9 %collective-permute-start.55 = (bf16[384,1536]{1,0:T(8,128)(2,1)}, bf16[384,1536]{1,0:T(8,128)(2,1)}, u32[]{:S(2)}, u32[]{:S(2)}) collective-permute-start(bf16[384,1536]{1,0:T(8,128)(2,1)} %get-tuple-element.128), channel_id=1, source_target_pairs={{0,4},{4,0},{8,12},{12,8},{16,20},{20,16},{24,28},{28,24},{1,5},{5... | collective-permute-start | bytes 3538952 | tf_op jit(solution)/shard_map/ppermute | solution.py:713
  251.9 13.1 %collective-permute-start.50 = (bf16[256,384]{1,0:T(8,128)(2,1)S(1)}, bf16[256,384]{1,0:T(8,128)(2,1)S(1)}, u32[]{:S(2)}, u32[]{:S(2)}) collective-permute-start(bf16[256,384]{1,0:T(8,128)(2,1)S(1)} %get-tuple-element.137), channel_id=1, source_target_pairs={{0,3},{1,2},{2,1},{3,0},{4,7},{5,6},{6,5},{7,4},{8,11},{9,10},{10,... | collective-permute-start | bytes 589832 | tf_op jit(solution)/shard_map/ppermute | solution.py:713
  254.2 12.8 %collective-permute-start.49 = (bf16[256,384]{1,0:T(8,128)(2,1)}, bf16[256,384]{1,0:T(8,128)(2,1)S(1)}, u32[]{:S(2)}, u32[]{:S(2)}) collective-permute-start(bf16[256,384]{1,0:T(8,128)(2,1)} %get-tuple-element.138), channel_id=1, source_target_pairs={{0,2},{1,3},{2,0},{3,1},{4,6},{5,7},{6,4},{7,5},{8,10},{9,11},{10,... | collective-permute-start | bytes 589832 | tf_op jit(solution)/shard_map/ppermute | solution.py:713
  254.9 77.9 %copy-start.68 = (f32[21392]{0:T(1024)}, f32[21392]{0:T(1024)S(1)}, u32[]{:S(2)}) copy-start(f32[21392]{0:T(1024)S(1)} %concatenate.44) | copy-start | bytes 256708
  254.9 12.7 %collective-permute-start.48 = (bf16[256,384]{1,0:T(8,128)(2,1)}, bf16[256,384]{1,0:T(8,128)(2,1)S(1)}, u32[]{:S(2)}, u32[]{:S(2)}) collective-permute-start(bf16[256,384]{1,0:T(8,128)(2,1)} %get-tuple-element.139), channel_id=1, source_target_pairs={{0,1},{1,0},{2,3},{3,2},{4,5},{5,4},{6,7},{7,6},{8,9},{9,8},{10,11... | collective-permute-start | bytes 589832 | tf_op jit(solution)/shard_map/ppermute | solution.py:713
  257.1 13.0 %collective-permute-start.32 = (bf16[320,384]{1,0:T(8,128)(2,1)S(1)}, bf16[320,384]{1,0:T(8,128)(2,1)S(1)}, u32[]{:S(2)}, u32[]{:S(2)}) collective-permute-start(bf16[320,384]{1,0:T(8,128)(2,1)S(1)} %get-tuple-element.135), channel_id=1, source_target_pairs={{0,1},{1,0},{2,3},{3,2},{4,5},{5,4},{6,7},{7,6},{8,9},{9,8},{10,11... | collective-permute-start | bytes 737288 | tf_op jit(solution)/shard_map/ppermute | solution.py:713
  260.2 31.3 %collective-permute-start.56 = (bf16[384,1536]{1,0:T(8,128)(2,1)S(1)}, bf16[384,1536]{1,0:T(8,128)(2,1)S(1)}, u32[]{:S(2)}, u32[]{:S(2)}) collective-permute-start(bf16[384,1536]{1,0:T(8,128)(2,1)S(1)} %add_convert_fusion.2), channel_id=1, source_target_pairs={{0,8},{4,12},{24,16},{28,20},{1,9},{5,13},{25,17},{29,21},{2,10},{... | collective-permute-start | bytes 3538952 | tf_op jit(solution)/shard_map/ppermute | solution.py:733
  265.0 11.4 %collective-permute-start.42 = (bf16[384,384]{1,0:T(8,128)(2,1)S(1)}, bf16[384,384]{1,0:T(8,128)(2,1)S(1)}, u32[]{:S(2)}, u32[]{:S(2)}) collective-permute-start(bf16[384,384]{1,0:T(8,128)(2,1)S(1)} %get-tuple-element.130), channel_id=1, source_target_pairs={{0,3},{1,2},{2,1},{3,0},{4,7},{5,6},{6,5},{7,4},{8,11},{9,10},{10,... | collective-permute-start | bytes 884744 | tf_op jit(solution)/shard_map/ppermute | solution.py:713
  267.0 15.8 %collective-permute-start.41 = (bf16[384,384]{1,0:T(8,128)(2,1)S(1)}, bf16[384,384]{1,0:T(8,128)(2,1)S(1)}, u32[]{:S(2)}, u32[]{:S(2)}) collective-permute-start(bf16[384,384]{1,0:T(8,128)(2,1)S(1)} %get-tuple-element.131), channel_id=1, source_target_pairs={{0,2},{1,3},{2,0},{3,1},{4,6},{5,7},{6,4},{7,5},{8,10},{9,11},{10,... | collective-permute-start | bytes 884744 | tf_op jit(solution)/shard_map/ppermute | solution.py:713
  267.7 16.7 %collective-permute-start.40 = (bf16[384,384]{1,0:T(8,128)(2,1)S(1)}, bf16[384,384]{1,0:T(8,128)(2,1)S(1)}, u32[]{:S(2)}, u32[]{:S(2)}) collective-permute-start(bf16[384,384]{1,0:T(8,128)(2,1)S(1)} %get-tuple-element.132), channel_id=1, source_target_pairs={{0,1},{1,0},{2,3},{3,2},{4,5},{5,4},{6,7},{7,6},{8,9},{9,8},{10,11... | collective-permute-start | bytes 884744 | tf_op jit(solution)/shard_map/ppermute | solution.py:713
  270.1 21.3 %collective-permute-start.33 = (bf16[320,384]{1,0:T(8,128)(2,1)S(1)}, bf16[320,384]{1,0:T(8,128)(2,1)S(1)}, u32[]{:S(2)}, u32[]{:S(2)}) collective-permute-start(bf16[320,384]{1,0:T(8,128)(2,1)S(1)} %get-tuple-element.134), channel_id=1, source_target_pairs={{0,2},{1,3},{2,0},{3,1},{4,6},{5,7},{6,4},{7,5},{8,10},{9,11},{10,... | collective-permute-start | bytes 737288 | tf_op jit(solution)/shard_map/ppermute | solution.py:713
  276.4 15.0 %collective-permute-start.34 = (bf16[320,384]{1,0:T(8,128)(2,1)S(1)}, bf16[320,384]{1,0:T(8,128)(2,1)S(1)}, u32[]{:S(2)}, u32[]{:S(2)}) collective-permute-start(bf16[320,384]{1,0:T(8,128)(2,1)S(1)} %get-tuple-element.133), channel_id=1, source_target_pairs={{0,3},{1,2},{2,1},{3,0},{4,7},{5,6},{6,5},{7,4},{8,11},{9,10},{10,... | collective-permute-start | bytes 737288 | tf_op jit(solution)/shard_map/ppermute | solution.py:713
  282.8 51.4 %collective-permute-start.51 = (bf16[1024,384]{1,0:T(8,128)(2,1)S(1)}, bf16[1024,384]{1,0:T(8,128)(2,1)S(1)}, u32[]{:S(2)}, u32[]{:S(2)}) collective-permute-start(bf16[1024,384]{1,0:T(8,128)(2,1)S(1)} %pad_maximum_fusion.1), channel_id=1, source_target_pairs={{0,8},{4,12},{24,16},{28,20},{1,9},{5,13},{25,17},{29,21},{2,10},{... | collective-permute-start | bytes 2359304 | tf_op jit(solution)/shard_map/ppermute | solution.py:733
  284.5 47.2 %collective-permute-start.43 = (bf16[1536,384]{1,0:T(8,128)(2,1)S(1)}, bf16[1536,384]{1,0:T(8,128)(2,1)S(1)}, u32[]{:S(2)}, u32[]{:S(2)}) collective-permute-start(bf16[1536,384]{1,0:T(8,128)(2,1)S(1)} %pad_maximum_fusion), channel_id=1, source_target_pairs={{0,8},{4,12},{24,16},{28,20},{1,9},{5,13},{25,17},{29,21},{2,10},{... | collective-permute-start | bytes 3538952 | tf_op jit(solution)/shard_map/ppermute | solution.py:733
  291.8 51.0 %collective-permute-start.57 = (bf16[384,1536]{1,0:T(8,128)(2,1)S(1)}, bf16[384,1536]{1,0:T(8,128)(2,1)S(1)}, u32[]{:S(2)}, u32[]{:S(2)}) collective-permute-start(bf16[384,1536]{1,0:T(8,128)(2,1)S(1)} %add_convert_fusion.1), channel_id=1, source_target_pairs={{8,16},{12,20},{16,8},{20,12},{9,17},{13,21},{17,9},{21,13},{10,18... | collective-permute-start | bytes 3538952 | tf_op jit(solution)/shard_map/ppermute | solution.py:735
  292.6 48.7 %collective-permute-start.35 = (bf16[704,384]{1,0:T(8,128)(2,1)S(1)}, bf16[704,384]{1,0:T(8,128)(2,1)S(1)}, u32[]{:S(2)}, u32[]{:S(2)}) collective-permute-start(bf16[704,384]{1,0:T(8,128)(2,1)S(1)} %fusion), channel_id=1, source_target_pairs={{0,8},{4,12},{24,16},{28,20},{1,9},{5,13},{25,17},{29,21},{2,10},{... | collective-permute-start | bytes 1622024 | tf_op jit(solution)/shard_map/ppermute | solution.py:733
  332.1 12.7 %collective-permute-start.44 = (bf16[1536,384]{1,0:T(8,128)(2,1)S(1)}, bf16[1536,384]{1,0:T(8,128)(2,1)S(1)}, u32[]{:S(2)}, u32[]{:S(2)}) collective-permute-start(bf16[1536,384]{1,0:T(8,128)(2,1)S(1)} %add_convert_fusion.4), channel_id=1, source_target_pairs={{8,16},{12,20},{16,8},{20,12},{9,17},{13,21},{17,9},{21,13},{10,18... | collective-permute-start | bytes 3538952 | tf_op jit(solution)/shard_map/ppermute | solution.py:735
  332.8 11.0 %collective-permute-start.25 = (f32[168,128]{1,0:T(8,128)S(1)}, f32[168,128]{1,0:T(8,128)S(1)}, u32[]{:S(2)}, u32[]{:S(2)}) collective-permute-start(f32[168,128]{1,0:T(8,128)S(1)} %pad_bitcast_fusion), channel_id=1, source_target_pairs={{0,2},{1,3},{2,0},{3,1},{4,6},{5,7},{6,4},{7,5},{8,10},{9,11},{10,... | collective-permute-start | bytes 258056 | tf_op jit(solution)/shard_map/ppermute | solution.py:713
  334.3 12.1 %collective-permute-start.26 = (f32[168,128]{1,0:T(8,128)S(1)}, f32[168,128]{1,0:T(8,128)S(1)}, u32[]{:S(2)}, u32[]{:S(2)}) collective-permute-start(f32[168,128]{1,0:T(8,128)S(1)} %pad_bitcast_fusion), channel_id=1, source_target_pairs={{0,3},{1,2},{2,1},{3,0},{4,7},{5,6},{6,5},{7,4},{8,11},{9,10},{10,... | collective-permute-start | bytes 258056 | tf_op jit(solution)/shard_map/ppermute | solution.py:713
  341.3 6.4 %collective-permute-start.24 = (f32[168,128]{1,0:T(8,128)S(1)}, f32[168,128]{1,0:T(8,128)S(1)}, u32[]{:S(2)}, u32[]{:S(2)}) collective-permute-start(f32[168,128]{1,0:T(8,128)S(1)} %pad_bitcast_fusion), channel_id=1, source_target_pairs={{0,1},{1,0},{2,3},{3,2},{4,5},{5,4},{6,7},{7,6},{8,9},{9,8},{10,11... | collective-permute-start | bytes 258056 | tf_op jit(solution)/shard_map/ppermute | solution.py:713
  342.8 25.6 %collective-permute-start.36 = (bf16[704,384]{1,0:T(8,128)(2,1)S(1)}, bf16[704,384]{1,0:T(8,128)(2,1)S(1)}, u32[]{:S(2)}, u32[]{:S(2)}) collective-permute-start(bf16[704,384]{1,0:T(8,128)(2,1)S(1)} %add_convert_fusion.11), channel_id=1, source_target_pairs={{8,16},{12,20},{16,8},{20,12},{9,17},{13,21},{17,9},{21,13},{10,18... | collective-permute-start | bytes 1622024 | tf_op jit(solution)/shard_map/ppermute | solution.py:735
  343.9 24.8 %collective-permute-start.52 = (bf16[1024,384]{1,0:T(8,128)(2,1)S(1)}, bf16[1024,384]{1,0:T(8,128)(2,1)S(1)}, u32[]{:S(2)}, u32[]{:S(2)}) collective-permute-start(bf16[1024,384]{1,0:T(8,128)(2,1)S(1)} %add_convert_fusion.8), channel_id=1, source_target_pairs={{8,16},{12,20},{16,8},{20,12},{9,17},{13,21},{17,9},{21,13},{10,18... | collective-permute-start | bytes 2359304 | tf_op jit(solution)/shard_map/ppermute | solution.py:735
  344.7 48.6 %collective-permute-start.58 = (bf16[384,1536]{1,0:T(8,128)(2,1)S(1)}, bf16[384,1536]{1,0:T(8,128)(2,1)S(1)}, u32[]{:S(2)}, u32[]{:S(2)}) collective-permute-start(bf16[384,1536]{1,0:T(8,128)(2,1)S(1)} %add_convert_fusion), channel_id=1, source_target_pairs={{8,0},{12,4},{16,24},{20,28},{9,1},{13,5},{17,25},{21,29},{10,2},{... | collective-permute-start | bytes 3538952 | tf_op jit(solution)/shard_map/ppermute | solution.py:737
  346.4 72.3 %collective-permute-start.45 = (bf16[1536,384]{1,0:T(8,128)(2,1)S(1)}, bf16[1536,384]{1,0:T(8,128)(2,1)S(1)}, u32[]{:S(2)}, u32[]{:S(2)}) collective-permute-start(bf16[1536,384]{1,0:T(8,128)(2,1)S(1)} %add_convert_fusion.3), channel_id=1, source_target_pairs={{8,0},{12,4},{16,24},{20,28},{9,1},{13,5},{17,25},{21,29},{10,2},{... | collective-permute-start | bytes 3538952 | tf_op jit(solution)/shard_map/ppermute | solution.py:737
  347.7 93.3 %collective-permute-start.28 = (f32[168,128]{1,0:T(8,128)S(1)}, f32[168,128]{1,0:T(8,128)S(1)}, u32[]{:S(2)}, u32[]{:S(2)}) collective-permute-start(f32[168,128]{1,0:T(8,128)S(1)} %add_add_fusion.1), channel_id=1, source_target_pairs={{0,8},{4,12},{8,0},{12,4},{16,24},{20,28},{24,16},{28,20},{1,9},{5... | collective-permute-start | bytes 258056 | tf_op jit(solution)/shard_map/ppermute | solution.py:713
  368.5 74.1 %collective-permute-start.29 = (f32[168,128]{1,0:T(8,128)S(1)}, f32[168,128]{1,0:T(8,128)S(1)}, u32[]{:S(2)}, u32[]{:S(2)}) collective-permute-start(f32[168,128]{1,0:T(8,128)S(1)} %add_add_fusion.1), channel_id=1, source_target_pairs={{0,12},{4,8},{8,4},{12,0},{16,28},{20,24},{24,20},{28,16},{1,13},{... | collective-permute-start | bytes 258056 | tf_op jit(solution)/shard_map/ppermute | solution.py:713
  368.6 73.0 %collective-permute-start.37 = (bf16[704,384]{1,0:T(8,128)(2,1)S(1)}, bf16[704,384]{1,0:T(8,128)(2,1)S(1)}, u32[]{:S(2)}, u32[]{:S(2)}) collective-permute-start(bf16[704,384]{1,0:T(8,128)(2,1)S(1)} %add_convert_fusion.10), channel_id=1, source_target_pairs={{8,0},{12,4},{16,24},{20,28},{9,1},{13,5},{17,25},{21,29},{10,2},{... | collective-permute-start | bytes 1622024 | tf_op jit(solution)/shard_map/ppermute | solution.py:737
  393.4 47.6 %collective-permute-start.53 = (bf16[1024,384]{1,0:T(8,128)(2,1)S(1)}, bf16[1024,384]{1,0:T(8,128)(2,1)S(1)}, u32[]{:S(2)}, u32[]{:S(2)}) collective-permute-start(bf16[1024,384]{1,0:T(8,128)(2,1)S(1)} %add_convert_fusion.7), channel_id=1, source_target_pairs={{8,0},{12,4},{16,24},{20,28},{9,1},{13,5},{17,25},{21,29},{10,2},{... | collective-permute-start | bytes 2359304 | tf_op jit(solution)/shard_map/ppermute | solution.py:737
  418.6 35.8 %collective-permute-start.59 = (bf16[384,1536]{1,0:T(8,128)(2,1)S(1)}, bf16[384,1536]{1,0:T(8,128)(2,1)}, u32[]{:S(2)}, u32[]{:S(2)}) collective-permute-start(bf16[384,1536]{1,0:T(8,128)(2,1)S(1)} %broadcast_select_fusion.refs_1_), channel_id=1, source_target_pairs={{0,4},{4,0},{8,12},{12,8},{16,20},{20,16},{24,28},{28,24},{1,5},{5... | collective-permute-start | bytes 3538952 | tf_op jit(solution)/shard_map/ppermute | solution.py:713
  441.0 17.2 %collective-permute-start.46 = (bf16[1536,384]{1,0:T(8,128)(2,1)S(1)}, bf16[1536,384]{1,0:T(8,128)(2,1)}, u32[]{:S(2)}, u32[]{:S(2)}) collective-permute-start(bf16[1536,384]{1,0:T(8,128)(2,1)S(1)} %broadcast_select_fusion.1.refs_1_), channel_id=1, source_target_pairs={{0,4},{4,0},{8,12},{12,8},{16,20},{20,16},{24,28},{28,24},{1,5},{5... | collective-permute-start | bytes 3538952 | tf_op jit(solution)/shard_map/ppermute | solution.py:713
  441.1 2.9 collective-permute-start.27
  441.6 16.5 %collective-permute-start.54 = (bf16[1024,384]{1,0:T(8,128)(2,1)S(1)}, bf16[1024,384]{1,0:T(8,128)(2,1)}, u32[]{:S(2)}, u32[]{:S(2)}) collective-permute-start(bf16[1024,384]{1,0:T(8,128)(2,1)S(1)} %broadcast_select_fusion.2.refs_3_), channel_id=1, source_target_pairs={{0,4},{4,0},{8,12},{12,8},{16,20},{20,16},{24,28},{28,24},{1,5},{5... | collective-permute-start | bytes 2359304 | tf_op jit(solution)/shard_map/ppermute | solution.py:713
  442.6 20.6 %collective-permute-start.38 = (bf16[704,384]{1,0:T(8,128)(2,1)}, bf16[704,384]{1,0:T(8,128)(2,1)}, u32[]{:S(2)}, u32[]{:S(2)}) collective-permute-start(bf16[704,384]{1,0:T(8,128)(2,1)} %broadcast_select_fusion.3.refs_1_), channel_id=1, source_target_pairs={{0,4},{4,0},{8,12},{12,8},{16,20},{20,16},{24,28},{28,24},{1,5},{5... | collective-permute-start | bytes 1622024 | tf_op jit(solution)/shard_map/ppermute | solution.py:713
  444.0 7.1 %collective-permute-start.30 = (f32[168,128]{1,0:T(8,128)S(1)}, f32[168,128]{1,0:T(8,128)S(1)}, u32[]{:S(2)}, u32[]{:S(2)}) collective-permute-start(f32[168,128]{1,0:T(8,128)S(1)} %add_add_fusion), channel_id=1, source_target_pairs={{0,16},{4,20},{8,24},{12,28},{16,0},{20,4},{24,8},{28,12},{1,17},{... | collective-permute-start | bytes 258056 | tf_op jit(solution)/shard_map/ppermute | solution.py:713
  (83 other events, 803.2 us)
where the time goes:
time: 468 us; the launch traced here: 467 us
  waiting for transfers between devices  199 us (43%)
  Pallas kernels  125 us (27%)
  starting transfers between devices  86.3 us (18%)
  local copies, waits for them, and re-layouts  42.4 us (9%)
  other arithmetic  11.4 us (2%)
    pallas_call x19, Pallas kernels, run(): pl.pallas_call(kernel, out_shape=out_shape, cost_estimate=pl.CostEstimate...  125 us
    ppermute x48, waiting for transfers between devices, swap(): return lax.ppermute(value, axis, [(i, i ^ step) for i in range(size)])  91.2 us
    ppermute x4, waiting for transfers between devices, line_sum(): back = lax.ppermute(value, 'rep', outward)  69.2 us
    ppermute x48, starting transfers between devices, swap(): return lax.ppermute(value, axis, [(i, i ^ step) for i in range(size)])  65.8 us
    ppermute x4, waiting for transfers between devices, line_sum(): got = lax.ppermute(value, 'rep', inward)  38.9 us
    unnamed x182, local copies, waits for them, and re-layouts  30.5 us
    ppermute x4, starting transfers between devices, line_sum(): got = lax.ppermute(value, 'rep', inward)  12.3 us
  transfers between devices with their start and end apart: 60, of which 15 were waited for; matrix products, arithmetic and copies ran while one was open for 5% of the time, Pallas kernels for 24%

commit v1 on v0

--- a/solution.py
+++ b/solution.py
@@ -327,28 +327,35 @@
         square_sum_ref[...] = jnp.zeros_like(square_sum_ref)
 
     masks = [mask_ref[:, s * LANES : (s + 1) * LANES] for s in range(KERNEL - 1)]
-    taps = [taps_v_ref[k : k + 1, :] for k in range(KERNEL)]
-    total = conv_forward(v_ref[...], masks, taps, taps_v_ref[KERNEL : KERNEL + 1, :])
-    total_ref[...] = total
-    values = total * sigmoid(total)
-    columns, rows, stepx, low, _ = pair_columns(pair, run_ref, runt_ref, step_ref)
-    fed = (stepx * values).astype(BF)
-    skipped = taps_v_ref[KERNEL + 1 : KERNEL + 2, :] * values
-    cut = fed.shape[0] // 2
-    for n in range(2):
-        at = slice(n * cut, (n + 1) * cut)
-        seen = (n + 1) * cut
-        affinity = affinity_ref[at, :seen]
-        parts = []
-        for e in range(2):
-            decay = jnp.exp(jnp.minimum(columns[e][at] - rows[e][:, :seen], 0.0))
-            parts.append(mm((decay * affinity).astype(BF), fed[:seen], NN))
-        scanned = jnp.where(low[at], parts[0], parts[1]) + skipped[at]
-        z = z_ref[at, :]
+    count = v_ref.shape[1] // LANES
+    squares = 0.0
+    for m in range(count):
+        lanes = slice(m * LANES, (m + 1) * LANES)
+        taps = [taps_v_ref[k : k + 1, lanes] for k in range(KERNEL)]
+        total = conv_forward(v_ref[:, lanes], masks, taps, taps_v_ref[KERNEL : KERNEL + 1, lanes])
+        total_ref[:, lanes] = total
+        values = total * sigmoid(total)
+        columns, rows, stepx, low, _ = pair_columns(count * pair + m, run_ref, runt_ref, step_ref)
+        fed = (stepx * values).astype(BF)
+        skipped = taps_v_ref[KERNEL + 1 : KERNEL + 2, lanes] * values
+        cut = fed.shape[0] // 2
+        inner = []
+        for n in range(2):
+            at = slice(n * cut, (n + 1) * cut)
+            seen = (n + 1) * cut
+            affinity = affinity_ref[at, :seen]
+            parts = []
+            for e in range(2):
+                decay = jnp.exp(jnp.minimum(columns[e][at] - rows[e][:, :seen], 0.0))
+                parts.append(mm((decay * affinity).astype(BF), fed[:seen], NN))
+            inner.append(jnp.where(low[at], parts[0], parts[1]))
+        scanned = jnp.concatenate(inner, axis=0) + skipped
+        z = z_ref[:, lanes]
         g = scanned * (z * sigmoid(z))
-        scanned_ref[at, :] = scanned
-        gated_ref[at, :] = (g * taps_v_ref[KERNEL + 2 : KERNEL + 3, :]).astype(BF)
-        square_sum_ref[at, :] = square_sum_ref[at, :] + g * g
+        scanned_ref[:, lanes] = scanned
+        gated_ref[:, lanes] = (g * taps_v_ref[KERNEL + 2 : KERNEL + 3, lanes]).astype(BF)
+        squares = squares + g * g
+    square_sum_ref[...] = square_sum_ref[...] + squares
 
     @pl.when(pair == pl.num_programs(1) - 1)
     def _():
@@ -358,15 +365,20 @@
 
 def mixgrad_kernel(groups, *refs):
     cots = refs[:groups]
-    out_w_ref, gated_ref, square_ref, dm_ref, sums_ref = refs[groups:]
+    out_w_ref, gated_ref, square_ref, dm_ref, sums_ref, cot_ref, sems = refs[groups:]
     span = cots[0].shape[0]
+    loads = [pltpu.make_async_copy(cots[r], cot_ref.at[r], sems.at[r]) for r in range(groups)]
+    for load in loads:
+        load.start()
+    for load in loads:
+        load.wait()
     width = 384 if out_w_ref.shape[0] % 384 == 0 else LANES
 
     def column(n, carry):
         cols = pl.ds(pl.multiple_of(n * width, LANES), width)
         weight = out_w_ref[cols, :]
         for r in range(groups):
-            dm_ref[r * span : (r + 1) * span, cols] = mm(cots[r][...], weight, NT)
+            dm_ref[r * span : (r + 1) * span, cols] = mm(cot_ref[r], weight, NT)
         return carry
 
     lax.fori_loop(0, out_w_ref.shape[0] // width, column, 0)
@@ -541,14 +553,19 @@
     place_ref = refs[0]
     left_refs = refs[1 : 1 + lefts]
     right_refs = refs[1 + lefts : 1 + lefts + rights]
-    given_ref, kept_ref, stage_ref, sems = refs[1 + lefts + rights :]
+    given_ref, kept_ref, stage_ref, sems, right_ref, right_sems = refs[1 + lefts + rights :]
     core = place_ref[1]
     model = stage_ref.shape[1]
+    loads = [pltpu.make_async_copy(right_refs[n], right_ref.at[n], right_sems.at[n]) for n in range(rights)]
+    for load in loads:
+        load.start()
+    for load in loads:
+        load.wait()
     width = 384 if model % 384 == 0 else LANES
 
     def column(n, carry):
         cols = pl.ds(pl.multiple_of(n * width, LANES), width)
-        right = jnp.concatenate([ref[:, cols] for ref in right_refs], axis=0)
+        right = jnp.concatenate([right_ref[n, :, cols] for n in range(rights)], axis=0)
         row = 0
         for ref in left_refs:
             rows = ref.shape[1]
@@ -584,9 +601,14 @@
         (half, half),
         2 * tokens * rows * model,
         2 * tokens * (rows + model) + 2 * rows * model,
-        in_specs=[pl.BlockSpec(memory_space=pltpu.SMEM)] + [VM] * (len(lefts) + len(rights)),
+        in_specs=[pl.BlockSpec(memory_space=pltpu.SMEM)] + [VM] * len(lefts) + [HBM] * len(rights),
         out_specs=(HBM, HBM),
-        scratch_shapes=[pltpu.VMEM((rows, model), BF), pltpu.SemaphoreType.DMA((2 * len(parts),))],
+        scratch_shapes=[
+            pltpu.VMEM((rows, model), BF),
+            pltpu.SemaphoreType.DMA((2 * len(parts),)),
+            pltpu.VMEM((len(rights), rights[0].shape[0], model), BF),
+            pltpu.SemaphoreType.DMA((len(rights),)),
+        ],
     )(place, *lefts, *rights)
 
 
@@ -906,6 +928,8 @@
     seg_spec = pl.BlockSpec((8, span), lambda r, p: (r, 0))
     shared_spec = per_row(padded, 2 * inner // padded)
     scan_flops = 4 * whole * span * inner
+    joint = 2 if pairs % 2 == 0 else 1
+    broad = lambda col: pl.BlockSpec((span, joint * LANES), lambda r, p: (r, col + p))
     side = lambda w: jax.ShapeDtypeStruct((whole, w), F32)
     flipped_spec = pl.BlockSpec((LANES, span), lambda r, p: (r, 0))
     kept_shapes = (
@@ -940,18 +964,18 @@
         8 * scan_flops,
         20 * whole * inner,
         mib=12,
-        grid=(groups, pairs),
+        grid=(groups, pairs // joint),
         in_specs=[
             smem,
-            tile(0),
-            tile(pairs),
+            broad(0),
+            broad(pairs // joint),
             shared_spec,
             seg_spec,
             fixed((8, conv - full)),
-            pair_cols,
+            pl.BlockSpec((8, joint * LANES), lambda r, p: (0, p)),
             fixed((8, LANES)),
         ],
-        out_specs=(tile(0), tile(0), tile(0), seg_spec) + kept_specs,
+        out_specs=(broad(0), broad(0), broad(0), seg_spec) + kept_specs,
         scratch_shapes=[pltpu.VMEM((span, span), F32), pltpu.VMEM((span, LANES), F32)],
     )(place, projected, projected, projected, segs, taps_s, taps_v, heads)
 
@@ -961,8 +985,9 @@
         (jax.ShapeDtypeStruct((whole, inner), F32), jax.ShapeDtypeStruct((8 * groups, span), F32)),
         proj_flops,
         2 * whole * model + 6 * whole * inner + 2 * inner * model,
-        in_specs=[VM] * (groups + 3),
+        in_specs=[HBM] * groups + [VM] * 3,
         out_specs=(VM, VM),
+        scratch_shapes=[pltpu.VMEM((groups, span, model), BF), pltpu.SemaphoreType.DMA((groups,))],
     )(*cots, out_weight, gated, squares)
     sums_all = [sums] + [swap(sums, "fsdp", k) for k in range(1, groups)]
 
@@ -1097,9 +1122,7 @@
     def returned(part):
         return [part, swap(part, "rep", 1)]
 
-    grad_outproj = place_rows(
-        place, 1, out_weight.shape, ((((inner // 2, 0),), 0, None),), returned(out_part)
-    )
+    grad_outproj = place_rows(place, 1, out_weight.shape, ((((inner // 2, 0),), 0, None),), returned(out_part))
     early = returned(z_part) + returned(v1_part)
     gin = place_rows(
         place,

time: 468 us -> 466 us (level)
  no operation moved by 1% of the time
where the time goes in v1:
time: 466 us; the launch traced here: 464 us
  waiting for transfers between devices  199 us (43%)
  Pallas kernels  123 us (26%)
  starting transfers between devices  86.3 us (19%)
  local copies, waits for them, and re-layouts  42.4 us (9%)
  other arithmetic  11.4 us (2%)
    pallas_call x19, Pallas kernels, run(): pl.pallas_call(kernel, out_shape=out_shape, cost_estimate=pl.CostEstimate...  123 us
    ppermute x48, waiting for transfers between devices, swap(): return lax.ppermute(value, axis, [(i, i ^ step) for i in range(size)])  91.2 us
    ppermute x4, waiting for transfers between devices, line_sum(): back = lax.ppermute(value, 'rep', outward)  69.2 us
    ppermute x48, starting transfers between devices, swap(): return lax.ppermute(value, axis, [(i, i ^ step) for i in range(size)])  65.8 us
    ppermute x4, waiting for transfers between devices, line_sum(): got = lax.ppermute(value, 'rep', inward)  38.9 us
    unnamed x182, local copies, waits for them, and re-layouts  30.5 us
    ppermute x4, starting transfers between devices, line_sum(): got = lax.ppermute(value, 'rep', inward)  12.3 us
  transfers between devices with their start and end apart: 60, of which 15 were waited for; matrix products, arithmetic and copies ran while one was open for 5% of the time, Pallas kernels for 24%

profile of v1, /device:TPU:0, one launch (start us, length us, event | category | flops | bytes accessed | tf_op | source)
XLA Modules:
  0.0 464.3 jit_solution(5998603427849593093)
XLA Ops:
  2.1 2.4 copy-done.7
  5.9 2.1 shard_map.203
  8.1 3.0 collective-permute-start.6
  11.1 1.5 collective-permute-start.7
  12.6 7.9 %collective-permute-done.6 = bf16[480,384]{1,0:T(8,128)(2,1)S(1)} collective-permute-done((bf16[480,384]{1,0:T(8,128)(2,1)S(1)}, bf16[480,384]{1,0:T(8,128)(2,1)S(1)}, u32[]{:S(2)}, u32[]{:S(2)}) %collective-permute-start.6) | collective-permute-done | bytes 368672 | tf_op jit(solution)/shard_map/ppermute | solution.py:735
  20.6 8.5 %collective-permute-done.7 = bf16[480,384]{1,0:T(8,128)(2,1)S(1)} collective-permute-done((bf16[480,384]{1,0:T(8,128)(2,1)S(1)}, bf16[480,384]{1,0:T(8,128)(2,1)S(1)}, u32[]{:S(2)}, u32[]{:S(2)}) %collective-permute-start.7) | collective-permute-done | bytes 368672 | tf_op jit(solution)/shard_map/ppermute | solution.py:735
  29.2 1.4 collective-permute-start.10
  30.6 1.5 collective-permute-start.5
  34.5 19.8 %collective-permute-done.10.refs_9_ = bf16[1440,384]{1,0:T(8,128)(2,1)S(1)} collective-permute-done((bf16[1440,384]{1,0:T(8,128)(2,1)S(1)}, bf16[1440,384]{1,0:T(8,128)(2,1)S(1)}, u32[]{:S(2)}, u32[]{:S(2)}) %collective-permute-start.10) | collective-permute-done | bytes 1105952 | tf_op jit(solution)/shard_map/ppermute | solution.py:735
  55.7 1.4 collective-permute-start
  57.7 1.5 collective-permute-start.2
  61.6 31.1 %collective-permute-done.2.refs_3_ = bf16[256,1536]{1,0:T(8,128)(2,1)} collective-permute-done((bf16[256,1536]{1,0:T(8,128)(2,1)S(1)}, bf16[256,1536]{1,0:T(8,128)(2,1)}, u32[]{:S(2)}, u32[]{:S(2)}) %collective-permute-start.2) | collective-permute-done | bytes 786464 | tf_op jit(solution)/shard_map/ppermute | solution.py:735
  92.7 1.5 collective-permute-start.15
  94.1 1.4 collective-permute-start.16
  96.2 2.4 copy-done.8
  98.6 13.1 %shard_map.205 = (bf16[1024,1536]{1,0:T(8,128)(2,1)S(1)}, f32[1024,1920]{1,0:T(8,128)S(1)}, bf16[1920,1536]{1,0:T(8,128)(2,1)S(1)}) custom-call(bf16[256,1536]{1,0:T(8,128)(2,1)S(1)} %copy-done.15, bf16[256,1536]{1,0:T(8,128)(2,1)} %collective-permute-done.refs_1_, bf16[256,1536]{1,0:T(8,128)(2,1)} %collective-permute-done.1.refs_2_, ...), custom_call_target="tpu_custom_call" | custom-call | flops 6039797760 | bytes 25952256 | tf_op jit(solution)/shard_map/pallas_call | solution.py:60
  111.7 1.8 copy-done.62
  113.5 16.1 %shard_map.206 = (f32[1024,768]{1,0:T(8,128)S(1)}, f32[1024,768]{1,0:T(8,128)S(1)}, bf16[1024,768]{1,0:T(8,128)(2,1)S(1)}, f32[32,256]{1,0:T(8,128)S(1)}, f32[10...) custom-call(s32[3]{0:T(128)S(1)} %pad_add_fusion.refs_0_.refs_5_.pla, ...), custom_call_target="tpu_custom_call" | custom-call | flops 6442450944 | bytes 15728640 | tf_op jit(solution)/shard_map/pallas_call | solution.py:60
  131.8 5.7 %shard_map.208 = (f32[1024,768]{1,0:T(8,128)S(1)}, f32[32,256]{1,0:T(8,128)S(1)}) custom-call(bf16[256,1536]{1,0:T(8,128)(2,1)} %refs_2_.1, bf16[256,1536]{1,0:T(8,128)(2,1)S(1)} %collective-permute-done.15.refs_1_.refs_3_, bf16[256,1536]{1,0:T(8,128)(2,1)S(1)} %collective-permute-done.16.refs_2_.refs_4_, ...), custom_call_target="tpu_custom_call" | custom-call | flops 2415919104 | bytes 10223616 | tf_op jit(solution)/shard_map/pallas_call | solution.py:60
  140.2 1.5 collective-permute-start.18
  141.7 1.4 collective-permute-start.19
  143.7 4.9 %shard_map.207 = (f32[256,1536]{1,0:T(8,128)S(1)}, bf16[256,1536]{1,0:T(8,128)(2,1)}, bf16[256,1536]{1,0:T(8,128)(2,1)}, bf16[256,1536]{1,0:T(8,128)(2,1)}) custom-call(bf16[1024,768]{1,0:T(8,128)(2,1)S(1)} %get-tuple-element.75.gated_ref.refs_5_, bf16[768,1536]{1,0:T(8,128)(2,1)S(1)} %copy-done.38), custom_call_target="tpu_custom_call" | custom-call | flops 2415919104 | bytes 7077888 | tf_op jit(solution)/shard_map/pallas_call | solution.py:60
  148.6 1.5 collective-permute-start.12
  150.1 1.4 collective-permute-start.13
  152.2 3.6 shard_map.209
  155.9 7.0 %shard_map.210 = (bf16[1024,256]{1,0:T(8,128)(2,1)S(1)}, f32[8,256]{1,0:T(8,128)S(1)}, f32[1024,256]{1,0:T(8,128)S(1)}, f32[1024,128]{1,0:T(8,128)S(1)}, f32[1024,128]{1,0:T(8,128)S(1)}) custom-call(f32[1024,768]{1,0:T(8,128)S(1)} %get-tuple-element.86.refs_0_, f32[1024,1920]{1,0:T(8,128)S(1)} %get-tuple-element.74.z_ref.v_ref.shared_ref.refs_4_.refs_1_.refs_13_, ...), custom_call_target="tpu_custom_call" | custom-call | flops 4294967296 | bytes 6291456 | tf_op jit(solution)/shard_map/pallas_call | solution.py:60
  163.1 7.2 %shard_map.211 = (bf16[1024,256]{1,0:T(8,128)(2,1)S(1)}, f32[8,256]{1,0:T(8,128)S(1)}, f32[1024,256]{1,0:T(8,128)S(1)}, f32[1024,128]{1,0:T(8,128)S(1)}, f32[1024,128]{1,0:T(8,128)S(1)}) custom-call(f32[1024,768]{1,0:T(8,128)S(1)} %get-tuple-element.86.refs_0_, f32[1024,1920]{1,0:T(8,128)S(1)} %get-tuple-element.74.z_ref.v_ref.shared_ref.refs_4_.refs_1_.refs_13_, ...), custom_call_target="tpu_custom_call" | custom-call | flops 4294967296 | bytes 6291456 | tf_op jit(solution)/shard_map/pallas_call | solution.py:60
  176.5 12.9 %shard_map.212 = (bf16[1024,256]{1,0:T(8,128)(2,1)S(1)}, f32[8,256]{1,0:T(8,128)S(1)}, bf16[1024,384]{1,0:T(8,128)(2,1)S(1)}, f32[8,384]{1,0:T(8,128)S(1)}) custom-call(f32[1024,768]{1,0:T(8,128)} %copy-done.3, f32[1024,1920]{1,0:T(8,128)} %copy-done, f32[1024,768]{1,0:T(8,128)} %copy-done.2, f32[1024,768]{1,0:T(8,128)} %copy-done.1, f32[1024,384]{1,0:T(8,128)} %copy-done.4, ...), custom_call_target="tpu_custom_call" | custom-call | flops 4294967296 | bytes 6291456 | tf_op jit(solution)/shard_map/pallas_call | solution.py:60
  189.4 3.1 copy-done.65
  192.5 9.6 %shard_map.213 = (f32[256,1536]{1,0:T(8,128)S(1)}, bf16[256,1536]{1,0:T(8,128)(2,1)}, bf16[256,1536]{1,0:T(8,128)(2,1)}, bf16[256,1536]{1,0:T(8,128)(2,1)S(1)}) custom-call(bf16[1024,768]{1,0:T(8,128)(2,1)S(1)} %copy-done.42, bf16[1024,256]{1,0:T(8,128)(2,1)S(1)} %copy-done.55, bf16[1024,256]{1,0:T(8,128)(2,1)S(1)} %copy-done.58, ...), custom_call_target="tpu_custom_call" | custom-call | flops 6039797760 | bytes 12976128 | tf_op jit(solution)/shard_map/pallas_call | solution.py:60
  203.0 1.5 collective-permute-start.21
  204.5 1.4 collective-permute-start.22
  211.0 1.9 copy-done.63
  212.9 5.3 %shard_map.215 = (bf16[320,1536]{1,0:T(8,128)(2,1)}, bf16[320,1536]{1,0:T(8,128)(2,1)S(1)}) custom-call(s32[3]{0:T(128)S(1)} %pad_add_fusion.refs_0_.refs_5_.place_ref.refs_20_.refs_12_, bf16[1024,256]{1,0:T(8,128)(2,1)S(1)} %copy-done.61, bf16[1024,384]{1,0:T(8,128)(2,1)S(1)} %copy-done.53, bf16[1024,1536]{1,0:T(8,128)(2,1)S(1)} %copy-done.63), custom_call_target="tpu_custom_call" | custom-call | flops 2013265920 | bytes 6422528 | tf_op jit(solution)/shard_map/pallas_call | solution.py:60
  220.0 4.8 %shard_map.217 = (bf16[256,1536]{1,0:T(8,128)(2,1)}, bf16[256,1536]{1,0:T(8,128)(2,1)S(1)}) custom-call(s32[3]{0:T(128)S(1)} %pad_add_fusion.refs_0_.refs_5_.place_ref.refs_20_.refs_12_, bf16[1024,256]{1,0:T(8,128)(2,1)S(1)} %copy-done.56, bf16[1024,256]{1,0:T(8,128)(2,1)S(1)} %copy-done.59, bf16[1024,1536]{1,0:T(8,128)(2,1)S(1)} %copy-done.63), custom_call_target="tpu_custom_call" | custom-call | flops 1610612736 | bytes 5767168 | tf_op jit(solution)/shard_map/pallas_call | solution.py:60
  224.9 5.8 %shard_map.216 = (bf16[384,1536]{1,0:T(8,128)(2,1)}, bf16[384,1536]{1,0:T(8,128)(2,1)S(1)}) custom-call(s32[3]{0:T(128)S(1)} %pad_add_fusion.refs_0_.refs_5_.place_ref.refs_20_.refs_12_, bf16[1024,768]{1,0:T(8,128)(2,1)S(1)} %copy-done.43, bf16[1024,1536]{1,0:T(8,128)(2,1)S(1)} %copy-done.63), custom_call_target="tpu_custom_call" | custom-call | flops 2415919104 | bytes 7077888 | tf_op jit(solution)/shard_map/pallas_call | solution.py:60
  232.2 7.0 %shard_map.220 = (bf16[384,1536]{1,0:T(8,128)(2,1)}, bf16[384,1536]{1,0:T(8,128)(2,1)S(1)}) custom-call(s32[3]{0:T(128)S(1)} %pad_add_fusion.refs_0_.refs_5_.place_ref.refs_20_.refs_12_, bf16[1024,768]{1,0:T(8,128)(2,1)S(1)} %copy-done.40, bf16[256,1536]{1,0:T(8,128)(2,1)} %refs_2_.1, bf16[256,1536]{1,0:T(8,128)(2,1)S(1)} %copy-done.45, ...), custom_call_target="tpu_custom_call" | custom-call | flops 2415919104 | bytes 7077888 | tf_op jit(solution)/shard_map/pallas_call | solution.py:60
  241.2 5.1 %shard_map.214 = (bf16[256,1536]{1,0:T(8,128)(2,1)}, bf16[256,1536]{1,0:T(8,128)(2,1)}, f32[8,1536]{1,0:T(8,128)S(1)}) custom-call(f32[256,1536]{1,0:T(8,128)S(1)} %copy-done.18, bf16[256,1536]{1,0:T(8,128)(2,1)} %collective-permute-done.12.refs_1_, bf16[256,1536]{1,0:T(8,128)(2,1)} %collective-permute-done.13.refs_2_, ...), custom_call_target="tpu_custom_call" | custom-call | flops 11796480 | bytes 9437184 | tf_op jit(solution)/shard_map/pallas_call | solution.py:60
  247.2 1.4 add_convert_fusion.9
  249.4 2.3 collective-permute-start.50
  253.1 1.4 add_convert_fusion.6
  254.6 1.6 collective-permute-start.32
  256.2 1.6 add_convert_fusion.2
  257.8 3.4 collective-permute-start.56
  261.2 1.5 add_convert_fusion.5
  262.8 1.9 collective-permute-start.42
  268.2 5.8 %collective-permute-done.42 = bf16[384,384]{1,0:T(8,128)(2,1)S(1)} collective-permute-done((bf16[384,384]{1,0:T(8,128)(2,1)S(1)}, bf16[384,384]{1,0:T(8,128)(2,1)S(1)}, u32[]{:S(2)}, u32[]{:S(2)}) %collective-permute-start.42) | collective-permute-done | bytes 294944 | tf_op jit(solution)/shard_map/ppermute | solution.py:735
  274.0 2.3 collective-permute-start.34
  276.3 4.1 collective-permute-done.41
  280.4 1.8 collective-permute-start.51
  282.4 1.4 collective-permute-start.43
  283.7 5.4 %collective-permute-done.33 = bf16[320,384]{1,0:T(8,128)(2,1)S(1)} collective-permute-done((bf16[320,384]{1,0:T(8,128)(2,1)S(1)}, bf16[320,384]{1,0:T(8,128)(2,1)S(1)}, u32[]{:S(2)}, u32[]{:S(2)}) %collective-permute-start.33) | collective-permute-done | bytes 245792 | tf_op jit(solution)/shard_map/ppermute | solution.py:735
  290.3 5.7 %collective-permute-start.35 = (bf16[704,384]{1,0:T(8,128)(2,1)S(1)}, bf16[704,384]{1,0:T(8,128)(2,1)S(1)}, u32[]{:S(2)}, u32[]{:S(2)}) collective-permute-start(bf16[704,384]{1,0:T(8,128)(2,1)S(1)} %fusion), channel_id=1, source_target_pairs={{0,8},{4,12},{24,16},{28,20},{1,9},{5,13},{25,17},{29,21},{2,10},{... | collective-permute-start | bytes 1622024 | tf_op jit(solution)/shard_map/ppermute | solution.py:755
  296.1 33.2 %collective-permute-done.43 = bf16[1536,384]{1,0:T(8,128)(2,1)S(1)} collective-permute-done((bf16[1536,384]{1,0:T(8,128)(2,1)S(1)}, bf16[1536,384]{1,0:T(8,128)(2,1)S(1)}, u32[]{:S(2)}, u32[]{:S(2)}) %collective-permute-start.43) | collective-permute-done | bytes 1179680 | tf_op jit(solution)/shard_map/ppermute | solution.py:755
  330.4 1.4 collective-permute-start.25
  333.2 5.7 %collective-permute-done.35 = bf16[704,384]{1,0:T(8,128)(2,1)S(1)} collective-permute-done((bf16[704,384]{1,0:T(8,128)(2,1)S(1)}, bf16[704,384]{1,0:T(8,128)(2,1)S(1)}, u32[]{:S(2)}, u32[]{:S(2)}) %collective-permute-start.35) | collective-permute-done | bytes 540704 | tf_op jit(solution)/shard_map/ppermute | solution.py:755
  345.3 20.8 %collective-permute-start.28 = (f32[168,128]{1,0:T(8,128)S(1)}, f32[168,128]{1,0:T(8,128)S(1)}, u32[]{:S(2)}, u32[]{:S(2)}) collective-permute-start(f32[168,128]{1,0:T(8,128)S(1)} %add_add_fusion.1), channel_id=1, source_target_pairs={{0,8},{4,12},{8,0},{12,4},{16,24},{20,28},{24,16},{28,20},{1,9},{5... | collective-permute-start | bytes 258056 | tf_op jit(solution)/shard_map/ppermute | solution.py:735
  367.7 23.2 %collective-permute-done.58 = bf16[384,1536]{1,0:T(8,128)(2,1)S(1)} collective-permute-done((bf16[384,1536]{1,0:T(8,128)(2,1)S(1)}, bf16[384,1536]{1,0:T(8,128)(2,1)S(1)}, u32[]{:S(2)}, u32[]{:S(2)}) %collective-permute-start.58) | collective-permute-done | bytes 1179680 | tf_op jit(solution)/shard_map/ppermute | solution.py:759
  392.4 23.8 %collective-permute-done.45 = bf16[1536,384]{1,0:T(8,128)(2,1)S(1)} collective-permute-done((bf16[1536,384]{1,0:T(8,128)(2,1)S(1)}, bf16[1536,384]{1,0:T(8,128)(2,1)S(1)}, u32[]{:S(2)}, u32[]{:S(2)}) %collective-permute-start.45) | collective-permute-done | bytes 1179680 | tf_op jit(solution)/shard_map/ppermute | solution.py:759
  416.3 22.2 %collective-permute-done.53 = bf16[1024,384]{1,0:T(8,128)(2,1)S(1)} collective-permute-done((bf16[1024,384]{1,0:T(8,128)(2,1)S(1)}, bf16[1024,384]{1,0:T(8,128)(2,1)S(1)}, u32[]{:S(2)}, u32[]{:S(2)}) %collective-permute-start.53) | collective-permute-done | bytes 786464 | tf_op jit(solution)/shard_map/ppermute | solution.py:759
  442.0 6.6 %collective-permute-done.30 = f32[168,128]{1,0:T(8,128)S(1)} collective-permute-done((f32[168,128]{1,0:T(8,128)S(1)}, f32[168,128]{1,0:T(8,128)S(1)}, u32[]{:S(2)}, u32[]{:S(2)}) %collective-permute-start.30) | collective-permute-done | bytes 86048 | tf_op jit(solution)/shard_map/ppermute | solution.py:735
  451.9 3.7 shard_map.221
  455.7 5.1 %shard_map.218.refs_3_ = f32[6448,384]{1,0:T(8,128)} custom-call(s32[3]{0:T(128)S(1)} %pad_add_fusion.refs_0_.refs_5_.place_ref.refs_20_.refs_12_, bf16[1536,384]{1,0:T(8,128)(2,1)S(1)} %broadcast_select_fusion.1.refs_1_, bf16[1536,384]{1,0:T(8,128)(2,1)} %collective-permute-done.46.refs_2_, bf16[1024,384]{1,0:T(8,128)(2,1)S(1)} %broadcast_select_fusion.2.refs_3_, ...), custom_call_target="tpu_custom_call" | custom-call | flops 1966080 | bytes 11796480 | tf_op jit(solution)/shard_map/pallas_call | solution.py:60
  460.8 3.4 shard_map.219
  (359 shorter events, 60.5 us)
Async XLA Ops:
  8.0 46.8 %copy-start.73 = (bf16[768]{0:T(1024)(128)(2,1)S(1)}, bf16[768]{0:T(1024)(128)(2,1)}, u32[]{:S(2)}) copy-start(bf16[768]{0:T(1024)(128)(2,1)} %param.22) | copy-start | bytes 4612
  8.1 47.6 %copy-start.15 = (bf16[256,1536]{1,0:T(8,128)(2,1)S(1)}, bf16[256,1536]{1,0:T(8,128)(2,1)}, u32[]{:S(2)}) copy-start(bf16[256,1536]{1,0:T(8,128)(2,1)} %refs_14_.1) | copy-start | bytes 2359300
  8.1 12.5 %collective-permute-start.6 = (bf16[480,384]{1,0:T(8,128)(2,1)S(1)}, bf16[480,384]{1,0:T(8,128)(2,1)S(1)}, u32[]{:S(2)}, u32[]{:S(2)}) collective-permute-start(bf16[480,384]{1,0:T(8,128)(2,1)S(1)} %get-tuple-element.71), channel_id=1, source_target_pairs={{0,1},{1,0},{2,3},{3,2},{4,5},{5,4},{6,7},{7,6},{8,9},{9,8},{10,11... | collective-permute-start | bytes 1105928 | tf_op jit(solution)/shard_map/ppermute | solution.py:735
  11.1 17.9 %collective-permute-start.7 = (bf16[480,384]{1,0:T(8,128)(2,1)S(1)}, bf16[480,384]{1,0:T(8,128)(2,1)S(1)}, u32[]{:S(2)}, u32[]{:S(2)}) collective-permute-start(bf16[480,384]{1,0:T(8,128)(2,1)S(1)} %get-tuple-element.72), channel_id=1, source_target_pairs={{0,2},{1,3},{2,0},{3,1},{4,6},{5,7},{6,4},{7,5},{8,10},{9,11},{10,... | collective-permute-start | bytes 1105928 | tf_op jit(solution)/shard_map/ppermute | solution.py:735
  12.6 16.5 %collective-permute-start.8 = (bf16[480,384]{1,0:T(8,128)(2,1)S(1)}, bf16[480,384]{1,0:T(8,128)(2,1)S(1)}, u32[]{:S(2)}, u32[]{:S(2)}) collective-permute-start(bf16[480,384]{1,0:T(8,128)(2,1)S(1)} %get-tuple-element.73), channel_id=1, source_target_pairs={{0,3},{1,2},{2,1},{3,0},{4,7},{5,6},{6,5},{7,4},{8,11},{9,10},{10,... | collective-permute-start | bytes 1105928 | tf_op jit(solution)/shard_map/ppermute | solution.py:735
  29.2 25.1 %collective-permute-start.10 = (bf16[1440,384]{1,0:T(8,128)(2,1)S(1)}, bf16[1440,384]{1,0:T(8,128)(2,1)S(1)}, u32[]{:S(2)}, u32[]{:S(2)}) collective-permute-start(bf16[1440,384]{1,0:T(8,128)(2,1)S(1)} %constant_dynamic-update-slice_fusion.refs_7_), channel_id=1, source_target_pairs={{0,8},{4,12},{8,0},{12,4},{16,24},{20,28},{24,16},{28,20},{1,9},{5... | collective-permute-start | bytes 3317768 | tf_op jit(solution)/shard_map/ppermute | solution.py:735
  30.6 25.1 %collective-permute-start.5 = (f32[8,896]{1,0:T(8,128)S(1)}, f32[8,896]{1,0:T(8,128)S(1)}, u32[]{:S(2)}, u32[]{:S(2)}) collective-permute-start(f32[8,896]{1,0:T(8,128)S(1)} %get-tuple-element.70.source_ref), channel_id=1, source_target_pairs={{0,3},{1,2},{2,1},{3,0},{4,7},{5,6},{6,5},{7,4},{8,11},{9,10},{10,... | collective-permute-start | bytes 86024 | tf_op jit(solution)/shard_map/ppermute | solution.py:735
  32.1 25.0 %collective-permute-start.4 = (f32[8,896]{1,0:T(8,128)S(1)}, f32[8,896]{1,0:T(8,128)S(1)}, u32[]{:S(2)}, u32[]{:S(2)}) collective-permute-start(f32[8,896]{1,0:T(8,128)S(1)} %get-tuple-element.70.source_ref), channel_id=1, source_target_pairs={{0,2},{1,3},{2,0},{3,1},{4,6},{5,7},{6,4},{7,5},{8,10},{9,11},{10,... | collective-permute-start | bytes 86024 | tf_op jit(solution)/shard_map/ppermute | solution.py:735
  33.2 24.5 %collective-permute-start.3 = (f32[8,896]{1,0:T(8,128)S(1)}, f32[8,896]{1,0:T(8,128)S(1)}, u32[]{:S(2)}, u32[]{:S(2)}) collective-permute-start(f32[8,896]{1,0:T(8,128)S(1)} %get-tuple-element.70.source_ref), channel_id=1, source_target_pairs={{0,1},{1,0},{2,3},{3,2},{4,5},{5,4},{6,7},{7,6},{8,9},{9,8},{10,11... | collective-permute-start | bytes 86024 | tf_op jit(solution)/shard_map/ppermute | solution.py:735
  34.5 61.7 %collective-permute-start.9 = (bf16[1440,384]{1,0:T(8,128)(2,1)S(1)}, bf16[1440,384]{1,0:T(8,128)(2,1)}, u32[]{:S(2)}, u32[]{:S(2)}) collective-permute-start(bf16[1440,384]{1,0:T(8,128)(2,1)S(1)} %constant_dynamic-update-slice_fusion.refs_7_), channel_id=1, source_target_pairs={{0,4},{4,0},{8,12},{12,8},{16,20},{20,16},{24,28},{28,24},{1,5},{5... | collective-permute-start | bytes 3317768 | tf_op jit(solution)/shard_map/ppermute | solution.py:735
  54.2 41.9 %collective-permute-start.11 = (bf16[1440,384]{1,0:T(8,128)(2,1)S(1)}, bf16[1440,384]{1,0:T(8,128)(2,1)}, u32[]{:S(2)}, u32[]{:S(2)}) collective-permute-start(bf16[1440,384]{1,0:T(8,128)(2,1)S(1)} %collective-permute-done.10.refs_9_), channel_id=1, source_target_pairs={{0,4},{4,0},{8,12},{12,8},{16,20},{20,16},{24,28},{28,24},{1,5},{5... | collective-permute-start | bytes 3317768 | tf_op jit(solution)/shard_map/ppermute | solution.py:735
  55.7 38.4 %collective-permute-start = (bf16[256,1536]{1,0:T(8,128)(2,1)S(1)}, bf16[256,1536]{1,0:T(8,128)(2,1)}, u32[]{:S(2)}, u32[]{:S(2)}) collective-permute-start(bf16[256,1536]{1,0:T(8,128)(2,1)S(1)} %copy-done.15), channel_id=1, source_target_pairs={{0,1},{1,0},{2,3},{3,2},{4,5},{5,4},{6,7},{7,6},{8,9},{9,8},{10,11... | collective-permute-start | bytes 2359304 | tf_op jit(solution)/shard_map/ppermute | solution.py:735
  57.1 38.4 %collective-permute-start.1 = (bf16[256,1536]{1,0:T(8,128)(2,1)S(1)}, bf16[256,1536]{1,0:T(8,128)(2,1)}, u32[]{:S(2)}, u32[]{:S(2)}) collective-permute-start(bf16[256,1536]{1,0:T(8,128)(2,1)S(1)} %copy-done.15), channel_id=1, source_target_pairs={{0,2},{1,3},{2,0},{3,1},{4,6},{5,7},{6,4},{7,5},{8,10},{9,11},{10,... | collective-permute-start | bytes 2359304 | tf_op jit(solution)/shard_map/ppermute | solution.py:735
  57.7 35.0 %collective-permute-start.2 = (bf16[256,1536]{1,0:T(8,128)(2,1)S(1)}, bf16[256,1536]{1,0:T(8,128)(2,1)}, u32[]{:S(2)}, u32[]{:S(2)}) collective-permute-start(bf16[256,1536]{1,0:T(8,128)(2,1)S(1)} %copy-done.15), channel_id=1, source_target_pairs={{0,3},{1,2},{2,1},{3,0},{4,7},{5,6},{6,5},{7,4},{8,11},{9,10},{10,... | collective-permute-start | bytes 2359304 | tf_op jit(solution)/shard_map/ppermute | solution.py:735
  92.7 39.0 %collective-permute-start.15 = (bf16[256,1536]{1,0:T(8,128)(2,1)}, bf16[256,1536]{1,0:T(8,128)(2,1)S(1)}, u32[]{:S(2)}, u32[]{:S(2)}) collective-permute-start(bf16[256,1536]{1,0:T(8,128)(2,1)} %refs_2_.1), channel_id=1, source_target_pairs={{0,1},{1,0},{2,3},{3,2},{4,5},{5,4},{6,7},{7,6},{8,9},{9,8},{10,11... | collective-permute-start | bytes 2359304 | tf_op jit(solution)/shard_map/ppermute | solution.py:735
  94.1 37.6 %collective-permute-start.16 = (bf16[256,1536]{1,0:T(8,128)(2,1)}, bf16[256,1536]{1,0:T(8,128)(2,1)S(1)}, u32[]{:S(2)}, u32[]{:S(2)}) collective-permute-start(bf16[256,1536]{1,0:T(8,128)(2,1)} %refs_2_.1), channel_id=1, source_target_pairs={{0,2},{1,3},{2,0},{3,1},{4,6},{5,7},{6,4},{7,5},{8,10},{9,11},{10,... | collective-permute-start | bytes 2359304 | tf_op jit(solution)/shard_map/ppermute | solution.py:735
  95.5 36.2 %collective-permute-start.17 = (bf16[256,1536]{1,0:T(8,128)(2,1)}, bf16[256,1536]{1,0:T(8,128)(2,1)S(1)}, u32[]{:S(2)}, u32[]{:S(2)}) collective-permute-start(bf16[256,1536]{1,0:T(8,128)(2,1)} %refs_2_.1), channel_id=1, source_target_pairs={{0,3},{1,2},{2,1},{3,0},{4,7},{5,6},{6,5},{7,4},{8,11},{9,10},{10,... | collective-permute-start | bytes 2359304 | tf_op jit(solution)/shard_map/ppermute | solution.py:735
  113.5 49.5 %copy-start = (f32[1024,1920]{1,0:T(8,128)}, f32[1024,1920]{1,0:T(8,128)S(1)}, u32[]{:S(2)}) copy-start(f32[1024,1920]{1,0:T(8,128)S(1)} %get-tuple-element.74.z_ref.v_ref.shared_ref.refs_4_.refs_1_.refs_13_) | copy-start | bytes 23592964
  140.2 11.3 %collective-permute-start.18 = (f32[32,256]{1,0:T(8,128)S(1)}, f32[32,256]{1,0:T(8,128)S(1)}, u32[]{:S(2)}, u32[]{:S(2)}) collective-permute-start(f32[32,256]{1,0:T(8,128)S(1)} %get-tuple-element.82.refs_0_.refs_8_), channel_id=1, source_target_pairs={{0,1},{1,0},{2,3},{3,2},{4,5},{5,4},{6,7},{7,6},{8,9},{9,8},{10,11... | collective-permute-start | bytes 98312 | tf_op jit(solution)/shard_map/ppermute | solution.py:735
  141.7 10.5 %collective-permute-start.19 = (f32[32,256]{1,0:T(8,128)S(1)}, f32[32,256]{1,0:T(8,128)S(1)}, u32[]{:S(2)}, u32[]{:S(2)}) collective-permute-start(f32[32,256]{1,0:T(8,128)S(1)} %get-tuple-element.82.refs_0_.refs_8_), channel_id=1, source_target_pairs={{0,2},{1,3},{2,0},{3,1},{4,6},{5,7},{6,4},{7,5},{8,10},{9,11},{10,... | collective-permute-start | bytes 98312 | tf_op jit(solution)/shard_map/ppermute | solution.py:735
  143.0 9.1 %collective-permute-start.20 = (f32[32,256]{1,0:T(8,128)S(1)}, f32[32,256]{1,0:T(8,128)S(1)}, u32[]{:S(2)}, u32[]{:S(2)}) collective-permute-start(f32[32,256]{1,0:T(8,128)S(1)} %get-tuple-element.82.refs_0_.refs_8_), channel_id=1, source_target_pairs={{0,3},{1,2},{2,1},{3,0},{4,7},{5,6},{6,5},{7,4},{8,11},{9,10},{10,... | collective-permute-start | bytes 98312 | tf_op jit(solution)/shard_map/ppermute | solution.py:735
  148.6 70.7 %collective-permute-start.12 = (bf16[256,1536]{1,0:T(8,128)(2,1)}, bf16[256,1536]{1,0:T(8,128)(2,1)}, u32[]{:S(2)}, u32[]{:S(2)}) collective-permute-start(bf16[256,1536]{1,0:T(8,128)(2,1)} %get-tuple-element.77), channel_id=1, source_target_pairs={{0,1},{1,0},{2,3},{3,2},{4,5},{5,4},{6,7},{7,6},{8,9},{9,8},{10,11... | collective-permute-start | bytes 2359304 | tf_op jit(solution)/shard_map/ppermute | solution.py:735
  150.1 80.6 %collective-permute-start.13 = (bf16[256,1536]{1,0:T(8,128)(2,1)}, bf16[256,1536]{1,0:T(8,128)(2,1)}, u32[]{:S(2)}, u32[]{:S(2)}) collective-permute-start(bf16[256,1536]{1,0:T(8,128)(2,1)} %get-tuple-element.78), channel_id=1, source_target_pairs={{0,2},{1,3},{2,0},{3,1},{4,6},{5,7},{6,4},{7,5},{8,10},{9,11},{10,... | collective-permute-start | bytes 2359304 | tf_op jit(solution)/shard_map/ppermute | solution.py:735
  151.5 88.7 %collective-permute-start.14 = (bf16[256,1536]{1,0:T(8,128)(2,1)}, bf16[256,1536]{1,0:T(8,128)(2,1)}, u32[]{:S(2)}, u32[]{:S(2)}) collective-permute-start(bf16[256,1536]{1,0:T(8,128)(2,1)} %get-tuple-element.79), channel_id=1, source_target_pairs={{0,3},{1,2},{2,1},{3,0},{4,7},{5,6},{6,5},{7,4},{8,11},{9,10},{10,... | collective-permute-start | bytes 2359304 | tf_op jit(solution)/shard_map/ppermute | solution.py:735
  203.0 37.6 %collective-permute-start.21 = (bf16[256,1536]{1,0:T(8,128)(2,1)}, bf16[256,1536]{1,0:T(8,128)(2,1)}, u32[]{:S(2)}, u32[]{:S(2)}) collective-permute-start(bf16[256,1536]{1,0:T(8,128)(2,1)} %get-tuple-element.108), channel_id=1, source_target_pairs={{0,1},{1,0},{2,3},{3,2},{4,5},{5,4},{6,7},{7,6},{8,9},{9,8},{10,11... | collective-permute-start | bytes 2359304 | tf_op jit(solution)/shard_map/ppermute | solution.py:735
  204.5 36.3 %collective-permute-start.22 = (bf16[256,1536]{1,0:T(8,128)(2,1)}, bf16[256,1536]{1,0:T(8,128)(2,1)}, u32[]{:S(2)}, u32[]{:S(2)}) collective-permute-start(bf16[256,1536]{1,0:T(8,128)(2,1)} %get-tuple-element.109), channel_id=1, source_target_pairs={{0,2},{1,3},{2,0},{3,1},{4,6},{5,7},{6,4},{7,5},{8,10},{9,11},{10,... | collective-permute-start | bytes 2359304 | tf_op jit(solution)/shard_map/ppermute | solution.py:735
  219.3 21.9 %collective-permute-start.23 = (bf16[256,1536]{1,0:T(8,128)(2,1)S(1)}, bf16[256,1536]{1,0:T(8,128)(2,1)S(1)}, u32[]{:S(2)}, u32[]{:S(2)}) collective-permute-start(bf16[256,1536]{1,0:T(8,128)(2,1)S(1)} %copy-done.51), channel_id=1, source_target_pairs={{0,3},{1,2},{2,1},{3,0},{4,7},{5,6},{6,5},{7,4},{8,11},{9,10},{10,... | collective-permute-start | bytes 2359304 | tf_op jit(solution)/shard_map/ppermute | solution.py:735
  230.7 16.4 %collective-permute-start.47 = (bf16[256,1536]{1,0:T(8,128)(2,1)}, bf16[256,1536]{1,0:T(8,128)(2,1)}, u32[]{:S(2)}, u32[]{:S(2)}) collective-permute-start(bf16[256,1536]{1,0:T(8,128)(2,1)} %get-tuple-element.125), channel_id=1, source_target_pairs={{0,4},{4,0},{8,12},{12,8},{16,20},{20,16},{24,28},{28,24},{1,5},{5... | collective-permute-start | bytes 2359304 | tf_op jit(solution)/shard_map/ppermute | solution.py:735
  240.2 12.3 %collective-permute-start.31 = (bf16[320,1536]{1,0:T(8,128)(2,1)}, bf16[320,1536]{1,0:T(8,128)(2,1)}, u32[]{:S(2)}, u32[]{:S(2)}) collective-permute-start(bf16[320,1536]{1,0:T(8,128)(2,1)} %get-tuple-element.121), channel_id=1, source_target_pairs={{0,4},{4,0},{8,12},{12,8},{16,20},{20,16},{24,28},{28,24},{1,5},{5... | collective-permute-start | bytes 2949128 | tf_op jit(solution)/shard_map/ppermute | solution.py:735
  240.7 17.1 %collective-permute-start.39 = (bf16[384,1536]{1,0:T(8,128)(2,1)}, bf16[384,1536]{1,0:T(8,128)(2,1)}, u32[]{:S(2)}, u32[]{:S(2)}) collective-permute-start(bf16[384,1536]{1,0:T(8,128)(2,1)} %get-tuple-element.123), channel_id=1, source_target_pairs={{0,4},{4,0},{8,12},{12,8},{16,20},{20,16},{24,28},{28,24},{1,5},{5... | collective-permute-start | bytes 3538952 | tf_op jit(solution)/shard_map/ppermute | solution.py:735
  240.7 13.9 %collective-permute-start.55 = (bf16[384,1536]{1,0:T(8,128)(2,1)}, bf16[384,1536]{1,0:T(8,128)(2,1)}, u32[]{:S(2)}, u32[]{:S(2)}) collective-permute-start(bf16[384,1536]{1,0:T(8,128)(2,1)} %get-tuple-element.128), channel_id=1, source_target_pairs={{0,4},{4,0},{8,12},{12,8},{16,20},{20,16},{24,28},{28,24},{1,5},{5... | collective-permute-start | bytes 3538952 | tf_op jit(solution)/shard_map/ppermute | solution.py:735
  249.4 13.4 %collective-permute-start.50 = (bf16[256,384]{1,0:T(8,128)(2,1)S(1)}, bf16[256,384]{1,0:T(8,128)(2,1)S(1)}, u32[]{:S(2)}, u32[]{:S(2)}) collective-permute-start(bf16[256,384]{1,0:T(8,128)(2,1)S(1)} %get-tuple-element.137), channel_id=1, source_target_pairs={{0,3},{1,2},{2,1},{3,0},{4,7},{5,6},{6,5},{7,4},{8,11},{9,10},{10,... | collective-permute-start | bytes 589832 | tf_op jit(solution)/shard_map/ppermute | solution.py:735
  251.7 13.1 %collective-permute-start.49 = (bf16[256,384]{1,0:T(8,128)(2,1)}, bf16[256,384]{1,0:T(8,128)(2,1)S(1)}, u32[]{:S(2)}, u32[]{:S(2)}) collective-permute-start(bf16[256,384]{1,0:T(8,128)(2,1)} %get-tuple-element.138), channel_id=1, source_target_pairs={{0,2},{1,3},{2,0},{3,1},{4,6},{5,7},{6,4},{7,5},{8,10},{9,11},{10,... | collective-permute-start | bytes 589832 | tf_op jit(solution)/shard_map/ppermute | solution.py:735
  252.5 77.9 %copy-start.68 = (f32[21392]{0:T(1024)}, f32[21392]{0:T(1024)S(1)}, u32[]{:S(2)}) copy-start(f32[21392]{0:T(1024)S(1)} %concatenate.44) | copy-start | bytes 256708
  252.5 13.0 %collective-permute-start.48 = (bf16[256,384]{1,0:T(8,128)(2,1)}, bf16[256,384]{1,0:T(8,128)(2,1)S(1)}, u32[]{:S(2)}, u32[]{:S(2)}) collective-permute-start(bf16[256,384]{1,0:T(8,128)(2,1)} %get-tuple-element.139), channel_id=1, source_target_pairs={{0,1},{1,0},{2,3},{3,2},{4,5},{5,4},{6,7},{7,6},{8,9},{9,8},{10,11... | collective-permute-start | bytes 589832 | tf_op jit(solution)/shard_map/ppermute | solution.py:735
  254.6 13.0 %collective-permute-start.32 = (bf16[320,384]{1,0:T(8,128)(2,1)S(1)}, bf16[320,384]{1,0:T(8,128)(2,1)S(1)}, u32[]{:S(2)}, u32[]{:S(2)}) collective-permute-start(bf16[320,384]{1,0:T(8,128)(2,1)S(1)} %get-tuple-element.135), channel_id=1, source_target_pairs={{0,1},{1,0},{2,3},{3,2},{4,5},{5,4},{6,7},{7,6},{8,9},{9,8},{10,11... | collective-permute-start | bytes 737288 | tf_op jit(solution)/shard_map/ppermute | solution.py:735
  257.8 31.4 %collective-permute-start.56 = (bf16[384,1536]{1,0:T(8,128)(2,1)S(1)}, bf16[384,1536]{1,0:T(8,128)(2,1)S(1)}, u32[]{:S(2)}, u32[]{:S(2)}) collective-permute-start(bf16[384,1536]{1,0:T(8,128)(2,1)S(1)} %add_convert_fusion.2), channel_id=1, source_target_pairs={{0,8},{4,12},{24,16},{28,20},{1,9},{5,13},{25,17},{29,21},{2,10},{... | collective-permute-start | bytes 3538952 | tf_op jit(solution)/shard_map/ppermute | solution.py:755
  262.8 11.2 %collective-permute-start.42 = (bf16[384,384]{1,0:T(8,128)(2,1)S(1)}, bf16[384,384]{1,0:T(8,128)(2,1)S(1)}, u32[]{:S(2)}, u32[]{:S(2)}) collective-permute-start(bf16[384,384]{1,0:T(8,128)(2,1)S(1)} %get-tuple-element.130), channel_id=1, source_target_pairs={{0,3},{1,2},{2,1},{3,0},{4,7},{5,6},{6,5},{7,4},{8,11},{9,10},{10,... | collective-permute-start | bytes 884744 | tf_op jit(solution)/shard_map/ppermute | solution.py:735
  264.8 15.6 %collective-permute-start.41 = (bf16[384,384]{1,0:T(8,128)(2,1)S(1)}, bf16[384,384]{1,0:T(8,128)(2,1)S(1)}, u32[]{:S(2)}, u32[]{:S(2)}) collective-permute-start(bf16[384,384]{1,0:T(8,128)(2,1)S(1)} %get-tuple-element.131), channel_id=1, source_target_pairs={{0,2},{1,3},{2,0},{3,1},{4,6},{5,7},{6,4},{7,5},{8,10},{9,11},{10,... | collective-permute-start | bytes 884744 | tf_op jit(solution)/shard_map/ppermute | solution.py:735
  265.5 16.7 %collective-permute-start.40 = (bf16[384,384]{1,0:T(8,128)(2,1)S(1)}, bf16[384,384]{1,0:T(8,128)(2,1)S(1)}, u32[]{:S(2)}, u32[]{:S(2)}) collective-permute-start(bf16[384,384]{1,0:T(8,128)(2,1)S(1)} %get-tuple-element.132), channel_id=1, source_target_pairs={{0,1},{1,0},{2,3},{3,2},{4,5},{5,4},{6,7},{7,6},{8,9},{9,8},{10,11... | collective-permute-start | bytes 884744 | tf_op jit(solution)/shard_map/ppermute | solution.py:735
  267.7 21.4 %collective-permute-start.33 = (bf16[320,384]{1,0:T(8,128)(2,1)S(1)}, bf16[320,384]{1,0:T(8,128)(2,1)S(1)}, u32[]{:S(2)}, u32[]{:S(2)}) collective-permute-start(bf16[320,384]{1,0:T(8,128)(2,1)S(1)} %get-tuple-element.134), channel_id=1, source_target_pairs={{0,2},{1,3},{2,0},{3,1},{4,6},{5,7},{6,4},{7,5},{8,10},{9,11},{10,... | collective-permute-start | bytes 737288 | tf_op jit(solution)/shard_map/ppermute | solution.py:735
  274.0 15.1 %collective-permute-start.34 = (bf16[320,384]{1,0:T(8,128)(2,1)S(1)}, bf16[320,384]{1,0:T(8,128)(2,1)S(1)}, u32[]{:S(2)}, u32[]{:S(2)}) collective-permute-start(bf16[320,384]{1,0:T(8,128)(2,1)S(1)} %get-tuple-element.133), channel_id=1, source_target_pairs={{0,3},{1,2},{2,1},{3,0},{4,7},{5,6},{6,5},{7,4},{8,11},{9,10},{10,... | collective-permute-start | bytes 737288 | tf_op jit(solution)/shard_map/ppermute | solution.py:735
  280.4 51.4 %collective-permute-start.51 = (bf16[1024,384]{1,0:T(8,128)(2,1)S(1)}, bf16[1024,384]{1,0:T(8,128)(2,1)S(1)}, u32[]{:S(2)}, u32[]{:S(2)}) collective-permute-start(bf16[1024,384]{1,0:T(8,128)(2,1)S(1)} %pad_maximum_fusion.1), channel_id=1, source_target_pairs={{0,8},{4,12},{24,16},{28,20},{1,9},{5,13},{25,17},{29,21},{2,10},{... | collective-permute-start | bytes 2359304 | tf_op jit(solution)/shard_map/ppermute | solution.py:755
  282.4 46.9 %collective-permute-start.43 = (bf16[1536,384]{1,0:T(8,128)(2,1)S(1)}, bf16[1536,384]{1,0:T(8,128)(2,1)S(1)}, u32[]{:S(2)}, u32[]{:S(2)}) collective-permute-start(bf16[1536,384]{1,0:T(8,128)(2,1)S(1)} %pad_maximum_fusion), channel_id=1, source_target_pairs={{0,8},{4,12},{24,16},{28,20},{1,9},{5,13},{25,17},{29,21},{2,10},{... | collective-permute-start | bytes 3538952 | tf_op jit(solution)/shard_map/ppermute | solution.py:755
  289.5 50.9 %collective-permute-start.57 = (bf16[384,1536]{1,0:T(8,128)(2,1)S(1)}, bf16[384,1536]{1,0:T(8,128)(2,1)S(1)}, u32[]{:S(2)}, u32[]{:S(2)}) collective-permute-start(bf16[384,1536]{1,0:T(8,128)(2,1)S(1)} %add_convert_fusion.1), channel_id=1, source_target_pairs={{8,16},{12,20},{16,8},{20,12},{9,17},{13,21},{17,9},{21,13},{10,18... | collective-permute-start | bytes 3538952 | tf_op jit(solution)/shard_map/ppermute | solution.py:757
  290.3 48.5 %collective-permute-start.35 = (bf16[704,384]{1,0:T(8,128)(2,1)S(1)}, bf16[704,384]{1,0:T(8,128)(2,1)S(1)}, u32[]{:S(2)}, u32[]{:S(2)}) collective-permute-start(bf16[704,384]{1,0:T(8,128)(2,1)S(1)} %fusion), channel_id=1, source_target_pairs={{0,8},{4,12},{24,16},{28,20},{1,9},{5,13},{25,17},{29,21},{2,10},{... | collective-permute-start | bytes 1622024 | tf_op jit(solution)/shard_map/ppermute | solution.py:755
  329.6 12.7 %collective-permute-start.44 = (bf16[1536,384]{1,0:T(8,128)(2,1)S(1)}, bf16[1536,384]{1,0:T(8,128)(2,1)S(1)}, u32[]{:S(2)}, u32[]{:S(2)}) collective-permute-start(bf16[1536,384]{1,0:T(8,128)(2,1)S(1)} %add_convert_fusion.4), channel_id=1, source_target_pairs={{8,16},{12,20},{16,8},{20,12},{9,17},{13,21},{17,9},{21,13},{10,18... | collective-permute-start | bytes 3538952 | tf_op jit(solution)/shard_map/ppermute | solution.py:757
  330.4 11.0 %collective-permute-start.25 = (f32[168,128]{1,0:T(8,128)S(1)}, f32[168,128]{1,0:T(8,128)S(1)}, u32[]{:S(2)}, u32[]{:S(2)}) collective-permute-start(f32[168,128]{1,0:T(8,128)S(1)} %pad_bitcast_fusion), channel_id=1, source_target_pairs={{0,2},{1,3},{2,0},{3,1},{4,6},{5,7},{6,4},{7,5},{8,10},{9,11},{10,... | collective-permute-start | bytes 258056 | tf_op jit(solution)/shard_map/ppermute | solution.py:735
  331.8 12.1 %collective-permute-start.26 = (f32[168,128]{1,0:T(8,128)S(1)}, f32[168,128]{1,0:T(8,128)S(1)}, u32[]{:S(2)}, u32[]{:S(2)}) collective-permute-start(f32[168,128]{1,0:T(8,128)S(1)} %pad_bitcast_fusion), channel_id=1, source_target_pairs={{0,3},{1,2},{2,1},{3,0},{4,7},{5,6},{6,5},{7,4},{8,11},{9,10},{10,... | collective-permute-start | bytes 258056 | tf_op jit(solution)/shard_map/ppermute | solution.py:735
  338.9 6.4 %collective-permute-start.24 = (f32[168,128]{1,0:T(8,128)S(1)}, f32[168,128]{1,0:T(8,128)S(1)}, u32[]{:S(2)}, u32[]{:S(2)}) collective-permute-start(f32[168,128]{1,0:T(8,128)S(1)} %pad_bitcast_fusion), channel_id=1, source_target_pairs={{0,1},{1,0},{2,3},{3,2},{4,5},{5,4},{6,7},{7,6},{8,9},{9,8},{10,11... | collective-permute-start | bytes 258056 | tf_op jit(solution)/shard_map/ppermute | solution.py:735
  340.4 25.6 %collective-permute-start.36 = (bf16[704,384]{1,0:T(8,128)(2,1)S(1)}, bf16[704,384]{1,0:T(8,128)(2,1)S(1)}, u32[]{:S(2)}, u32[]{:S(2)}) collective-permute-start(bf16[704,384]{1,0:T(8,128)(2,1)S(1)} %add_convert_fusion.11), channel_id=1, source_target_pairs={{8,16},{12,20},{16,8},{20,12},{9,17},{13,21},{17,9},{21,13},{10,18... | collective-permute-start | bytes 1622024 | tf_op jit(solution)/shard_map/ppermute | solution.py:757
  341.4 24.8 %collective-permute-start.52 = (bf16[1024,384]{1,0:T(8,128)(2,1)S(1)}, bf16[1024,384]{1,0:T(8,128)(2,1)S(1)}, u32[]{:S(2)}, u32[]{:S(2)}) collective-permute-start(bf16[1024,384]{1,0:T(8,128)(2,1)S(1)} %add_convert_fusion.8), channel_id=1, source_target_pairs={{8,16},{12,20},{16,8},{20,12},{9,17},{13,21},{17,9},{21,13},{10,18... | collective-permute-start | bytes 2359304 | tf_op jit(solution)/shard_map/ppermute | solution.py:757
  342.3 48.6 %collective-permute-start.58 = (bf16[384,1536]{1,0:T(8,128)(2,1)S(1)}, bf16[384,1536]{1,0:T(8,128)(2,1)S(1)}, u32[]{:S(2)}, u32[]{:S(2)}) collective-permute-start(bf16[384,1536]{1,0:T(8,128)(2,1)S(1)} %add_convert_fusion), channel_id=1, source_target_pairs={{8,0},{12,4},{16,24},{20,28},{9,1},{13,5},{17,25},{21,29},{10,2},{... | collective-permute-start | bytes 3538952 | tf_op jit(solution)/shard_map/ppermute | solution.py:759
  343.9 72.3 %collective-permute-start.45 = (bf16[1536,384]{1,0:T(8,128)(2,1)S(1)}, bf16[1536,384]{1,0:T(8,128)(2,1)S(1)}, u32[]{:S(2)}, u32[]{:S(2)}) collective-permute-start(bf16[1536,384]{1,0:T(8,128)(2,1)S(1)} %add_convert_fusion.3), channel_id=1, source_target_pairs={{8,0},{12,4},{16,24},{20,28},{9,1},{13,5},{17,25},{21,29},{10,2},{... | collective-permute-start | bytes 3538952 | tf_op jit(solution)/shard_map/ppermute | solution.py:759
  345.3 93.3 %collective-permute-start.28 = (f32[168,128]{1,0:T(8,128)S(1)}, f32[168,128]{1,0:T(8,128)S(1)}, u32[]{:S(2)}, u32[]{:S(2)}) collective-permute-start(f32[168,128]{1,0:T(8,128)S(1)} %add_add_fusion.1), channel_id=1, source_target_pairs={{0,8},{4,12},{8,0},{12,4},{16,24},{20,28},{24,16},{28,20},{1,9},{5... | collective-permute-start | bytes 258056 | tf_op jit(solution)/shard_map/ppermute | solution.py:735
  366.0 74.1 %collective-permute-start.29 = (f32[168,128]{1,0:T(8,128)S(1)}, f32[168,128]{1,0:T(8,128)S(1)}, u32[]{:S(2)}, u32[]{:S(2)}) collective-permute-start(f32[168,128]{1,0:T(8,128)S(1)} %add_add_fusion.1), channel_id=1, source_target_pairs={{0,12},{4,8},{8,4},{12,0},{16,28},{20,24},{24,20},{28,16},{1,13},{... | collective-permute-start | bytes 258056 | tf_op jit(solution)/shard_map/ppermute | solution.py:735
  366.2 73.0 %collective-permute-start.37 = (bf16[704,384]{1,0:T(8,128)(2,1)S(1)}, bf16[704,384]{1,0:T(8,128)(2,1)S(1)}, u32[]{:S(2)}, u32[]{:S(2)}) collective-permute-start(bf16[704,384]{1,0:T(8,128)(2,1)S(1)} %add_convert_fusion.10), channel_id=1, source_target_pairs={{8,0},{12,4},{16,24},{20,28},{9,1},{13,5},{17,25},{21,29},{10,2},{... | collective-permute-start | bytes 1622024 | tf_op jit(solution)/shard_map/ppermute | solution.py:759
  390.9 47.6 %collective-permute-start.53 = (bf16[1024,384]{1,0:T(8,128)(2,1)S(1)}, bf16[1024,384]{1,0:T(8,128)(2,1)S(1)}, u32[]{:S(2)}, u32[]{:S(2)}) collective-permute-start(bf16[1024,384]{1,0:T(8,128)(2,1)S(1)} %add_convert_fusion.7), channel_id=1, source_target_pairs={{8,0},{12,4},{16,24},{20,28},{9,1},{13,5},{17,25},{21,29},{10,2},{... | collective-permute-start | bytes 2359304 | tf_op jit(solution)/shard_map/ppermute | solution.py:759
  416.2 35.8 %collective-permute-start.59 = (bf16[384,1536]{1,0:T(8,128)(2,1)S(1)}, bf16[384,1536]{1,0:T(8,128)(2,1)}, u32[]{:S(2)}, u32[]{:S(2)}) collective-permute-start(bf16[384,1536]{1,0:T(8,128)(2,1)S(1)} %broadcast_select_fusion.refs_1_), channel_id=1, source_target_pairs={{0,4},{4,0},{8,12},{12,8},{16,20},{20,16},{24,28},{28,24},{1,5},{5... | collective-permute-start | bytes 3538952 | tf_op jit(solution)/shard_map/ppermute | solution.py:735
  438.5 17.2 %collective-permute-start.46 = (bf16[1536,384]{1,0:T(8,128)(2,1)S(1)}, bf16[1536,384]{1,0:T(8,128)(2,1)}, u32[]{:S(2)}, u32[]{:S(2)}) collective-permute-start(bf16[1536,384]{1,0:T(8,128)(2,1)S(1)} %broadcast_select_fusion.1.refs_1_), channel_id=1, source_target_pairs={{0,4},{4,0},{8,12},{12,8},{16,20},{20,16},{24,28},{28,24},{1,5},{5... | collective-permute-start | bytes 3538952 | tf_op jit(solution)/shard_map/ppermute | solution.py:735
  438.6 2.9 collective-permute-start.27
  439.2 16.5 %collective-permute-start.54 = (bf16[1024,384]{1,0:T(8,128)(2,1)S(1)}, bf16[1024,384]{1,0:T(8,128)(2,1)}, u32[]{:S(2)}, u32[]{:S(2)}) collective-permute-start(bf16[1024,384]{1,0:T(8,128)(2,1)S(1)} %broadcast_select_fusion.2.refs_3_), channel_id=1, source_target_pairs={{0,4},{4,0},{8,12},{12,8},{16,20},{20,16},{24,28},{28,24},{1,5},{5... | collective-permute-start | bytes 2359304 | tf_op jit(solution)/shard_map/ppermute | solution.py:735
  440.1 20.6 %collective-permute-start.38 = (bf16[704,384]{1,0:T(8,128)(2,1)}, bf16[704,384]{1,0:T(8,128)(2,1)}, u32[]{:S(2)}, u32[]{:S(2)}) collective-permute-start(bf16[704,384]{1,0:T(8,128)(2,1)} %broadcast_select_fusion.3.refs_1_), channel_id=1, source_target_pairs={{0,4},{4,0},{8,12},{12,8},{16,20},{20,16},{24,28},{28,24},{1,5},{5... | collective-permute-start | bytes 1622024 | tf_op jit(solution)/shard_map/ppermute | solution.py:735
  441.5 7.1 %collective-permute-start.30 = (f32[168,128]{1,0:T(8,128)S(1)}, f32[168,128]{1,0:T(8,128)S(1)}, u32[]{:S(2)}, u32[]{:S(2)}) collective-permute-start(f32[168,128]{1,0:T(8,128)S(1)} %add_add_fusion), channel_id=1, source_target_pairs={{0,16},{4,20},{8,24},{12,28},{16,0},{20,4},{24,8},{28,12},{1,17},{... | collective-permute-start | bytes 258056 | tf_op jit(solution)/shard_map/ppermute | solution.py:735
  (83 other events, 801.5 us)

commit v2 on v1

--- a/solution.py
+++ b/solution.py
@@ -11,6 +11,8 @@
 HEADS = 48
 HEADDIM = 64
 KERNEL = 4
+FS = "fsdp"
+REP = "rep"
 LANES = 128
 EPSILON = 1e-05
 BF = jnp.bfloat16
@@ -54,7 +56,7 @@
 
 
 def call(kernel, out_shape, flops, moved, mib=None, **kw):
-    grant = (mib or 4 * lax.axis_size("fsdp")) * 1024 * 1024
+    grant = (mib or 4 * lax.axis_size(FS)) * 1024 * 1024
 
     def run(*operands):
         return pl.pallas_call(
@@ -740,28 +742,28 @@
 
 
 def line_sum(value):
-    size = lax.axis_size("rep")
+    size = lax.axis_size(REP)
     bits = size.bit_length() - 1
     last = bits - 2 if bits >= 3 else bits
     for b in range(1, last):
-        value = rounded_sum(value, swap(value, "rep", 1 << b))
+        value = rounded_sum(value, swap(value, REP, 1 << b))
     if bits < 3:
         return value
     low = size // 4
-    where = lax.axis_index("rep") // low
+    where = lax.axis_index(REP) // low
     inward = [(low * a + i, low * b + i) for a, b in ((0, 1), (3, 2)) for i in range(low)]
     middle = [(low * a + i, low * b + i) for a, b in ((1, 2), (2, 1)) for i in range(low)]
     outward = [(low * a + i, low * b + i) for a, b in ((1, 0), (2, 3)) for i in range(low)]
-    got = lax.ppermute(value, "rep", inward)
+    got = lax.ppermute(value, REP, inward)
     value = rounded_sum(value, got)
-    got = lax.ppermute(value, "rep", middle)
+    got = lax.ppermute(value, REP, middle)
     value = rounded_sum(value, got)
-    back = lax.ppermute(value, "rep", outward)
+    back = lax.ppermute(value, REP, outward)
     return jnp.where((where == 0) | (where == 3), back, value)
 
 
 def all_sum(value):
-    for axis in ("fsdp", "rep"):
+    for axis in (FS, REP):
         size = lax.axis_size(axis)
         step = 1
         while step < size:
@@ -778,12 +780,12 @@
 def to_owners(total, groups):
     rows = total.shape[1] // groups
     blocks = [total[:, k * rows : (k + 1) * rows] for k in range(groups)]
-    return [blocks[0]] + [swap(blocks[k], "fsdp", k) for k in range(1, groups)]
+    return [blocks[0]] + [swap(blocks[k], FS, k) for k in range(1, groups)]
 
 
 def core_sum(halves_):
     given, kept = halves_
-    got = swap(given, "rep", 1)
+    got = swap(given, REP, 1)
     return rounded_sum(kept, got)
 
 
@@ -801,9 +803,9 @@
     gate_gain,
     out_weight,
 ):
-    groups = lax.axis_size("fsdp")
-    member = lax.axis_index("fsdp")
-    core = lax.axis_index("rep") % 2
+    groups = lax.axis_size(FS)
+    member = lax.axis_index(FS)
+    core = lax.axis_index(REP) % 2
     span, model = tokens.shape
     per = HEADS // groups
     inner = per * HEADDIM
@@ -814,7 +816,7 @@
     width = 2 * inner + padded
     pairs = per // 2
     whole = groups * span
-    quarter = lax.axis_index("rep") % 4
+    quarter = lax.axis_index(REP) % 4
     place = jnp.stack([member, core, quarter]).astype(jnp.int32)
 
     rows = in_weight.shape[0]
@@ -823,7 +825,7 @@
     smem = pl.BlockSpec(memory_space=pltpu.SMEM)
     weight_t = in_weight.T
 
-    xs = [tokens] + [swap(tokens, "fsdp", k) for k in range(1, groups)]
+    xs = [tokens] + [swap(tokens, FS, k) for k in range(1, groups)]
     small_width = -(-max(rows, cols, span) // LANES) * LANES
     packed = call(
         partial(pack_kernel, groups),
@@ -835,16 +837,16 @@
         out_specs=(VM,) * groups,
         scratch_shapes=[pltpu.SemaphoreType.DMA((3 * groups,))],
     )(place, weight_t, norm_gain.reshape(1, -1), conv_weight, conv_bias.reshape(1, -1), segment_ids)
-    near = [swap(packed[k - 1], "fsdp", k) for k in range(1, groups)]
+    near = [swap(packed[k - 1], FS, k) for k in range(1, groups)]
     own_small = call(
         copy_kernel, jax.ShapeDtypeStruct(packed[-1].shape, F32), 1, 1, in_specs=[VM], out_specs=VM
     )(packed[-1])
-    small = [own_small] + [swap(packed[-1], "fsdp", k) for k in range(1, groups)]
+    small = [own_small] + [swap(packed[-1], FS, k) for k in range(1, groups)]
     near = jnp.concatenate(near, axis=0)
-    across = swap(near, "rep", 2)
-    given = [near, swap(near, "rep", 1), across, swap(across, "rep", 1)]
+    across = swap(near, REP, 2)
+    given = [near, swap(near, REP, 1), across, swap(across, REP, 1)]
     late, _ = lax.optimization_barrier((cotangent, (near, xs[-1])))
-    cots = [cotangent] + [swap(late, "fsdp", k) for k in range(1, groups)]
+    cots = [cotangent] + [swap(late, FS, k) for k in range(1, groups)]
 
     gain_x = jnp.concatenate([t[0:1, :rows] for t in small], axis=1)
     order = jnp.arange(groups) ^ member
@@ -989,7 +991,7 @@
         out_specs=(VM, VM),
         scratch_shapes=[pltpu.VMEM((groups, span, model), BF), pltpu.SemaphoreType.DMA((groups,))],
     )(*cots, out_weight, gated, squares)
-    sums_all = [sums] + [swap(sums, "fsdp", k) for k in range(1, groups)]
+    sums_all = [sums] + [swap(sums, FS, k) for k in range(1, groups)]
 
     outs = call(
         partial(outproj_kernel, groups),
@@ -999,7 +1001,7 @@
         in_specs=[VM, VM],
         out_specs=(VM,) * groups,
     )(gated, out_weight)
-    outs = [outs[0]] + [swap(outs[k], "fsdp", k) for k in range(1, groups)]
+    outs = [outs[0]] + [swap(outs[k], FS, k) for k in range(1, groups)]
 
     row_spec = lambda cols_, col=0: pl.BlockSpec((span, cols_), lambda r: (r, col))
     gz, ds, mixed, gate_sum = call(
@@ -1087,7 +1089,7 @@
         in_specs=[VM] * 6,
         out_specs=(VM,) * groups,
     )(gz, gva, gvb, gv2, gs, weight)
-    backs = [backs[0]] + [swap(backs[k], "fsdp", k) for k in range(1, groups)]
+    backs = [backs[0]] + [swap(backs[k], FS, k) for k in range(1, groups)]
 
     v1_part = line_sum(jnp.concatenate(to_owners(v1_sum, groups), axis=0))
     deep = (pairs - split) * HEADDIM
@@ -1120,7 +1122,7 @@
     norm_sum = jnp.take(norm_sum[0].reshape(groups, rows), order, axis=0).reshape(1, model)
 
     def returned(part):
-        return [part, swap(part, "rep", 1)]
+        return [part, swap(part, REP, 1)]
 
     grad_outproj = place_rows(place, 1, out_weight.shape, ((((inner // 2, 0),), 0, None),), returned(out_part))
     early = returned(z_part) + returned(v1_part)
@@ -1183,33 +1185,33 @@
 
 
 def solution(mesh):
-    rows = P(("rep", "fsdp"), None)
+    rows = P((REP, FS), None)
     in_specs = (
         rows,
         rows,
         rows,
-        P("fsdp"),
-        P("fsdp", None),
-        P(None, "fsdp"),
-        P("fsdp"),
+        P(FS),
+        P(FS, None),
+        P(None, FS),
+        P(FS),
         P(),
         P(),
         P(),
-        P("fsdp"),
-        P("fsdp", None),
+        P(FS),
+        P(FS, None),
     )
     out_specs = (
         rows,
         rows,
-        P("fsdp"),
-        P("fsdp", None),
-        P(None, "fsdp"),
-        P("fsdp"),
+        P(FS),
+        P(FS, None),
+        P(None, FS),
+        P(FS),
         P(),
         P(),
         P(),
-        P("fsdp"),
-        P("fsdp", None),
+        P(FS),
+        P(FS, None),
     )
 
     return jax.shard_map(body, mesh=mesh, in_specs=in_specs, out_specs=out_specs, check_vma=False)

time: 466 us -> 466 us (level)
  no operation moved by 1% of the time
where the time goes in v2:
time: 466 us; the launch traced here: 464 us
  waiting for transfers between devices  199 us (43%)
  Pallas kernels  123 us (26%)
  starting transfers between devices  86.3 us (19%)
  local copies, waits for them, and re-layouts  42.4 us (9%)
  other arithmetic  11.4 us (2%)
    pallas_call x19, Pallas kernels, run(): pl.pallas_call(kernel, out_shape=out_shape, cost_estimate=pl.CostEstimate...  123 us
    ppermute x48, waiting for transfers between devices, swap(): return lax.ppermute(value, axis, [(i, i ^ step) for i in range(size)])  91.2 us
    ppermute x4, waiting for transfers between devices, line_sum(): back = lax.ppermute(value, REP, outward)  69.2 us
    ppermute x48, starting transfers between devices, swap(): return lax.ppermute(value, axis, [(i, i ^ step) for i in range(size)])  65.8 us
    ppermute x4, waiting for transfers between devices, line_sum(): got = lax.ppermute(value, REP, inward)  38.9 us
    unnamed x182, local copies, waits for them, and re-layouts  30.5 us
    ppermute x4, starting transfers between devices, line_sum(): got = lax.ppermute(value, REP, inward)  12.3 us
  transfers between devices with their start and end apart: 60, of which 15 were waited for; matrix products, arithmetic and copies ran while one was open for 5% of the time, Pallas kernels for 24%

profile of v2, /device:TPU:0, one launch (start us, length us, event | category | flops | bytes accessed | tf_op | source)
XLA Modules:
  0.0 464.3 jit_solution(5998603427849593093)
XLA Ops:
  2.1 2.4 copy-done.7
  5.9 2.1 shard_map.203
  8.1 3.0 collective-permute-start.6
  11.1 1.5 collective-permute-start.7
  12.6 7.9 %collective-permute-done.6 = bf16[480,384]{1,0:T(8,128)(2,1)S(1)} collective-permute-done((bf16[480,384]{1,0:T(8,128)(2,1)S(1)}, bf16[480,384]{1,0:T(8,128)(2,1)S(1)}, u32[]{:S(2)}, u32[]{:S(2)}) %collective-permute-start.6) | collective-permute-done | bytes 368672 | tf_op jit(solution)/shard_map/ppermute | solution.py:737
  20.6 8.5 %collective-permute-done.7 = bf16[480,384]{1,0:T(8,128)(2,1)S(1)} collective-permute-done((bf16[480,384]{1,0:T(8,128)(2,1)S(1)}, bf16[480,384]{1,0:T(8,128)(2,1)S(1)}, u32[]{:S(2)}, u32[]{:S(2)}) %collective-permute-start.7) | collective-permute-done | bytes 368672 | tf_op jit(solution)/shard_map/ppermute | solution.py:737
  29.2 1.4 collective-permute-start.10
  30.6 1.5 collective-permute-start.5
  34.5 19.8 %collective-permute-done.10.refs_9_ = bf16[1440,384]{1,0:T(8,128)(2,1)S(1)} collective-permute-done((bf16[1440,384]{1,0:T(8,128)(2,1)S(1)}, bf16[1440,384]{1,0:T(8,128)(2,1)S(1)}, u32[]{:S(2)}, u32[]{:S(2)}) %collective-permute-start.10) | collective-permute-done | bytes 1105952 | tf_op jit(solution)/shard_map/ppermute | solution.py:737
  55.7 1.4 collective-permute-start
  57.7 1.5 collective-permute-start.2
  61.6 31.1 %collective-permute-done.2.refs_3_ = bf16[256,1536]{1,0:T(8,128)(2,1)} collective-permute-done((bf16[256,1536]{1,0:T(8,128)(2,1)S(1)}, bf16[256,1536]{1,0:T(8,128)(2,1)}, u32[]{:S(2)}, u32[]{:S(2)}) %collective-permute-start.2) | collective-permute-done | bytes 786464 | tf_op jit(solution)/shard_map/ppermute | solution.py:737
  92.7 1.5 collective-permute-start.15
  94.1 1.4 collective-permute-start.16
  96.2 2.4 copy-done.8
  98.6 13.1 %shard_map.205 = (bf16[1024,1536]{1,0:T(8,128)(2,1)S(1)}, f32[1024,1920]{1,0:T(8,128)S(1)}, bf16[1920,1536]{1,0:T(8,128)(2,1)S(1)}) custom-call(bf16[256,1536]{1,0:T(8,128)(2,1)S(1)} %copy-done.15, bf16[256,1536]{1,0:T(8,128)(2,1)} %collective-permute-done.refs_1_, bf16[256,1536]{1,0:T(8,128)(2,1)} %collective-permute-done.1.refs_2_, ...), custom_call_target="tpu_custom_call" | custom-call | flops 6039797760 | bytes 25952256 | tf_op jit(solution)/shard_map/pallas_call | solution.py:62
  111.7 1.8 copy-done.62
  113.5 16.1 %shard_map.206 = (f32[1024,768]{1,0:T(8,128)S(1)}, f32[1024,768]{1,0:T(8,128)S(1)}, bf16[1024,768]{1,0:T(8,128)(2,1)S(1)}, f32[32,256]{1,0:T(8,128)S(1)}, f32[10...) custom-call(s32[3]{0:T(128)S(1)} %pad_add_fusion.refs_0_.refs_5_.pla, ...), custom_call_target="tpu_custom_call" | custom-call | flops 6442450944 | bytes 15728640 | tf_op jit(solution)/shard_map/pallas_call | solution.py:62
  131.8 5.7 %shard_map.208 = (f32[1024,768]{1,0:T(8,128)S(1)}, f32[32,256]{1,0:T(8,128)S(1)}) custom-call(bf16[256,1536]{1,0:T(8,128)(2,1)} %refs_2_.1, bf16[256,1536]{1,0:T(8,128)(2,1)S(1)} %collective-permute-done.15.refs_1_.refs_3_, bf16[256,1536]{1,0:T(8,128)(2,1)S(1)} %collective-permute-done.16.refs_2_.refs_4_, ...), custom_call_target="tpu_custom_call" | custom-call | flops 2415919104 | bytes 10223616 | tf_op jit(solution)/shard_map/pallas_call | solution.py:62
  140.2 1.5 collective-permute-start.18
  141.7 1.4 collective-permute-start.19
  143.7 4.9 %shard_map.207 = (f32[256,1536]{1,0:T(8,128)S(1)}, bf16[256,1536]{1,0:T(8,128)(2,1)}, bf16[256,1536]{1,0:T(8,128)(2,1)}, bf16[256,1536]{1,0:T(8,128)(2,1)}) custom-call(bf16[1024,768]{1,0:T(8,128)(2,1)S(1)} %get-tuple-element.75.gated_ref.refs_5_, bf16[768,1536]{1,0:T(8,128)(2,1)S(1)} %copy-done.38), custom_call_target="tpu_custom_call" | custom-call | flops 2415919104 | bytes 7077888 | tf_op jit(solution)/shard_map/pallas_call | solution.py:62
  148.6 1.5 collective-permute-start.12
  150.1 1.4 collective-permute-start.13
  152.2 3.6 shard_map.209
  155.9 7.0 %shard_map.210 = (bf16[1024,256]{1,0:T(8,128)(2,1)S(1)}, f32[8,256]{1,0:T(8,128)S(1)}, f32[1024,256]{1,0:T(8,128)S(1)}, f32[1024,128]{1,0:T(8,128)S(1)}, f32[1024,128]{1,0:T(8,128)S(1)}) custom-call(f32[1024,768]{1,0:T(8,128)S(1)} %get-tuple-element.86.refs_0_, f32[1024,1920]{1,0:T(8,128)S(1)} %get-tuple-element.74.z_ref.v_ref.shared_ref.refs_4_.refs_1_.refs_13_, ...), custom_call_target="tpu_custom_call" | custom-call | flops 4294967296 | bytes 6291456 | tf_op jit(solution)/shard_map/pallas_call | solution.py:62
  163.1 7.2 %shard_map.211 = (bf16[1024,256]{1,0:T(8,128)(2,1)S(1)}, f32[8,256]{1,0:T(8,128)S(1)}, f32[1024,256]{1,0:T(8,128)S(1)}, f32[1024,128]{1,0:T(8,128)S(1)}, f32[1024,128]{1,0:T(8,128)S(1)}) custom-call(f32[1024,768]{1,0:T(8,128)S(1)} %get-tuple-element.86.refs_0_, f32[1024,1920]{1,0:T(8,128)S(1)} %get-tuple-element.74.z_ref.v_ref.shared_ref.refs_4_.refs_1_.refs_13_, ...), custom_call_target="tpu_custom_call" | custom-call | flops 4294967296 | bytes 6291456 | tf_op jit(solution)/shard_map/pallas_call | solution.py:62
  176.5 12.9 %shard_map.212 = (bf16[1024,256]{1,0:T(8,128)(2,1)S(1)}, f32[8,256]{1,0:T(8,128)S(1)}, bf16[1024,384]{1,0:T(8,128)(2,1)S(1)}, f32[8,384]{1,0:T(8,128)S(1)}) custom-call(f32[1024,768]{1,0:T(8,128)} %copy-done.3, f32[1024,1920]{1,0:T(8,128)} %copy-done, f32[1024,768]{1,0:T(8,128)} %copy-done.2, f32[1024,768]{1,0:T(8,128)} %copy-done.1, f32[1024,384]{1,0:T(8,128)} %copy-done.4, ...), custom_call_target="tpu_custom_call" | custom-call | flops 4294967296 | bytes 6291456 | tf_op jit(solution)/shard_map/pallas_call | solution.py:62
  189.4 3.1 copy-done.65
  192.5 9.6 %shard_map.213 = (f32[256,1536]{1,0:T(8,128)S(1)}, bf16[256,1536]{1,0:T(8,128)(2,1)}, bf16[256,1536]{1,0:T(8,128)(2,1)}, bf16[256,1536]{1,0:T(8,128)(2,1)S(1)}) custom-call(bf16[1024,768]{1,0:T(8,128)(2,1)S(1)} %copy-done.42, bf16[1024,256]{1,0:T(8,128)(2,1)S(1)} %copy-done.55, bf16[1024,256]{1,0:T(8,128)(2,1)S(1)} %copy-done.58, ...), custom_call_target="tpu_custom_call" | custom-call | flops 6039797760 | bytes 12976128 | tf_op jit(solution)/shard_map/pallas_call | solution.py:62
  203.0 1.5 collective-permute-start.21
  204.5 1.4 collective-permute-start.22
  211.0 1.9 copy-done.63
  212.9 5.3 %shard_map.215 = (bf16[320,1536]{1,0:T(8,128)(2,1)}, bf16[320,1536]{1,0:T(8,128)(2,1)S(1)}) custom-call(s32[3]{0:T(128)S(1)} %pad_add_fusion.refs_0_.refs_5_.place_ref.refs_20_.refs_12_, bf16[1024,256]{1,0:T(8,128)(2,1)S(1)} %copy-done.61, bf16[1024,384]{1,0:T(8,128)(2,1)S(1)} %copy-done.53, bf16[1024,1536]{1,0:T(8,128)(2,1)S(1)} %copy-done.63), custom_call_target="tpu_custom_call" | custom-call | flops 2013265920 | bytes 6422528 | tf_op jit(solution)/shard_map/pallas_call | solution.py:62
  220.0 4.8 %shard_map.217 = (bf16[256,1536]{1,0:T(8,128)(2,1)}, bf16[256,1536]{1,0:T(8,128)(2,1)S(1)}) custom-call(s32[3]{0:T(128)S(1)} %pad_add_fusion.refs_0_.refs_5_.place_ref.refs_20_.refs_12_, bf16[1024,256]{1,0:T(8,128)(2,1)S(1)} %copy-done.56, bf16[1024,256]{1,0:T(8,128)(2,1)S(1)} %copy-done.59, bf16[1024,1536]{1,0:T(8,128)(2,1)S(1)} %copy-done.63), custom_call_target="tpu_custom_call" | custom-call | flops 1610612736 | bytes 5767168 | tf_op jit(solution)/shard_map/pallas_call | solution.py:62
  224.9 5.8 %shard_map.216 = (bf16[384,1536]{1,0:T(8,128)(2,1)}, bf16[384,1536]{1,0:T(8,128)(2,1)S(1)}) custom-call(s32[3]{0:T(128)S(1)} %pad_add_fusion.refs_0_.refs_5_.place_ref.refs_20_.refs_12_, bf16[1024,768]{1,0:T(8,128)(2,1)S(1)} %copy-done.43, bf16[1024,1536]{1,0:T(8,128)(2,1)S(1)} %copy-done.63), custom_call_target="tpu_custom_call" | custom-call | flops 2415919104 | bytes 7077888 | tf_op jit(solution)/shard_map/pallas_call | solution.py:62
  232.2 7.0 %shard_map.220 = (bf16[384,1536]{1,0:T(8,128)(2,1)}, bf16[384,1536]{1,0:T(8,128)(2,1)S(1)}) custom-call(s32[3]{0:T(128)S(1)} %pad_add_fusion.refs_0_.refs_5_.place_ref.refs_20_.refs_12_, bf16[1024,768]{1,0:T(8,128)(2,1)S(1)} %copy-done.40, bf16[256,1536]{1,0:T(8,128)(2,1)} %refs_2_.1, bf16[256,1536]{1,0:T(8,128)(2,1)S(1)} %copy-done.45, ...), custom_call_target="tpu_custom_call" | custom-call | flops 2415919104 | bytes 7077888 | tf_op jit(solution)/shard_map/pallas_call | solution.py:62
  241.2 5.1 %shard_map.214 = (bf16[256,1536]{1,0:T(8,128)(2,1)}, bf16[256,1536]{1,0:T(8,128)(2,1)}, f32[8,1536]{1,0:T(8,128)S(1)}) custom-call(f32[256,1536]{1,0:T(8,128)S(1)} %copy-done.18, bf16[256,1536]{1,0:T(8,128)(2,1)} %collective-permute-done.12.refs_1_, bf16[256,1536]{1,0:T(8,128)(2,1)} %collective-permute-done.13.refs_2_, ...), custom_call_target="tpu_custom_call" | custom-call | flops 11796480 | bytes 9437184 | tf_op jit(solution)/shard_map/pallas_call | solution.py:62
  247.2 1.4 add_convert_fusion.9
  249.4 2.3 collective-permute-start.50
  253.1 1.4 add_convert_fusion.6
  254.6 1.6 collective-permute-start.32
  256.2 1.6 add_convert_fusion.2
  257.8 3.4 collective-permute-start.56
  261.2 1.5 add_convert_fusion.5
  262.8 1.9 collective-permute-start.42
  268.2 5.8 %collective-permute-done.42 = bf16[384,384]{1,0:T(8,128)(2,1)S(1)} collective-permute-done((bf16[384,384]{1,0:T(8,128)(2,1)S(1)}, bf16[384,384]{1,0:T(8,128)(2,1)S(1)}, u32[]{:S(2)}, u32[]{:S(2)}) %collective-permute-start.42) | collective-permute-done | bytes 294944 | tf_op jit(solution)/shard_map/ppermute | solution.py:737
  274.0 2.3 collective-permute-start.34
  276.3 4.1 collective-permute-done.41
  280.4 1.8 collective-permute-start.51
  282.4 1.4 collective-permute-start.43
  283.7 5.4 %collective-permute-done.33 = bf16[320,384]{1,0:T(8,128)(2,1)S(1)} collective-permute-done((bf16[320,384]{1,0:T(8,128)(2,1)S(1)}, bf16[320,384]{1,0:T(8,128)(2,1)S(1)}, u32[]{:S(2)}, u32[]{:S(2)}) %collective-permute-start.33) | collective-permute-done | bytes 245792 | tf_op jit(solution)/shard_map/ppermute | solution.py:737
  290.3 5.7 %collective-permute-start.35 = (bf16[704,384]{1,0:T(8,128)(2,1)S(1)}, bf16[704,384]{1,0:T(8,128)(2,1)S(1)}, u32[]{:S(2)}, u32[]{:S(2)}) collective-permute-start(bf16[704,384]{1,0:T(8,128)(2,1)S(1)} %fusion), channel_id=1, source_target_pairs={{0,8},{4,12},{24,16},{28,20},{1,9},{5,13},{25,17},{29,21},{2,10},{... | collective-permute-start | bytes 1622024 | tf_op jit(solution)/shard_map/ppermute | solution.py:757
  296.1 33.2 %collective-permute-done.43 = bf16[1536,384]{1,0:T(8,128)(2,1)S(1)} collective-permute-done((bf16[1536,384]{1,0:T(8,128)(2,1)S(1)}, bf16[1536,384]{1,0:T(8,128)(2,1)S(1)}, u32[]{:S(2)}, u32[]{:S(2)}) %collective-permute-start.43) | collective-permute-done | bytes 1179680 | tf_op jit(solution)/shard_map/ppermute | solution.py:757
  330.4 1.4 collective-permute-start.25
  333.2 5.7 %collective-permute-done.35 = bf16[704,384]{1,0:T(8,128)(2,1)S(1)} collective-permute-done((bf16[704,384]{1,0:T(8,128)(2,1)S(1)}, bf16[704,384]{1,0:T(8,128)(2,1)S(1)}, u32[]{:S(2)}, u32[]{:S(2)}) %collective-permute-start.35) | collective-permute-done | bytes 540704 | tf_op jit(solution)/shard_map/ppermute | solution.py:757
  345.3 20.8 %collective-permute-start.28 = (f32[168,128]{1,0:T(8,128)S(1)}, f32[168,128]{1,0:T(8,128)S(1)}, u32[]{:S(2)}, u32[]{:S(2)}) collective-permute-start(f32[168,128]{1,0:T(8,128)S(1)} %add_add_fusion.1), channel_id=1, source_target_pairs={{0,8},{4,12},{8,0},{12,4},{16,24},{20,28},{24,16},{28,20},{1,9},{5... | collective-permute-start | bytes 258056 | tf_op jit(solution)/shard_map/ppermute | solution.py:737
  367.7 23.2 %collective-permute-done.58 = bf16[384,1536]{1,0:T(8,128)(2,1)S(1)} collective-permute-done((bf16[384,1536]{1,0:T(8,128)(2,1)S(1)}, bf16[384,1536]{1,0:T(8,128)(2,1)S(1)}, u32[]{:S(2)}, u32[]{:S(2)}) %collective-permute-start.58) | collective-permute-done | bytes 1179680 | tf_op jit(solution)/shard_map/ppermute | solution.py:761
  392.4 23.8 %collective-permute-done.45 = bf16[1536,384]{1,0:T(8,128)(2,1)S(1)} collective-permute-done((bf16[1536,384]{1,0:T(8,128)(2,1)S(1)}, bf16[1536,384]{1,0:T(8,128)(2,1)S(1)}, u32[]{:S(2)}, u32[]{:S(2)}) %collective-permute-start.45) | collective-permute-done | bytes 1179680 | tf_op jit(solution)/shard_map/ppermute | solution.py:761
  416.3 22.2 %collective-permute-done.53 = bf16[1024,384]{1,0:T(8,128)(2,1)S(1)} collective-permute-done((bf16[1024,384]{1,0:T(8,128)(2,1)S(1)}, bf16[1024,384]{1,0:T(8,128)(2,1)S(1)}, u32[]{:S(2)}, u32[]{:S(2)}) %collective-permute-start.53) | collective-permute-done | bytes 786464 | tf_op jit(solution)/shard_map/ppermute | solution.py:761
  442.0 6.6 %collective-permute-done.30 = f32[168,128]{1,0:T(8,128)S(1)} collective-permute-done((f32[168,128]{1,0:T(8,128)S(1)}, f32[168,128]{1,0:T(8,128)S(1)}, u32[]{:S(2)}, u32[]{:S(2)}) %collective-permute-start.30) | collective-permute-done | bytes 86048 | tf_op jit(solution)/shard_map/ppermute | solution.py:737
  451.9 3.7 shard_map.221
  455.7 5.1 %shard_map.218.refs_3_ = f32[6448,384]{1,0:T(8,128)} custom-call(s32[3]{0:T(128)S(1)} %pad_add_fusion.refs_0_.refs_5_.place_ref.refs_20_.refs_12_, bf16[1536,384]{1,0:T(8,128)(2,1)S(1)} %broadcast_select_fusion.1.refs_1_, bf16[1536,384]{1,0:T(8,128)(2,1)} %collective-permute-done.46.refs_2_, bf16[1024,384]{1,0:T(8,128)(2,1)S(1)} %broadcast_select_fusion.2.refs_3_, ...), custom_call_target="tpu_custom_call" | custom-call | flops 1966080 | bytes 11796480 | tf_op jit(solution)/shard_map/pallas_call | solution.py:62
  460.8 3.4 shard_map.219
  (359 shorter events, 60.5 us)
Async XLA Ops:
  8.0 46.8 %copy-start.73 = (bf16[768]{0:T(1024)(128)(2,1)S(1)}, bf16[768]{0:T(1024)(128)(2,1)}, u32[]{:S(2)}) copy-start(bf16[768]{0:T(1024)(128)(2,1)} %param.22) | copy-start | bytes 4612
  8.1 47.6 %copy-start.15 = (bf16[256,1536]{1,0:T(8,128)(2,1)S(1)}, bf16[256,1536]{1,0:T(8,128)(2,1)}, u32[]{:S(2)}) copy-start(bf16[256,1536]{1,0:T(8,128)(2,1)} %refs_14_.1) | copy-start | bytes 2359300
  8.1 12.5 %collective-permute-start.6 = (bf16[480,384]{1,0:T(8,128)(2,1)S(1)}, bf16[480,384]{1,0:T(8,128)(2,1)S(1)}, u32[]{:S(2)}, u32[]{:S(2)}) collective-permute-start(bf16[480,384]{1,0:T(8,128)(2,1)S(1)} %get-tuple-element.71), channel_id=1, source_target_pairs={{0,1},{1,0},{2,3},{3,2},{4,5},{5,4},{6,7},{7,6},{8,9},{9,8},{10,11... | collective-permute-start | bytes 1105928 | tf_op jit(solution)/shard_map/ppermute | solution.py:737
  11.1 17.9 %collective-permute-start.7 = (bf16[480,384]{1,0:T(8,128)(2,1)S(1)}, bf16[480,384]{1,0:T(8,128)(2,1)S(1)}, u32[]{:S(2)}, u32[]{:S(2)}) collective-permute-start(bf16[480,384]{1,0:T(8,128)(2,1)S(1)} %get-tuple-element.72), channel_id=1, source_target_pairs={{0,2},{1,3},{2,0},{3,1},{4,6},{5,7},{6,4},{7,5},{8,10},{9,11},{10,... | collective-permute-start | bytes 1105928 | tf_op jit(solution)/shard_map/ppermute | solution.py:737
  12.6 16.5 %collective-permute-start.8 = (bf16[480,384]{1,0:T(8,128)(2,1)S(1)}, bf16[480,384]{1,0:T(8,128)(2,1)S(1)}, u32[]{:S(2)}, u32[]{:S(2)}) collective-permute-start(bf16[480,384]{1,0:T(8,128)(2,1)S(1)} %get-tuple-element.73), channel_id=1, source_target_pairs={{0,3},{1,2},{2,1},{3,0},{4,7},{5,6},{6,5},{7,4},{8,11},{9,10},{10,... | collective-permute-start | bytes 1105928 | tf_op jit(solution)/shard_map/ppermute | solution.py:737
  29.2 25.1 %collective-permute-start.10 = (bf16[1440,384]{1,0:T(8,128)(2,1)S(1)}, bf16[1440,384]{1,0:T(8,128)(2,1)S(1)}, u32[]{:S(2)}, u32[]{:S(2)}) collective-permute-start(bf16[1440,384]{1,0:T(8,128)(2,1)S(1)} %constant_dynamic-update-slice_fusion.refs_7_), channel_id=1, source_target_pairs={{0,8},{4,12},{8,0},{12,4},{16,24},{20,28},{24,16},{28,20},{1,9},{5... | collective-permute-start | bytes 3317768 | tf_op jit(solution)/shard_map/ppermute | solution.py:737
  30.6 25.1 %collective-permute-start.5 = (f32[8,896]{1,0:T(8,128)S(1)}, f32[8,896]{1,0:T(8,128)S(1)}, u32[]{:S(2)}, u32[]{:S(2)}) collective-permute-start(f32[8,896]{1,0:T(8,128)S(1)} %get-tuple-element.70.source_ref), channel_id=1, source_target_pairs={{0,3},{1,2},{2,1},{3,0},{4,7},{5,6},{6,5},{7,4},{8,11},{9,10},{10,... | collective-permute-start | bytes 86024 | tf_op jit(solution)/shard_map/ppermute | solution.py:737
  32.1 25.0 %collective-permute-start.4 = (f32[8,896]{1,0:T(8,128)S(1)}, f32[8,896]{1,0:T(8,128)S(1)}, u32[]{:S(2)}, u32[]{:S(2)}) collective-permute-start(f32[8,896]{1,0:T(8,128)S(1)} %get-tuple-element.70.source_ref), channel_id=1, source_target_pairs={{0,2},{1,3},{2,0},{3,1},{4,6},{5,7},{6,4},{7,5},{8,10},{9,11},{10,... | collective-permute-start | bytes 86024 | tf_op jit(solution)/shard_map/ppermute | solution.py:737
  33.2 24.5 %collective-permute-start.3 = (f32[8,896]{1,0:T(8,128)S(1)}, f32[8,896]{1,0:T(8,128)S(1)}, u32[]{:S(2)}, u32[]{:S(2)}) collective-permute-start(f32[8,896]{1,0:T(8,128)S(1)} %get-tuple-element.70.source_ref), channel_id=1, source_target_pairs={{0,1},{1,0},{2,3},{3,2},{4,5},{5,4},{6,7},{7,6},{8,9},{9,8},{10,11... | collective-permute-start | bytes 86024 | tf_op jit(solution)/shard_map/ppermute | solution.py:737
  34.5 61.7 %collective-permute-start.9 = (bf16[1440,384]{1,0:T(8,128)(2,1)S(1)}, bf16[1440,384]{1,0:T(8,128)(2,1)}, u32[]{:S(2)}, u32[]{:S(2)}) collective-permute-start(bf16[1440,384]{1,0:T(8,128)(2,1)S(1)} %constant_dynamic-update-slice_fusion.refs_7_), channel_id=1, source_target_pairs={{0,4},{4,0},{8,12},{12,8},{16,20},{20,16},{24,28},{28,24},{1,5},{5... | collective-permute-start | bytes 3317768 | tf_op jit(solution)/shard_map/ppermute | solution.py:737
  54.2 41.9 %collective-permute-start.11 = (bf16[1440,384]{1,0:T(8,128)(2,1)S(1)}, bf16[1440,384]{1,0:T(8,128)(2,1)}, u32[]{:S(2)}, u32[]{:S(2)}) collective-permute-start(bf16[1440,384]{1,0:T(8,128)(2,1)S(1)} %collective-permute-done.10.refs_9_), channel_id=1, source_target_pairs={{0,4},{4,0},{8,12},{12,8},{16,20},{20,16},{24,28},{28,24},{1,5},{5... | collective-permute-start | bytes 3317768 | tf_op jit(solution)/shard_map/ppermute | solution.py:737
  55.7 38.4 %collective-permute-start = (bf16[256,1536]{1,0:T(8,128)(2,1)S(1)}, bf16[256,1536]{1,0:T(8,128)(2,1)}, u32[]{:S(2)}, u32[]{:S(2)}) collective-permute-start(bf16[256,1536]{1,0:T(8,128)(2,1)S(1)} %copy-done.15), channel_id=1, source_target_pairs={{0,1},{1,0},{2,3},{3,2},{4,5},{5,4},{6,7},{7,6},{8,9},{9,8},{10,11... | collective-permute-start | bytes 2359304 | tf_op jit(solution)/shard_map/ppermute | solution.py:737
  57.1 38.4 %collective-permute-start.1 = (bf16[256,1536]{1,0:T(8,128)(2,1)S(1)}, bf16[256,1536]{1,0:T(8,128)(2,1)}, u32[]{:S(2)}, u32[]{:S(2)}) collective-permute-start(bf16[256,1536]{1,0:T(8,128)(2,1)S(1)} %copy-done.15), channel_id=1, source_target_pairs={{0,2},{1,3},{2,0},{3,1},{4,6},{5,7},{6,4},{7,5},{8,10},{9,11},{10,... | collective-permute-start | bytes 2359304 | tf_op jit(solution)/shard_map/ppermute | solution.py:737
  57.7 35.0 %collective-permute-start.2 = (bf16[256,1536]{1,0:T(8,128)(2,1)S(1)}, bf16[256,1536]{1,0:T(8,128)(2,1)}, u32[]{:S(2)}, u32[]{:S(2)}) collective-permute-start(bf16[256,1536]{1,0:T(8,128)(2,1)S(1)} %copy-done.15), channel_id=1, source_target_pairs={{0,3},{1,2},{2,1},{3,0},{4,7},{5,6},{6,5},{7,4},{8,11},{9,10},{10,... | collective-permute-start | bytes 2359304 | tf_op jit(solution)/shard_map/ppermute | solution.py:737
  92.7 39.0 %collective-permute-start.15 = (bf16[256,1536]{1,0:T(8,128)(2,1)}, bf16[256,1536]{1,0:T(8,128)(2,1)S(1)}, u32[]{:S(2)}, u32[]{:S(2)}) collective-permute-start(bf16[256,1536]{1,0:T(8,128)(2,1)} %refs_2_.1), channel_id=1, source_target_pairs={{0,1},{1,0},{2,3},{3,2},{4,5},{5,4},{6,7},{7,6},{8,9},{9,8},{10,11... | collective-permute-start | bytes 2359304 | tf_op jit(solution)/shard_map/ppermute | solution.py:737
  94.1 37.6 %collective-permute-start.16 = (bf16[256,1536]{1,0:T(8,128)(2,1)}, bf16[256,1536]{1,0:T(8,128)(2,1)S(1)}, u32[]{:S(2)}, u32[]{:S(2)}) collective-permute-start(bf16[256,1536]{1,0:T(8,128)(2,1)} %refs_2_.1), channel_id=1, source_target_pairs={{0,2},{1,3},{2,0},{3,1},{4,6},{5,7},{6,4},{7,5},{8,10},{9,11},{10,... | collective-permute-start | bytes 2359304 | tf_op jit(solution)/shard_map/ppermute | solution.py:737
  95.5 36.2 %collective-permute-start.17 = (bf16[256,1536]{1,0:T(8,128)(2,1)}, bf16[256,1536]{1,0:T(8,128)(2,1)S(1)}, u32[]{:S(2)}, u32[]{:S(2)}) collective-permute-start(bf16[256,1536]{1,0:T(8,128)(2,1)} %refs_2_.1), channel_id=1, source_target_pairs={{0,3},{1,2},{2,1},{3,0},{4,7},{5,6},{6,5},{7,4},{8,11},{9,10},{10,... | collective-permute-start | bytes 2359304 | tf_op jit(solution)/shard_map/ppermute | solution.py:737
  113.5 49.5 %copy-start = (f32[1024,1920]{1,0:T(8,128)}, f32[1024,1920]{1,0:T(8,128)S(1)}, u32[]{:S(2)}) copy-start(f32[1024,1920]{1,0:T(8,128)S(1)} %get-tuple-element.74.z_ref.v_ref.shared_ref.refs_4_.refs_1_.refs_13_) | copy-start | bytes 23592964
  140.2 11.3 %collective-permute-start.18 = (f32[32,256]{1,0:T(8,128)S(1)}, f32[32,256]{1,0:T(8,128)S(1)}, u32[]{:S(2)}, u32[]{:S(2)}) collective-permute-start(f32[32,256]{1,0:T(8,128)S(1)} %get-tuple-element.82.refs_0_.refs_8_), channel_id=1, source_target_pairs={{0,1},{1,0},{2,3},{3,2},{4,5},{5,4},{6,7},{7,6},{8,9},{9,8},{10,11... | collective-permute-start | bytes 98312 | tf_op jit(solution)/shard_map/ppermute | solution.py:737
  141.7 10.5 %collective-permute-start.19 = (f32[32,256]{1,0:T(8,128)S(1)}, f32[32,256]{1,0:T(8,128)S(1)}, u32[]{:S(2)}, u32[]{:S(2)}) collective-permute-start(f32[32,256]{1,0:T(8,128)S(1)} %get-tuple-element.82.refs_0_.refs_8_), channel_id=1, source_target_pairs={{0,2},{1,3},{2,0},{3,1},{4,6},{5,7},{6,4},{7,5},{8,10},{9,11},{10,... | collective-permute-start | bytes 98312 | tf_op jit(solution)/shard_map/ppermute | solution.py:737
  143.0 9.1 %collective-permute-start.20 = (f32[32,256]{1,0:T(8,128)S(1)}, f32[32,256]{1,0:T(8,128)S(1)}, u32[]{:S(2)}, u32[]{:S(2)}) collective-permute-start(f32[32,256]{1,0:T(8,128)S(1)} %get-tuple-element.82.refs_0_.refs_8_), channel_id=1, source_target_pairs={{0,3},{1,2},{2,1},{3,0},{4,7},{5,6},{6,5},{7,4},{8,11},{9,10},{10,... | collective-permute-start | bytes 98312 | tf_op jit(solution)/shard_map/ppermute | solution.py:737
  148.6 70.7 %collective-permute-start.12 = (bf16[256,1536]{1,0:T(8,128)(2,1)}, bf16[256,1536]{1,0:T(8,128)(2,1)}, u32[]{:S(2)}, u32[]{:S(2)}) collective-permute-start(bf16[256,1536]{1,0:T(8,128)(2,1)} %get-tuple-element.77), channel_id=1, source_target_pairs={{0,1},{1,0},{2,3},{3,2},{4,5},{5,4},{6,7},{7,6},{8,9},{9,8},{10,11... | collective-permute-start | bytes 2359304 | tf_op jit(solution)/shard_map/ppermute | solution.py:737
  150.1 80.6 %collective-permute-start.13 = (bf16[256,1536]{1,0:T(8,128)(2,1)}, bf16[256,1536]{1,0:T(8,128)(2,1)}, u32[]{:S(2)}, u32[]{:S(2)}) collective-permute-start(bf16[256,1536]{1,0:T(8,128)(2,1)} %get-tuple-element.78), channel_id=1, source_target_pairs={{0,2},{1,3},{2,0},{3,1},{4,6},{5,7},{6,4},{7,5},{8,10},{9,11},{10,... | collective-permute-start | bytes 2359304 | tf_op jit(solution)/shard_map/ppermute | solution.py:737
  151.5 88.7 %collective-permute-start.14 = (bf16[256,1536]{1,0:T(8,128)(2,1)}, bf16[256,1536]{1,0:T(8,128)(2,1)}, u32[]{:S(2)}, u32[]{:S(2)}) collective-permute-start(bf16[256,1536]{1,0:T(8,128)(2,1)} %get-tuple-element.79), channel_id=1, source_target_pairs={{0,3},{1,2},{2,1},{3,0},{4,7},{5,6},{6,5},{7,4},{8,11},{9,10},{10,... | collective-permute-start | bytes 2359304 | tf_op jit(solution)/shard_map/ppermute | solution.py:737
  203.0 37.6 %collective-permute-start.21 = (bf16[256,1536]{1,0:T(8,128)(2,1)}, bf16[256,1536]{1,0:T(8,128)(2,1)}, u32[]{:S(2)}, u32[]{:S(2)}) collective-permute-start(bf16[256,1536]{1,0:T(8,128)(2,1)} %get-tuple-element.108), channel_id=1, source_target_pairs={{0,1},{1,0},{2,3},{3,2},{4,5},{5,4},{6,7},{7,6},{8,9},{9,8},{10,11... | collective-permute-start | bytes 2359304 | tf_op jit(solution)/shard_map/ppermute | solution.py:737
  204.5 36.3 %collective-permute-start.22 = (bf16[256,1536]{1,0:T(8,128)(2,1)}, bf16[256,1536]{1,0:T(8,128)(2,1)}, u32[]{:S(2)}, u32[]{:S(2)}) collective-permute-start(bf16[256,1536]{1,0:T(8,128)(2,1)} %get-tuple-element.109), channel_id=1, source_target_pairs={{0,2},{1,3},{2,0},{3,1},{4,6},{5,7},{6,4},{7,5},{8,10},{9,11},{10,... | collective-permute-start | bytes 2359304 | tf_op jit(solution)/shard_map/ppermute | solution.py:737
  219.3 21.9 %collective-permute-start.23 = (bf16[256,1536]{1,0:T(8,128)(2,1)S(1)}, bf16[256,1536]{1,0:T(8,128)(2,1)S(1)}, u32[]{:S(2)}, u32[]{:S(2)}) collective-permute-start(bf16[256,1536]{1,0:T(8,128)(2,1)S(1)} %copy-done.51), channel_id=1, source_target_pairs={{0,3},{1,2},{2,1},{3,0},{4,7},{5,6},{6,5},{7,4},{8,11},{9,10},{10,... | collective-permute-start | bytes 2359304 | tf_op jit(solution)/shard_map/ppermute | solution.py:737
  230.7 16.4 %collective-permute-start.47 = (bf16[256,1536]{1,0:T(8,128)(2,1)}, bf16[256,1536]{1,0:T(8,128)(2,1)}, u32[]{:S(2)}, u32[]{:S(2)}) collective-permute-start(bf16[256,1536]{1,0:T(8,128)(2,1)} %get-tuple-element.125), channel_id=1, source_target_pairs={{0,4},{4,0},{8,12},{12,8},{16,20},{20,16},{24,28},{28,24},{1,5},{5... | collective-permute-start | bytes 2359304 | tf_op jit(solution)/shard_map/ppermute | solution.py:737
  240.2 12.3 %collective-permute-start.31 = (bf16[320,1536]{1,0:T(8,128)(2,1)}, bf16[320,1536]{1,0:T(8,128)(2,1)}, u32[]{:S(2)}, u32[]{:S(2)}) collective-permute-start(bf16[320,1536]{1,0:T(8,128)(2,1)} %get-tuple-element.121), channel_id=1, source_target_pairs={{0,4},{4,0},{8,12},{12,8},{16,20},{20,16},{24,28},{28,24},{1,5},{5... | collective-permute-start | bytes 2949128 | tf_op jit(solution)/shard_map/ppermute | solution.py:737
  240.7 17.1 %collective-permute-start.39 = (bf16[384,1536]{1,0:T(8,128)(2,1)}, bf16[384,1536]{1,0:T(8,128)(2,1)}, u32[]{:S(2)}, u32[]{:S(2)}) collective-permute-start(bf16[384,1536]{1,0:T(8,128)(2,1)} %get-tuple-element.123), channel_id=1, source_target_pairs={{0,4},{4,0},{8,12},{12,8},{16,20},{20,16},{24,28},{28,24},{1,5},{5... | collective-permute-start | bytes 3538952 | tf_op jit(solution)/shard_map/ppermute | solution.py:737
  240.7 13.9 %collective-permute-start.55 = (bf16[384,1536]{1,0:T(8,128)(2,1)}, bf16[384,1536]{1,0:T(8,128)(2,1)}, u32[]{:S(2)}, u32[]{:S(2)}) collective-permute-start(bf16[384,1536]{1,0:T(8,128)(2,1)} %get-tuple-element.128), channel_id=1, source_target_pairs={{0,4},{4,0},{8,12},{12,8},{16,20},{20,16},{24,28},{28,24},{1,5},{5... | collective-permute-start | bytes 3538952 | tf_op jit(solution)/shard_map/ppermute | solution.py:737
  249.4 13.4 %collective-permute-start.50 = (bf16[256,384]{1,0:T(8,128)(2,1)S(1)}, bf16[256,384]{1,0:T(8,128)(2,1)S(1)}, u32[]{:S(2)}, u32[]{:S(2)}) collective-permute-start(bf16[256,384]{1,0:T(8,128)(2,1)S(1)} %get-tuple-element.137), channel_id=1, source_target_pairs={{0,3},{1,2},{2,1},{3,0},{4,7},{5,6},{6,5},{7,4},{8,11},{9,10},{10,... | collective-permute-start | bytes 589832 | tf_op jit(solution)/shard_map/ppermute | solution.py:737
  251.7 13.1 %collective-permute-start.49 = (bf16[256,384]{1,0:T(8,128)(2,1)}, bf16[256,384]{1,0:T(8,128)(2,1)S(1)}, u32[]{:S(2)}, u32[]{:S(2)}) collective-permute-start(bf16[256,384]{1,0:T(8,128)(2,1)} %get-tuple-element.138), channel_id=1, source_target_pairs={{0,2},{1,3},{2,0},{3,1},{4,6},{5,7},{6,4},{7,5},{8,10},{9,11},{10,... | collective-permute-start | bytes 589832 | tf_op jit(solution)/shard_map/ppermute | solution.py:737
  252.5 77.9 %copy-start.68 = (f32[21392]{0:T(1024)}, f32[21392]{0:T(1024)S(1)}, u32[]{:S(2)}) copy-start(f32[21392]{0:T(1024)S(1)} %concatenate.44) | copy-start | bytes 256708
  252.5 13.0 %collective-permute-start.48 = (bf16[256,384]{1,0:T(8,128)(2,1)}, bf16[256,384]{1,0:T(8,128)(2,1)S(1)}, u32[]{:S(2)}, u32[]{:S(2)}) collective-permute-start(bf16[256,384]{1,0:T(8,128)(2,1)} %get-tuple-element.139), channel_id=1, source_target_pairs={{0,1},{1,0},{2,3},{3,2},{4,5},{5,4},{6,7},{7,6},{8,9},{9,8},{10,11... | collective-permute-start | bytes 589832 | tf_op jit(solution)/shard_map/ppermute | solution.py:737
  254.6 13.0 %collective-permute-start.32 = (bf16[320,384]{1,0:T(8,128)(2,1)S(1)}, bf16[320,384]{1,0:T(8,128)(2,1)S(1)}, u32[]{:S(2)}, u32[]{:S(2)}) collective-permute-start(bf16[320,384]{1,0:T(8,128)(2,1)S(1)} %get-tuple-element.135), channel_id=1, source_target_pairs={{0,1},{1,0},{2,3},{3,2},{4,5},{5,4},{6,7},{7,6},{8,9},{9,8},{10,11... | collective-permute-start | bytes 737288 | tf_op jit(solution)/shard_map/ppermute | solution.py:737
  257.8 31.4 %collective-permute-start.56 = (bf16[384,1536]{1,0:T(8,128)(2,1)S(1)}, bf16[384,1536]{1,0:T(8,128)(2,1)S(1)}, u32[]{:S(2)}, u32[]{:S(2)}) collective-permute-start(bf16[384,1536]{1,0:T(8,128)(2,1)S(1)} %add_convert_fusion.2), channel_id=1, source_target_pairs={{0,8},{4,12},{24,16},{28,20},{1,9},{5,13},{25,17},{29,21},{2,10},{... | collective-permute-start | bytes 3538952 | tf_op jit(solution)/shard_map/ppermute | solution.py:757
  262.8 11.2 %collective-permute-start.42 = (bf16[384,384]{1,0:T(8,128)(2,1)S(1)}, bf16[384,384]{1,0:T(8,128)(2,1)S(1)}, u32[]{:S(2)}, u32[]{:S(2)}) collective-permute-start(bf16[384,384]{1,0:T(8,128)(2,1)S(1)} %get-tuple-element.130), channel_id=1, source_target_pairs={{0,3},{1,2},{2,1},{3,0},{4,7},{5,6},{6,5},{7,4},{8,11},{9,10},{10,... | collective-permute-start | bytes 884744 | tf_op jit(solution)/shard_map/ppermute | solution.py:737
  264.8 15.6 %collective-permute-start.41 = (bf16[384,384]{1,0:T(8,128)(2,1)S(1)}, bf16[384,384]{1,0:T(8,128)(2,1)S(1)}, u32[]{:S(2)}, u32[]{:S(2)}) collective-permute-start(bf16[384,384]{1,0:T(8,128)(2,1)S(1)} %get-tuple-element.131), channel_id=1, source_target_pairs={{0,2},{1,3},{2,0},{3,1},{4,6},{5,7},{6,4},{7,5},{8,10},{9,11},{10,... | collective-permute-start | bytes 884744 | tf_op jit(solution)/shard_map/ppermute | solution.py:737
  265.5 16.7 %collective-permute-start.40 = (bf16[384,384]{1,0:T(8,128)(2,1)S(1)}, bf16[384,384]{1,0:T(8,128)(2,1)S(1)}, u32[]{:S(2)}, u32[]{:S(2)}) collective-permute-start(bf16[384,384]{1,0:T(8,128)(2,1)S(1)} %get-tuple-element.132), channel_id=1, source_target_pairs={{0,1},{1,0},{2,3},{3,2},{4,5},{5,4},{6,7},{7,6},{8,9},{9,8},{10,11... | collective-permute-start | bytes 884744 | tf_op jit(solution)/shard_map/ppermute | solution.py:737
  267.7 21.4 %collective-permute-start.33 = (bf16[320,384]{1,0:T(8,128)(2,1)S(1)}, bf16[320,384]{1,0:T(8,128)(2,1)S(1)}, u32[]{:S(2)}, u32[]{:S(2)}) collective-permute-start(bf16[320,384]{1,0:T(8,128)(2,1)S(1)} %get-tuple-element.134), channel_id=1, source_target_pairs={{0,2},{1,3},{2,0},{3,1},{4,6},{5,7},{6,4},{7,5},{8,10},{9,11},{10,... | collective-permute-start | bytes 737288 | tf_op jit(solution)/shard_map/ppermute | solution.py:737
  274.0 15.1 %collective-permute-start.34 = (bf16[320,384]{1,0:T(8,128)(2,1)S(1)}, bf16[320,384]{1,0:T(8,128)(2,1)S(1)}, u32[]{:S(2)}, u32[]{:S(2)}) collective-permute-start(bf16[320,384]{1,0:T(8,128)(2,1)S(1)} %get-tuple-element.133), channel_id=1, source_target_pairs={{0,3},{1,2},{2,1},{3,0},{4,7},{5,6},{6,5},{7,4},{8,11},{9,10},{10,... | collective-permute-start | bytes 737288 | tf_op jit(solution)/shard_map/ppermute | solution.py:737
  280.4 51.4 %collective-permute-start.51 = (bf16[1024,384]{1,0:T(8,128)(2,1)S(1)}, bf16[1024,384]{1,0:T(8,128)(2,1)S(1)}, u32[]{:S(2)}, u32[]{:S(2)}) collective-permute-start(bf16[1024,384]{1,0:T(8,128)(2,1)S(1)} %pad_maximum_fusion.1), channel_id=1, source_target_pairs={{0,8},{4,12},{24,16},{28,20},{1,9},{5,13},{25,17},{29,21},{2,10},{... | collective-permute-start | bytes 2359304 | tf_op jit(solution)/shard_map/ppermute | solution.py:757
  282.4 46.9 %collective-permute-start.43 = (bf16[1536,384]{1,0:T(8,128)(2,1)S(1)}, bf16[1536,384]{1,0:T(8,128)(2,1)S(1)}, u32[]{:S(2)}, u32[]{:S(2)}) collective-permute-start(bf16[1536,384]{1,0:T(8,128)(2,1)S(1)} %pad_maximum_fusion), channel_id=1, source_target_pairs={{0,8},{4,12},{24,16},{28,20},{1,9},{5,13},{25,17},{29,21},{2,10},{... | collective-permute-start | bytes 3538952 | tf_op jit(solution)/shard_map/ppermute | solution.py:757
  289.5 50.9 %collective-permute-start.57 = (bf16[384,1536]{1,0:T(8,128)(2,1)S(1)}, bf16[384,1536]{1,0:T(8,128)(2,1)S(1)}, u32[]{:S(2)}, u32[]{:S(2)}) collective-permute-start(bf16[384,1536]{1,0:T(8,128)(2,1)S(1)} %add_convert_fusion.1), channel_id=1, source_target_pairs={{8,16},{12,20},{16,8},{20,12},{9,17},{13,21},{17,9},{21,13},{10,18... | collective-permute-start | bytes 3538952 | tf_op jit(solution)/shard_map/ppermute | solution.py:759
  290.3 48.5 %collective-permute-start.35 = (bf16[704,384]{1,0:T(8,128)(2,1)S(1)}, bf16[704,384]{1,0:T(8,128)(2,1)S(1)}, u32[]{:S(2)}, u32[]{:S(2)}) collective-permute-start(bf16[704,384]{1,0:T(8,128)(2,1)S(1)} %fusion), channel_id=1, source_target_pairs={{0,8},{4,12},{24,16},{28,20},{1,9},{5,13},{25,17},{29,21},{2,10},{... | collective-permute-start | bytes 1622024 | tf_op jit(solution)/shard_map/ppermute | solution.py:757
  329.6 12.7 %collective-permute-start.44 = (bf16[1536,384]{1,0:T(8,128)(2,1)S(1)}, bf16[1536,384]{1,0:T(8,128)(2,1)S(1)}, u32[]{:S(2)}, u32[]{:S(2)}) collective-permute-start(bf16[1536,384]{1,0:T(8,128)(2,1)S(1)} %add_convert_fusion.4), channel_id=1, source_target_pairs={{8,16},{12,20},{16,8},{20,12},{9,17},{13,21},{17,9},{21,13},{10,18... | collective-permute-start | bytes 3538952 | tf_op jit(solution)/shard_map/ppermute | solution.py:759
  330.4 11.0 %collective-permute-start.25 = (f32[168,128]{1,0:T(8,128)S(1)}, f32[168,128]{1,0:T(8,128)S(1)}, u32[]{:S(2)}, u32[]{:S(2)}) collective-permute-start(f32[168,128]{1,0:T(8,128)S(1)} %pad_bitcast_fusion), channel_id=1, source_target_pairs={{0,2},{1,3},{2,0},{3,1},{4,6},{5,7},{6,4},{7,5},{8,10},{9,11},{10,... | collective-permute-start | bytes 258056 | tf_op jit(solution)/shard_map/ppermute | solution.py:737
  331.8 12.1 %collective-permute-start.26 = (f32[168,128]{1,0:T(8,128)S(1)}, f32[168,128]{1,0:T(8,128)S(1)}, u32[]{:S(2)}, u32[]{:S(2)}) collective-permute-start(f32[168,128]{1,0:T(8,128)S(1)} %pad_bitcast_fusion), channel_id=1, source_target_pairs={{0,3},{1,2},{2,1},{3,0},{4,7},{5,6},{6,5},{7,4},{8,11},{9,10},{10,... | collective-permute-start | bytes 258056 | tf_op jit(solution)/shard_map/ppermute | solution.py:737
  338.9 6.4 %collective-permute-start.24 = (f32[168,128]{1,0:T(8,128)S(1)}, f32[168,128]{1,0:T(8,128)S(1)}, u32[]{:S(2)}, u32[]{:S(2)}) collective-permute-start(f32[168,128]{1,0:T(8,128)S(1)} %pad_bitcast_fusion), channel_id=1, source_target_pairs={{0,1},{1,0},{2,3},{3,2},{4,5},{5,4},{6,7},{7,6},{8,9},{9,8},{10,11... | collective-permute-start | bytes 258056 | tf_op jit(solution)/shard_map/ppermute | solution.py:737
  340.4 25.6 %collective-permute-start.36 = (bf16[704,384]{1,0:T(8,128)(2,1)S(1)}, bf16[704,384]{1,0:T(8,128)(2,1)S(1)}, u32[]{:S(2)}, u32[]{:S(2)}) collective-permute-start(bf16[704,384]{1,0:T(8,128)(2,1)S(1)} %add_convert_fusion.11), channel_id=1, source_target_pairs={{8,16},{12,20},{16,8},{20,12},{9,17},{13,21},{17,9},{21,13},{10,18... | collective-permute-start | bytes 1622024 | tf_op jit(solution)/shard_map/ppermute | solution.py:759
  341.4 24.8 %collective-permute-start.52 = (bf16[1024,384]{1,0:T(8,128)(2,1)S(1)}, bf16[1024,384]{1,0:T(8,128)(2,1)S(1)}, u32[]{:S(2)}, u32[]{:S(2)}) collective-permute-start(bf16[1024,384]{1,0:T(8,128)(2,1)S(1)} %add_convert_fusion.8), channel_id=1, source_target_pairs={{8,16},{12,20},{16,8},{20,12},{9,17},{13,21},{17,9},{21,13},{10,18... | collective-permute-start | bytes 2359304 | tf_op jit(solution)/shard_map/ppermute | solution.py:759
  342.3 48.6 %collective-permute-start.58 = (bf16[384,1536]{1,0:T(8,128)(2,1)S(1)}, bf16[384,1536]{1,0:T(8,128)(2,1)S(1)}, u32[]{:S(2)}, u32[]{:S(2)}) collective-permute-start(bf16[384,1536]{1,0:T(8,128)(2,1)S(1)} %add_convert_fusion), channel_id=1, source_target_pairs={{8,0},{12,4},{16,24},{20,28},{9,1},{13,5},{17,25},{21,29},{10,2},{... | collective-permute-start | bytes 3538952 | tf_op jit(solution)/shard_map/ppermute | solution.py:761
  343.9 72.3 %collective-permute-start.45 = (bf16[1536,384]{1,0:T(8,128)(2,1)S(1)}, bf16[1536,384]{1,0:T(8,128)(2,1)S(1)}, u32[]{:S(2)}, u32[]{:S(2)}) collective-permute-start(bf16[1536,384]{1,0:T(8,128)(2,1)S(1)} %add_convert_fusion.3), channel_id=1, source_target_pairs={{8,0},{12,4},{16,24},{20,28},{9,1},{13,5},{17,25},{21,29},{10,2},{... | collective-permute-start | bytes 3538952 | tf_op jit(solution)/shard_map/ppermute | solution.py:761
  345.3 93.3 %collective-permute-start.28 = (f32[168,128]{1,0:T(8,128)S(1)}, f32[168,128]{1,0:T(8,128)S(1)}, u32[]{:S(2)}, u32[]{:S(2)}) collective-permute-start(f32[168,128]{1,0:T(8,128)S(1)} %add_add_fusion.1), channel_id=1, source_target_pairs={{0,8},{4,12},{8,0},{12,4},{16,24},{20,28},{24,16},{28,20},{1,9},{5... | collective-permute-start | bytes 258056 | tf_op jit(solution)/shard_map/ppermute | solution.py:737
  366.0 74.1 %collective-permute-start.29 = (f32[168,128]{1,0:T(8,128)S(1)}, f32[168,128]{1,0:T(8,128)S(1)}, u32[]{:S(2)}, u32[]{:S(2)}) collective-permute-start(f32[168,128]{1,0:T(8,128)S(1)} %add_add_fusion.1), channel_id=1, source_target_pairs={{0,12},{4,8},{8,4},{12,0},{16,28},{20,24},{24,20},{28,16},{1,13},{... | collective-permute-start | bytes 258056 | tf_op jit(solution)/shard_map/ppermute | solution.py:737
  366.2 73.0 %collective-permute-start.37 = (bf16[704,384]{1,0:T(8,128)(2,1)S(1)}, bf16[704,384]{1,0:T(8,128)(2,1)S(1)}, u32[]{:S(2)}, u32[]{:S(2)}) collective-permute-start(bf16[704,384]{1,0:T(8,128)(2,1)S(1)} %add_convert_fusion.10), channel_id=1, source_target_pairs={{8,0},{12,4},{16,24},{20,28},{9,1},{13,5},{17,25},{21,29},{10,2},{... | collective-permute-start | bytes 1622024 | tf_op jit(solution)/shard_map/ppermute | solution.py:761
  390.9 47.6 %collective-permute-start.53 = (bf16[1024,384]{1,0:T(8,128)(2,1)S(1)}, bf16[1024,384]{1,0:T(8,128)(2,1)S(1)}, u32[]{:S(2)}, u32[]{:S(2)}) collective-permute-start(bf16[1024,384]{1,0:T(8,128)(2,1)S(1)} %add_convert_fusion.7), channel_id=1, source_target_pairs={{8,0},{12,4},{16,24},{20,28},{9,1},{13,5},{17,25},{21,29},{10,2},{... | collective-permute-start | bytes 2359304 | tf_op jit(solution)/shard_map/ppermute | solution.py:761
  416.2 35.8 %collective-permute-start.59 = (bf16[384,1536]{1,0:T(8,128)(2,1)S(1)}, bf16[384,1536]{1,0:T(8,128)(2,1)}, u32[]{:S(2)}, u32[]{:S(2)}) collective-permute-start(bf16[384,1536]{1,0:T(8,128)(2,1)S(1)} %broadcast_select_fusion.refs_1_), channel_id=1, source_target_pairs={{0,4},{4,0},{8,12},{12,8},{16,20},{20,16},{24,28},{28,24},{1,5},{5... | collective-permute-start | bytes 3538952 | tf_op jit(solution)/shard_map/ppermute | solution.py:737
  438.5 17.2 %collective-permute-start.46 = (bf16[1536,384]{1,0:T(8,128)(2,1)S(1)}, bf16[1536,384]{1,0:T(8,128)(2,1)}, u32[]{:S(2)}, u32[]{:S(2)}) collective-permute-start(bf16[1536,384]{1,0:T(8,128)(2,1)S(1)} %broadcast_select_fusion.1.refs_1_), channel_id=1, source_target_pairs={{0,4},{4,0},{8,12},{12,8},{16,20},{20,16},{24,28},{28,24},{1,5},{5... | collective-permute-start | bytes 3538952 | tf_op jit(solution)/shard_map/ppermute | solution.py:737
  438.6 2.9 collective-permute-start.27
  439.2 16.5 %collective-permute-start.54 = (bf16[1024,384]{1,0:T(8,128)(2,1)S(1)}, bf16[1024,384]{1,0:T(8,128)(2,1)}, u32[]{:S(2)}, u32[]{:S(2)}) collective-permute-start(bf16[1024,384]{1,0:T(8,128)(2,1)S(1)} %broadcast_select_fusion.2.refs_3_), channel_id=1, source_target_pairs={{0,4},{4,0},{8,12},{12,8},{16,20},{20,16},{24,28},{28,24},{1,5},{5... | collective-permute-start | bytes 2359304 | tf_op jit(solution)/shard_map/ppermute | solution.py:737
  440.1 20.6 %collective-permute-start.38 = (bf16[704,384]{1,0:T(8,128)(2,1)}, bf16[704,384]{1,0:T(8,128)(2,1)}, u32[]{:S(2)}, u32[]{:S(2)}) collective-permute-start(bf16[704,384]{1,0:T(8,128)(2,1)} %broadcast_select_fusion.3.refs_1_), channel_id=1, source_target_pairs={{0,4},{4,0},{8,12},{12,8},{16,20},{20,16},{24,28},{28,24},{1,5},{5... | collective-permute-start | bytes 1622024 | tf_op jit(solution)/shard_map/ppermute | solution.py:737
  441.5 7.1 %collective-permute-start.30 = (f32[168,128]{1,0:T(8,128)S(1)}, f32[168,128]{1,0:T(8,128)S(1)}, u32[]{:S(2)}, u32[]{:S(2)}) collective-permute-start(f32[168,128]{1,0:T(8,128)S(1)} %add_add_fusion), channel_id=1, source_target_pairs={{0,16},{4,20},{8,24},{12,28},{16,0},{20,4},{24,8},{28,12},{1,17},{... | collective-permute-start | bytes 258056 | tf_op jit(solution)/shard_map/ppermute | solution.py:737
  (83 other events, 801.5 us)

commit v3 on v2

--- a/solution.py
+++ b/solution.py
@@ -555,19 +555,14 @@
     place_ref = refs[0]
     left_refs = refs[1 : 1 + lefts]
     right_refs = refs[1 + lefts : 1 + lefts + rights]
-    given_ref, kept_ref, stage_ref, sems, right_ref, right_sems = refs[1 + lefts + rights :]
+    given_ref, kept_ref, stage_ref, sems = refs[1 + lefts + rights :]
     core = place_ref[1]
     model = stage_ref.shape[1]
-    loads = [pltpu.make_async_copy(right_refs[n], right_ref.at[n], right_sems.at[n]) for n in range(rights)]
-    for load in loads:
-        load.start()
-    for load in loads:
-        load.wait()
     width = 384 if model % 384 == 0 else LANES
 
     def column(n, carry):
         cols = pl.ds(pl.multiple_of(n * width, LANES), width)
-        right = jnp.concatenate([right_ref[n, :, cols] for n in range(rights)], axis=0)
+        right = jnp.concatenate([ref[:, cols] for ref in right_refs], axis=0)
         row = 0
         for ref in left_refs:
             rows = ref.shape[1]
@@ -603,13 +598,11 @@
         (half, half),
         2 * tokens * rows * model,
         2 * tokens * (rows + model) + 2 * rows * model,
-        in_specs=[pl.BlockSpec(memory_space=pltpu.SMEM)] + [VM] * len(lefts) + [HBM] * len(rights),
+        in_specs=[pl.BlockSpec(memory_space=pltpu.SMEM)] + [VM] * (len(lefts) + len(rights)),
         out_specs=(HBM, HBM),
         scratch_shapes=[
             pltpu.VMEM((rows, model), BF),
             pltpu.SemaphoreType.DMA((2 * len(parts),)),
-            pltpu.VMEM((len(rights), rights[0].shape[0], model), BF),
-            pltpu.SemaphoreType.DMA((len(rights),)),
         ],
     )(place, *lefts, *rights)
 
@@ -930,7 +923,7 @@
     seg_spec = pl.BlockSpec((8, span), lambda r, p: (r, 0))
     shared_spec = per_row(padded, 2 * inner // padded)
     scan_flops = 4 * whole * span * inner
-    joint = 2 if pairs % 2 == 0 else 1
+    joint = 3 if pairs % 3 == 0 else 1
     broad = lambda col: pl.BlockSpec((span, joint * LANES), lambda r, p: (r, col + p))
     side = lambda w: jax.ShapeDtypeStruct((whole, w), F32)
     flipped_spec = pl.BlockSpec((LANES, span), lambda r, p: (r, 0))

time: 466 us -> 464 us (level)
  no operation moved by 1% of the time
where the time goes in v3:
time: 464 us; the launch traced here: 462 us
  waiting for transfers between devices  199 us (43%)
  Pallas kernels  121 us (26%)
  starting transfers between devices  86.3 us (19%)
  local copies, waits for them, and re-layouts  42.4 us (9%)
  other arithmetic  11.4 us (2%)
    pallas_call x19, Pallas kernels, run(): pl.pallas_call(kernel, out_shape=out_shape, cost_estimate=pl.CostEstimate...  121 us
    ppermute x48, waiting for transfers between devices, swap(): return lax.ppermute(value, axis, [(i, i ^ step) for i in range(size)])  91.2 us
    ppermute x4, waiting for transfers between devices, line_sum(): back = lax.ppermute(value, REP, outward)  69.2 us
    ppermute x48, starting transfers between devices, swap(): return lax.ppermute(value, axis, [(i, i ^ step) for i in range(size)])  65.8 us
    ppermute x4, waiting for transfers between devices, line_sum(): got = lax.ppermute(value, REP, inward)  38.9 us
    unnamed x182, local copies, waits for them, and re-layouts  30.5 us
    ppermute x4, starting transfers between devices, line_sum(): got = lax.ppermute(value, REP, inward)  12.3 us
  transfers between devices with their start and end apart: 60, of which 15 were waited for; matrix products, arithmetic and copies ran while one was open for 5% of the time, Pallas kernels for 24%

profile of v3, /device:TPU:0, one launch (start us, length us, event | category | flops | bytes accessed | tf_op | source)
XLA Modules:
  0.0 462.3 jit_solution(751545974820811253)
XLA Ops:
  2.1 2.4 copy-done.7
  5.9 2.1 shard_map.203
  8.1 3.0 collective-permute-start.6
  11.1 1.5 collective-permute-start.7
  12.6 7.9 %collective-permute-done.6 = bf16[480,384]{1,0:T(8,128)(2,1)S(1)} collective-permute-done((bf16[480,384]{1,0:T(8,128)(2,1)S(1)}, bf16[480,384]{1,0:T(8,128)(2,1)S(1)}, u32[]{:S(2)}, u32[]{:S(2)}) %collective-permute-start.6) | collective-permute-done | bytes 368672 | tf_op jit(solution)/shard_map/ppermute | solution.py:730
  20.6 8.5 %collective-permute-done.7 = bf16[480,384]{1,0:T(8,128)(2,1)S(1)} collective-permute-done((bf16[480,384]{1,0:T(8,128)(2,1)S(1)}, bf16[480,384]{1,0:T(8,128)(2,1)S(1)}, u32[]{:S(2)}, u32[]{:S(2)}) %collective-permute-start.7) | collective-permute-done | bytes 368672 | tf_op jit(solution)/shard_map/ppermute | solution.py:730
  29.2 1.4 collective-permute-start.10
  30.6 1.5 collective-permute-start.5
  34.5 19.8 %collective-permute-done.10.refs_9_ = bf16[1440,384]{1,0:T(8,128)(2,1)S(1)} collective-permute-done((bf16[1440,384]{1,0:T(8,128)(2,1)S(1)}, bf16[1440,384]{1,0:T(8,128)(2,1)S(1)}, u32[]{:S(2)}, u32[]{:S(2)}) %collective-permute-start.10) | collective-permute-done | bytes 1105952 | tf_op jit(solution)/shard_map/ppermute | solution.py:730
  55.7 1.4 collective-permute-start
  57.7 1.5 collective-permute-start.2
  61.6 31.1 %collective-permute-done.2.refs_3_ = bf16[256,1536]{1,0:T(8,128)(2,1)} collective-permute-done((bf16[256,1536]{1,0:T(8,128)(2,1)S(1)}, bf16[256,1536]{1,0:T(8,128)(2,1)}, u32[]{:S(2)}, u32[]{:S(2)}) %collective-permute-start.2) | collective-permute-done | bytes 786464 | tf_op jit(solution)/shard_map/ppermute | solution.py:730
  92.7 1.5 collective-permute-start.15
  94.1 1.4 collective-permute-start.16
  96.2 2.4 copy-done.8
  98.6 13.1 %shard_map.205 = (bf16[1024,1536]{1,0:T(8,128)(2,1)S(1)}, f32[1024,1920]{1,0:T(8,128)S(1)}, bf16[1920,1536]{1,0:T(8,128)(2,1)S(1)}) custom-call(bf16[256,1536]{1,0:T(8,128)(2,1)S(1)} %copy-done.15, bf16[256,1536]{1,0:T(8,128)(2,1)} %collective-permute-done.refs_1_, bf16[256,1536]{1,0:T(8,128)(2,1)} %collective-permute-done.1.refs_2_, ...), custom_call_target="tpu_custom_call" | custom-call | flops 6039797760 | bytes 25952256 | tf_op jit(solution)/shard_map/pallas_call | solution.py:62
  111.7 1.8 copy-done.62
  113.5 15.3 %shard_map.206 = (f32[1024,768]{1,0:T(8,128)S(1)}, f32[1024,768]{1,0:T(8,128)S(1)}, bf16[1024,768]{1,0:T(8,128)(2,1)S(1)}, f32[32,256]{1,0:T(8,128)S(1)}, f32[10...) custom-call(s32[3]{0:T(128)S(1)} %pad_add_fusion.refs_0_.refs_5_.pla, ...), custom_call_target="tpu_custom_call" | custom-call | flops 6442450944 | bytes 15728640 | tf_op jit(solution)/shard_map/pallas_call | solution.py:62
  131.0 5.7 %shard_map.208 = (f32[1024,768]{1,0:T(8,128)S(1)}, f32[32,256]{1,0:T(8,128)S(1)}) custom-call(bf16[256,1536]{1,0:T(8,128)(2,1)} %refs_2_.1, bf16[256,1536]{1,0:T(8,128)(2,1)S(1)} %collective-permute-done.15.refs_1_.refs_3_, bf16[256,1536]{1,0:T(8,128)(2,1)S(1)} %collective-permute-done.16.refs_2_.refs_4_, ...), custom_call_target="tpu_custom_call" | custom-call | flops 2415919104 | bytes 10223616 | tf_op jit(solution)/shard_map/pallas_call | solution.py:62
  139.4 1.5 collective-permute-start.18
  140.9 1.4 collective-permute-start.19
  142.9 4.9 %shard_map.207 = (f32[256,1536]{1,0:T(8,128)S(1)}, bf16[256,1536]{1,0:T(8,128)(2,1)}, bf16[256,1536]{1,0:T(8,128)(2,1)}, bf16[256,1536]{1,0:T(8,128)(2,1)}) custom-call(bf16[1024,768]{1,0:T(8,128)(2,1)S(1)} %get-tuple-element.75.gated_ref.refs_5_, bf16[768,1536]{1,0:T(8,128)(2,1)S(1)} %copy-done.38), custom_call_target="tpu_custom_call" | custom-call | flops 2415919104 | bytes 7077888 | tf_op jit(solution)/shard_map/pallas_call | solution.py:62
  147.9 1.5 collective-permute-start.12
  149.3 1.4 collective-permute-start.13
  151.4 3.6 shard_map.209
  155.2 7.0 %shard_map.210 = (bf16[1024,256]{1,0:T(8,128)(2,1)S(1)}, f32[8,256]{1,0:T(8,128)S(1)}, f32[1024,256]{1,0:T(8,128)S(1)}, f32[1024,128]{1,0:T(8,128)S(1)}, f32[1024,128]{1,0:T(8,128)S(1)}) custom-call(f32[1024,768]{1,0:T(8,128)S(1)} %get-tuple-element.86.refs_0_, f32[1024,1920]{1,0:T(8,128)S(1)} %get-tuple-element.74.z_ref.v_ref.shared_ref.refs_4_.refs_1_.refs_13_, ...), custom_call_target="tpu_custom_call" | custom-call | flops 4294967296 | bytes 6291456 | tf_op jit(solution)/shard_map/pallas_call | solution.py:62
  162.3 7.2 %shard_map.211 = (bf16[1024,256]{1,0:T(8,128)(2,1)S(1)}, f32[8,256]{1,0:T(8,128)S(1)}, f32[1024,256]{1,0:T(8,128)S(1)}, f32[1024,128]{1,0:T(8,128)S(1)}, f32[1024,128]{1,0:T(8,128)S(1)}) custom-call(f32[1024,768]{1,0:T(8,128)S(1)} %get-tuple-element.86.refs_0_, f32[1024,1920]{1,0:T(8,128)S(1)} %get-tuple-element.74.z_ref.v_ref.shared_ref.refs_4_.refs_1_.refs_13_, ...), custom_call_target="tpu_custom_call" | custom-call | flops 4294967296 | bytes 6291456 | tf_op jit(solution)/shard_map/pallas_call | solution.py:62
  175.7 12.9 %shard_map.212 = (bf16[1024,256]{1,0:T(8,128)(2,1)S(1)}, f32[8,256]{1,0:T(8,128)S(1)}, bf16[1024,384]{1,0:T(8,128)(2,1)S(1)}, f32[8,384]{1,0:T(8,128)S(1)}) custom-call(f32[1024,768]{1,0:T(8,128)} %copy-done.3, f32[1024,1920]{1,0:T(8,128)} %copy-done, f32[1024,768]{1,0:T(8,128)} %copy-done.2, f32[1024,768]{1,0:T(8,128)} %copy-done.1, f32[1024,384]{1,0:T(8,128)} %copy-done.4, ...), custom_call_target="tpu_custom_call" | custom-call | flops 4294967296 | bytes 6291456 | tf_op jit(solution)/shard_map/pallas_call | solution.py:62
  188.6 3.1 copy-done.65
  191.7 9.6 %shard_map.213 = (f32[256,1536]{1,0:T(8,128)S(1)}, bf16[256,1536]{1,0:T(8,128)(2,1)}, bf16[256,1536]{1,0:T(8,128)(2,1)}, bf16[256,1536]{1,0:T(8,128)(2,1)S(1)}) custom-call(bf16[1024,768]{1,0:T(8,128)(2,1)S(1)} %copy-done.42, bf16[1024,256]{1,0:T(8,128)(2,1)S(1)} %copy-done.55, bf16[1024,256]{1,0:T(8,128)(2,1)S(1)} %copy-done.58, ...), custom_call_target="tpu_custom_call" | custom-call | flops 6039797760 | bytes 12976128 | tf_op jit(solution)/shard_map/pallas_call | solution.py:62
  202.3 1.5 collective-permute-start.21
  203.7 1.4 collective-permute-start.22
  210.2 1.9 copy-done.63
  212.1 5.1 %shard_map.215 = (bf16[320,1536]{1,0:T(8,128)(2,1)}, bf16[320,1536]{1,0:T(8,128)(2,1)S(1)}) custom-call(s32[3]{0:T(128)S(1)} %pad_add_fusion.refs_0_.refs_5_.place_ref.refs_20_.refs_12_, bf16[1024,256]{1,0:T(8,128)(2,1)S(1)} %copy-done.61, bf16[1024,384]{1,0:T(8,128)(2,1)S(1)} %copy-done.53, bf16[1024,1536]{1,0:T(8,128)(2,1)S(1)} %copy-done.63), custom_call_target="tpu_custom_call" | custom-call | flops 2013265920 | bytes 6422528 | tf_op jit(solution)/shard_map/pallas_call | solution.py:62
  219.0 4.6 shard_map.217
  223.7 5.6 %shard_map.216 = (bf16[384,1536]{1,0:T(8,128)(2,1)}, bf16[384,1536]{1,0:T(8,128)(2,1)S(1)}) custom-call(s32[3]{0:T(128)S(1)} %pad_add_fusion.refs_0_.refs_5_.place_ref.refs_20_.refs_12_, bf16[1024,768]{1,0:T(8,128)(2,1)S(1)} %copy-done.43, bf16[1024,1536]{1,0:T(8,128)(2,1)S(1)} %copy-done.63), custom_call_target="tpu_custom_call" | custom-call | flops 2415919104 | bytes 7077888 | tf_op jit(solution)/shard_map/pallas_call | solution.py:62
  230.8 6.4 %shard_map.220 = (bf16[384,1536]{1,0:T(8,128)(2,1)}, bf16[384,1536]{1,0:T(8,128)(2,1)S(1)}) custom-call(s32[3]{0:T(128)S(1)} %pad_add_fusion.refs_0_.refs_5_.place_ref.refs_20_.refs_12_, bf16[1024,768]{1,0:T(8,128)(2,1)S(1)} %copy-done.40, bf16[256,1536]{1,0:T(8,128)(2,1)} %refs_2_.1, bf16[256,1536]{1,0:T(8,128)(2,1)S(1)} %copy-done.45, ...), custom_call_target="tpu_custom_call" | custom-call | flops 2415919104 | bytes 7077888 | tf_op jit(solution)/shard_map/pallas_call | solution.py:62
  239.2 5.1 %shard_map.214 = (bf16[256,1536]{1,0:T(8,128)(2,1)}, bf16[256,1536]{1,0:T(8,128)(2,1)}, f32[8,1536]{1,0:T(8,128)S(1)}) custom-call(f32[256,1536]{1,0:T(8,128)S(1)} %copy-done.18, bf16[256,1536]{1,0:T(8,128)(2,1)} %collective-permute-done.12.refs_1_, bf16[256,1536]{1,0:T(8,128)(2,1)} %collective-permute-done.13.refs_2_, ...), custom_call_target="tpu_custom_call" | custom-call | flops 11796480 | bytes 9437184 | tf_op jit(solution)/shard_map/pallas_call | solution.py:62
  245.2 1.4 add_convert_fusion.9
  247.4 2.3 collective-permute-start.50
  251.1 1.4 add_convert_fusion.6
  252.6 1.6 collective-permute-start.32
  254.2 1.6 add_convert_fusion.2
  255.8 3.4 collective-permute-start.56
  259.1 1.5 add_convert_fusion.5
  260.8 2.0 collective-permute-start.42
  266.2 5.8 %collective-permute-done.42 = bf16[384,384]{1,0:T(8,128)(2,1)S(1)} collective-permute-done((bf16[384,384]{1,0:T(8,128)(2,1)S(1)}, bf16[384,384]{1,0:T(8,128)(2,1)S(1)}, u32[]{:S(2)}, u32[]{:S(2)}) %collective-permute-start.42) | collective-permute-done | bytes 294944 | tf_op jit(solution)/shard_map/ppermute | solution.py:730
  272.0 2.3 collective-permute-start.34
  274.3 4.1 collective-permute-done.41
  278.4 1.8 collective-permute-start.51
  280.3 1.4 collective-permute-start.43
  281.7 5.4 %collective-permute-done.33 = bf16[320,384]{1,0:T(8,128)(2,1)S(1)} collective-permute-done((bf16[320,384]{1,0:T(8,128)(2,1)S(1)}, bf16[320,384]{1,0:T(8,128)(2,1)S(1)}, u32[]{:S(2)}, u32[]{:S(2)}) %collective-permute-start.33) | collective-permute-done | bytes 245792 | tf_op jit(solution)/shard_map/ppermute | solution.py:730
  288.3 5.7 %collective-permute-start.35 = (bf16[704,384]{1,0:T(8,128)(2,1)S(1)}, bf16[704,384]{1,0:T(8,128)(2,1)S(1)}, u32[]{:S(2)}, u32[]{:S(2)}) collective-permute-start(bf16[704,384]{1,0:T(8,128)(2,1)S(1)} %fusion), channel_id=1, source_target_pairs={{0,8},{4,12},{24,16},{28,20},{1,9},{5,13},{25,17},{29,21},{2,10},{... | collective-permute-start | bytes 1622024 | tf_op jit(solution)/shard_map/ppermute | solution.py:750
  294.0 33.2 %collective-permute-done.43 = bf16[1536,384]{1,0:T(8,128)(2,1)S(1)} collective-permute-done((bf16[1536,384]{1,0:T(8,128)(2,1)S(1)}, bf16[1536,384]{1,0:T(8,128)(2,1)S(1)}, u32[]{:S(2)}, u32[]{:S(2)}) %collective-permute-start.43) | collective-permute-done | bytes 1179680 | tf_op jit(solution)/shard_map/ppermute | solution.py:750
  328.4 1.4 collective-permute-start.25
  331.2 5.7 %collective-permute-done.35 = bf16[704,384]{1,0:T(8,128)(2,1)S(1)} collective-permute-done((bf16[704,384]{1,0:T(8,128)(2,1)S(1)}, bf16[704,384]{1,0:T(8,128)(2,1)S(1)}, u32[]{:S(2)}, u32[]{:S(2)}) %collective-permute-start.35) | collective-permute-done | bytes 540704 | tf_op jit(solution)/shard_map/ppermute | solution.py:750
  343.2 20.8 %collective-permute-start.28 = (f32[168,128]{1,0:T(8,128)S(1)}, f32[168,128]{1,0:T(8,128)S(1)}, u32[]{:S(2)}, u32[]{:S(2)}) collective-permute-start(f32[168,128]{1,0:T(8,128)S(1)} %add_add_fusion.1), channel_id=1, source_target_pairs={{0,8},{4,12},{8,0},{12,4},{16,24},{20,28},{24,16},{28,20},{1,9},{5... | collective-permute-start | bytes 258056 | tf_op jit(solution)/shard_map/ppermute | solution.py:730
  365.7 23.2 %collective-permute-done.58 = bf16[384,1536]{1,0:T(8,128)(2,1)S(1)} collective-permute-done((bf16[384,1536]{1,0:T(8,128)(2,1)S(1)}, bf16[384,1536]{1,0:T(8,128)(2,1)S(1)}, u32[]{:S(2)}, u32[]{:S(2)}) %collective-permute-start.58) | collective-permute-done | bytes 1179680 | tf_op jit(solution)/shard_map/ppermute | solution.py:754
  390.3 23.8 %collective-permute-done.45 = bf16[1536,384]{1,0:T(8,128)(2,1)S(1)} collective-permute-done((bf16[1536,384]{1,0:T(8,128)(2,1)S(1)}, bf16[1536,384]{1,0:T(8,128)(2,1)S(1)}, u32[]{:S(2)}, u32[]{:S(2)}) %collective-permute-start.45) | collective-permute-done | bytes 1179680 | tf_op jit(solution)/shard_map/ppermute | solution.py:754
  414.3 22.2 %collective-permute-done.53 = bf16[1024,384]{1,0:T(8,128)(2,1)S(1)} collective-permute-done((bf16[1024,384]{1,0:T(8,128)(2,1)S(1)}, bf16[1024,384]{1,0:T(8,128)(2,1)S(1)}, u32[]{:S(2)}, u32[]{:S(2)}) %collective-permute-start.53) | collective-permute-done | bytes 786464 | tf_op jit(solution)/shard_map/ppermute | solution.py:754
  440.0 6.6 %collective-permute-done.30 = f32[168,128]{1,0:T(8,128)S(1)} collective-permute-done((f32[168,128]{1,0:T(8,128)S(1)}, f32[168,128]{1,0:T(8,128)S(1)}, u32[]{:S(2)}, u32[]{:S(2)}) %collective-permute-start.30) | collective-permute-done | bytes 86048 | tf_op jit(solution)/shard_map/ppermute | solution.py:730
  449.9 3.7 shard_map.221
  453.7 5.1 %shard_map.218.refs_3_ = f32[6448,384]{1,0:T(8,128)} custom-call(s32[3]{0:T(128)S(1)} %pad_add_fusion.refs_0_.refs_5_.place_ref.refs_20_.refs_12_, bf16[1536,384]{1,0:T(8,128)(2,1)S(1)} %broadcast_select_fusion.1.refs_1_, bf16[1536,384]{1,0:T(8,128)(2,1)} %collective-permute-done.46.refs_2_, bf16[1024,384]{1,0:T(8,128)(2,1)S(1)} %broadcast_select_fusion.2.refs_3_, ...), custom_call_target="tpu_custom_call" | custom-call | flops 1966080 | bytes 11796480 | tf_op jit(solution)/shard_map/pallas_call | solution.py:62
  458.8 3.4 shard_map.219
  (359 shorter events, 60.5 us)
Async XLA Ops:
  8.0 46.8 %copy-start.73 = (bf16[768]{0:T(1024)(128)(2,1)S(1)}, bf16[768]{0:T(1024)(128)(2,1)}, u32[]{:S(2)}) copy-start(bf16[768]{0:T(1024)(128)(2,1)} %param.22) | copy-start | bytes 4612
  8.1 47.6 %copy-start.15 = (bf16[256,1536]{1,0:T(8,128)(2,1)S(1)}, bf16[256,1536]{1,0:T(8,128)(2,1)}, u32[]{:S(2)}) copy-start(bf16[256,1536]{1,0:T(8,128)(2,1)} %refs_14_.1) | copy-start | bytes 2359300
  8.1 12.5 %collective-permute-start.6 = (bf16[480,384]{1,0:T(8,128)(2,1)S(1)}, bf16[480,384]{1,0:T(8,128)(2,1)S(1)}, u32[]{:S(2)}, u32[]{:S(2)}) collective-permute-start(bf16[480,384]{1,0:T(8,128)(2,1)S(1)} %get-tuple-element.71), channel_id=1, source_target_pairs={{0,1},{1,0},{2,3},{3,2},{4,5},{5,4},{6,7},{7,6},{8,9},{9,8},{10,11... | collective-permute-start | bytes 1105928 | tf_op jit(solution)/shard_map/ppermute | solution.py:730
  11.1 17.9 %collective-permute-start.7 = (bf16[480,384]{1,0:T(8,128)(2,1)S(1)}, bf16[480,384]{1,0:T(8,128)(2,1)S(1)}, u32[]{:S(2)}, u32[]{:S(2)}) collective-permute-start(bf16[480,384]{1,0:T(8,128)(2,1)S(1)} %get-tuple-element.72), channel_id=1, source_target_pairs={{0,2},{1,3},{2,0},{3,1},{4,6},{5,7},{6,4},{7,5},{8,10},{9,11},{10,... | collective-permute-start | bytes 1105928 | tf_op jit(solution)/shard_map/ppermute | solution.py:730
  12.6 16.5 %collective-permute-start.8 = (bf16[480,384]{1,0:T(8,128)(2,1)S(1)}, bf16[480,384]{1,0:T(8,128)(2,1)S(1)}, u32[]{:S(2)}, u32[]{:S(2)}) collective-permute-start(bf16[480,384]{1,0:T(8,128)(2,1)S(1)} %get-tuple-element.73), channel_id=1, source_target_pairs={{0,3},{1,2},{2,1},{3,0},{4,7},{5,6},{6,5},{7,4},{8,11},{9,10},{10,... | collective-permute-start | bytes 1105928 | tf_op jit(solution)/shard_map/ppermute | solution.py:730
  29.2 25.1 %collective-permute-start.10 = (bf16[1440,384]{1,0:T(8,128)(2,1)S(1)}, bf16[1440,384]{1,0:T(8,128)(2,1)S(1)}, u32[]{:S(2)}, u32[]{:S(2)}) collective-permute-start(bf16[1440,384]{1,0:T(8,128)(2,1)S(1)} %constant_dynamic-update-slice_fusion.refs_7_), channel_id=1, source_target_pairs={{0,8},{4,12},{8,0},{12,4},{16,24},{20,28},{24,16},{28,20},{1,9},{5... | collective-permute-start | bytes 3317768 | tf_op jit(solution)/shard_map/ppermute | solution.py:730
  30.6 25.1 %collective-permute-start.5 = (f32[8,896]{1,0:T(8,128)S(1)}, f32[8,896]{1,0:T(8,128)S(1)}, u32[]{:S(2)}, u32[]{:S(2)}) collective-permute-start(f32[8,896]{1,0:T(8,128)S(1)} %get-tuple-element.70.source_ref), channel_id=1, source_target_pairs={{0,3},{1,2},{2,1},{3,0},{4,7},{5,6},{6,5},{7,4},{8,11},{9,10},{10,... | collective-permute-start | bytes 86024 | tf_op jit(solution)/shard_map/ppermute | solution.py:730
  32.1 25.0 %collective-permute-start.4 = (f32[8,896]{1,0:T(8,128)S(1)}, f32[8,896]{1,0:T(8,128)S(1)}, u32[]{:S(2)}, u32[]{:S(2)}) collective-permute-start(f32[8,896]{1,0:T(8,128)S(1)} %get-tuple-element.70.source_ref), channel_id=1, source_target_pairs={{0,2},{1,3},{2,0},{3,1},{4,6},{5,7},{6,4},{7,5},{8,10},{9,11},{10,... | collective-permute-start | bytes 86024 | tf_op jit(solution)/shard_map/ppermute | solution.py:730
  33.2 24.5 %collective-permute-start.3 = (f32[8,896]{1,0:T(8,128)S(1)}, f32[8,896]{1,0:T(8,128)S(1)}, u32[]{:S(2)}, u32[]{:S(2)}) collective-permute-start(f32[8,896]{1,0:T(8,128)S(1)} %get-tuple-element.70.source_ref), channel_id=1, source_target_pairs={{0,1},{1,0},{2,3},{3,2},{4,5},{5,4},{6,7},{7,6},{8,9},{9,8},{10,11... | collective-permute-start | bytes 86024 | tf_op jit(solution)/shard_map/ppermute | solution.py:730
  34.5 61.7 %collective-permute-start.9 = (bf16[1440,384]{1,0:T(8,128)(2,1)S(1)}, bf16[1440,384]{1,0:T(8,128)(2,1)}, u32[]{:S(2)}, u32[]{:S(2)}) collective-permute-start(bf16[1440,384]{1,0:T(8,128)(2,1)S(1)} %constant_dynamic-update-slice_fusion.refs_7_), channel_id=1, source_target_pairs={{0,4},{4,0},{8,12},{12,8},{16,20},{20,16},{24,28},{28,24},{1,5},{5... | collective-permute-start | bytes 3317768 | tf_op jit(solution)/shard_map/ppermute | solution.py:730
  54.2 41.9 %collective-permute-start.11 = (bf16[1440,384]{1,0:T(8,128)(2,1)S(1)}, bf16[1440,384]{1,0:T(8,128)(2,1)}, u32[]{:S(2)}, u32[]{:S(2)}) collective-permute-start(bf16[1440,384]{1,0:T(8,128)(2,1)S(1)} %collective-permute-done.10.refs_9_), channel_id=1, source_target_pairs={{0,4},{4,0},{8,12},{12,8},{16,20},{20,16},{24,28},{28,24},{1,5},{5... | collective-permute-start | bytes 3317768 | tf_op jit(solution)/shard_map/ppermute | solution.py:730
  55.7 38.4 %collective-permute-start = (bf16[256,1536]{1,0:T(8,128)(2,1)S(1)}, bf16[256,1536]{1,0:T(8,128)(2,1)}, u32[]{:S(2)}, u32[]{:S(2)}) collective-permute-start(bf16[256,1536]{1,0:T(8,128)(2,1)S(1)} %copy-done.15), channel_id=1, source_target_pairs={{0,1},{1,0},{2,3},{3,2},{4,5},{5,4},{6,7},{7,6},{8,9},{9,8},{10,11... | collective-permute-start | bytes 2359304 | tf_op jit(solution)/shard_map/ppermute | solution.py:730
  57.1 38.4 %collective-permute-start.1 = (bf16[256,1536]{1,0:T(8,128)(2,1)S(1)}, bf16[256,1536]{1,0:T(8,128)(2,1)}, u32[]{:S(2)}, u32[]{:S(2)}) collective-permute-start(bf16[256,1536]{1,0:T(8,128)(2,1)S(1)} %copy-done.15), channel_id=1, source_target_pairs={{0,2},{1,3},{2,0},{3,1},{4,6},{5,7},{6,4},{7,5},{8,10},{9,11},{10,... | collective-permute-start | bytes 2359304 | tf_op jit(solution)/shard_map/ppermute | solution.py:730
  57.7 35.0 %collective-permute-start.2 = (bf16[256,1536]{1,0:T(8,128)(2,1)S(1)}, bf16[256,1536]{1,0:T(8,128)(2,1)}, u32[]{:S(2)}, u32[]{:S(2)}) collective-permute-start(bf16[256,1536]{1,0:T(8,128)(2,1)S(1)} %copy-done.15), channel_id=1, source_target_pairs={{0,3},{1,2},{2,1},{3,0},{4,7},{5,6},{6,5},{7,4},{8,11},{9,10},{10,... | collective-permute-start | bytes 2359304 | tf_op jit(solution)/shard_map/ppermute | solution.py:730
  92.7 38.3 %collective-permute-start.15 = (bf16[256,1536]{1,0:T(8,128)(2,1)}, bf16[256,1536]{1,0:T(8,128)(2,1)S(1)}, u32[]{:S(2)}, u32[]{:S(2)}) collective-permute-start(bf16[256,1536]{1,0:T(8,128)(2,1)} %refs_2_.1), channel_id=1, source_target_pairs={{0,1},{1,0},{2,3},{3,2},{4,5},{5,4},{6,7},{7,6},{8,9},{9,8},{10,11... | collective-permute-start | bytes 2359304 | tf_op jit(solution)/shard_map/ppermute | solution.py:730
  94.1 36.8 %collective-permute-start.16 = (bf16[256,1536]{1,0:T(8,128)(2,1)}, bf16[256,1536]{1,0:T(8,128)(2,1)S(1)}, u32[]{:S(2)}, u32[]{:S(2)}) collective-permute-start(bf16[256,1536]{1,0:T(8,128)(2,1)} %refs_2_.1), channel_id=1, source_target_pairs={{0,2},{1,3},{2,0},{3,1},{4,6},{5,7},{6,4},{7,5},{8,10},{9,11},{10,... | collective-permute-start | bytes 2359304 | tf_op jit(solution)/shard_map/ppermute | solution.py:730
  95.5 35.5 %collective-permute-start.17 = (bf16[256,1536]{1,0:T(8,128)(2,1)}, bf16[256,1536]{1,0:T(8,128)(2,1)S(1)}, u32[]{:S(2)}, u32[]{:S(2)}) collective-permute-start(bf16[256,1536]{1,0:T(8,128)(2,1)} %refs_2_.1), channel_id=1, source_target_pairs={{0,3},{1,2},{2,1},{3,0},{4,7},{5,6},{6,5},{7,4},{8,11},{9,10},{10,... | collective-permute-start | bytes 2359304 | tf_op jit(solution)/shard_map/ppermute | solution.py:730
  113.5 48.7 %copy-start = (f32[1024,1920]{1,0:T(8,128)}, f32[1024,1920]{1,0:T(8,128)S(1)}, u32[]{:S(2)}) copy-start(f32[1024,1920]{1,0:T(8,128)S(1)} %get-tuple-element.74.z_ref.v_ref.shared_ref.refs_4_.refs_1_.refs_13_) | copy-start | bytes 23592964
  139.4 11.3 %collective-permute-start.18 = (f32[32,256]{1,0:T(8,128)S(1)}, f32[32,256]{1,0:T(8,128)S(1)}, u32[]{:S(2)}, u32[]{:S(2)}) collective-permute-start(f32[32,256]{1,0:T(8,128)S(1)} %get-tuple-element.82.refs_0_.refs_8_), channel_id=1, source_target_pairs={{0,1},{1,0},{2,3},{3,2},{4,5},{5,4},{6,7},{7,6},{8,9},{9,8},{10,11... | collective-permute-start | bytes 98312 | tf_op jit(solution)/shard_map/ppermute | solution.py:730
  140.9 10.5 %collective-permute-start.19 = (f32[32,256]{1,0:T(8,128)S(1)}, f32[32,256]{1,0:T(8,128)S(1)}, u32[]{:S(2)}, u32[]{:S(2)}) collective-permute-start(f32[32,256]{1,0:T(8,128)S(1)} %get-tuple-element.82.refs_0_.refs_8_), channel_id=1, source_target_pairs={{0,2},{1,3},{2,0},{3,1},{4,6},{5,7},{6,4},{7,5},{8,10},{9,11},{10,... | collective-permute-start | bytes 98312 | tf_op jit(solution)/shard_map/ppermute | solution.py:730
  142.3 9.1 %collective-permute-start.20 = (f32[32,256]{1,0:T(8,128)S(1)}, f32[32,256]{1,0:T(8,128)S(1)}, u32[]{:S(2)}, u32[]{:S(2)}) collective-permute-start(f32[32,256]{1,0:T(8,128)S(1)} %get-tuple-element.82.refs_0_.refs_8_), channel_id=1, source_target_pairs={{0,3},{1,2},{2,1},{3,0},{4,7},{5,6},{6,5},{7,4},{8,11},{9,10},{10,... | collective-permute-start | bytes 98312 | tf_op jit(solution)/shard_map/ppermute | solution.py:730
  147.9 70.4 %collective-permute-start.12 = (bf16[256,1536]{1,0:T(8,128)(2,1)}, bf16[256,1536]{1,0:T(8,128)(2,1)}, u32[]{:S(2)}, u32[]{:S(2)}) collective-permute-start(bf16[256,1536]{1,0:T(8,128)(2,1)} %get-tuple-element.77), channel_id=1, source_target_pairs={{0,1},{1,0},{2,3},{3,2},{4,5},{5,4},{6,7},{7,6},{8,9},{9,8},{10,11... | collective-permute-start | bytes 2359304 | tf_op jit(solution)/shard_map/ppermute | solution.py:730
  149.3 80.0 %collective-permute-start.13 = (bf16[256,1536]{1,0:T(8,128)(2,1)}, bf16[256,1536]{1,0:T(8,128)(2,1)}, u32[]{:S(2)}, u32[]{:S(2)}) collective-permute-start(bf16[256,1536]{1,0:T(8,128)(2,1)} %get-tuple-element.78), channel_id=1, source_target_pairs={{0,2},{1,3},{2,0},{3,1},{4,6},{5,7},{6,4},{7,5},{8,10},{9,11},{10,... | collective-permute-start | bytes 2359304 | tf_op jit(solution)/shard_map/ppermute | solution.py:730
  150.7 87.5 %collective-permute-start.14 = (bf16[256,1536]{1,0:T(8,128)(2,1)}, bf16[256,1536]{1,0:T(8,128)(2,1)}, u32[]{:S(2)}, u32[]{:S(2)}) collective-permute-start(bf16[256,1536]{1,0:T(8,128)(2,1)} %get-tuple-element.79), channel_id=1, source_target_pairs={{0,3},{1,2},{2,1},{3,0},{4,7},{5,6},{6,5},{7,4},{8,11},{9,10},{10,... | collective-permute-start | bytes 2359304 | tf_op jit(solution)/shard_map/ppermute | solution.py:730
  202.3 36.4 %collective-permute-start.21 = (bf16[256,1536]{1,0:T(8,128)(2,1)}, bf16[256,1536]{1,0:T(8,128)(2,1)}, u32[]{:S(2)}, u32[]{:S(2)}) collective-permute-start(bf16[256,1536]{1,0:T(8,128)(2,1)} %get-tuple-element.108), channel_id=1, source_target_pairs={{0,1},{1,0},{2,3},{3,2},{4,5},{5,4},{6,7},{7,6},{8,9},{9,8},{10,11... | collective-permute-start | bytes 2359304 | tf_op jit(solution)/shard_map/ppermute | solution.py:730
  203.7 35.0 %collective-permute-start.22 = (bf16[256,1536]{1,0:T(8,128)(2,1)}, bf16[256,1536]{1,0:T(8,128)(2,1)}, u32[]{:S(2)}, u32[]{:S(2)}) collective-permute-start(bf16[256,1536]{1,0:T(8,128)(2,1)} %get-tuple-element.109), channel_id=1, source_target_pairs={{0,2},{1,3},{2,0},{3,1},{4,6},{5,7},{6,4},{7,5},{8,10},{9,11},{10,... | collective-permute-start | bytes 2359304 | tf_op jit(solution)/shard_map/ppermute | solution.py:730
  218.3 20.8 %collective-permute-start.23 = (bf16[256,1536]{1,0:T(8,128)(2,1)S(1)}, bf16[256,1536]{1,0:T(8,128)(2,1)S(1)}, u32[]{:S(2)}, u32[]{:S(2)}) collective-permute-start(bf16[256,1536]{1,0:T(8,128)(2,1)S(1)} %copy-done.51), channel_id=1, source_target_pairs={{0,3},{1,2},{2,1},{3,0},{4,7},{5,6},{6,5},{7,4},{8,11},{9,10},{10,... | collective-permute-start | bytes 2359304 | tf_op jit(solution)/shard_map/ppermute | solution.py:730
  229.3 15.8 %collective-permute-start.47 = (bf16[256,1536]{1,0:T(8,128)(2,1)}, bf16[256,1536]{1,0:T(8,128)(2,1)}, u32[]{:S(2)}, u32[]{:S(2)}) collective-permute-start(bf16[256,1536]{1,0:T(8,128)(2,1)} %get-tuple-element.125), channel_id=1, source_target_pairs={{0,4},{4,0},{8,12},{12,8},{16,20},{20,16},{24,28},{28,24},{1,5},{5... | collective-permute-start | bytes 2359304 | tf_op jit(solution)/shard_map/ppermute | solution.py:730
  238.2 12.3 %collective-permute-start.31 = (bf16[320,1536]{1,0:T(8,128)(2,1)}, bf16[320,1536]{1,0:T(8,128)(2,1)}, u32[]{:S(2)}, u32[]{:S(2)}) collective-permute-start(bf16[320,1536]{1,0:T(8,128)(2,1)} %get-tuple-element.121), channel_id=1, source_target_pairs={{0,4},{4,0},{8,12},{12,8},{16,20},{20,16},{24,28},{28,24},{1,5},{5... | collective-permute-start | bytes 2949128 | tf_op jit(solution)/shard_map/ppermute | solution.py:730
  238.6 17.1 %collective-permute-start.39 = (bf16[384,1536]{1,0:T(8,128)(2,1)}, bf16[384,1536]{1,0:T(8,128)(2,1)}, u32[]{:S(2)}, u32[]{:S(2)}) collective-permute-start(bf16[384,1536]{1,0:T(8,128)(2,1)} %get-tuple-element.123), channel_id=1, source_target_pairs={{0,4},{4,0},{8,12},{12,8},{16,20},{20,16},{24,28},{28,24},{1,5},{5... | collective-permute-start | bytes 3538952 | tf_op jit(solution)/shard_map/ppermute | solution.py:730
  238.7 13.9 %collective-permute-start.55 = (bf16[384,1536]{1,0:T(8,128)(2,1)}, bf16[384,1536]{1,0:T(8,128)(2,1)}, u32[]{:S(2)}, u32[]{:S(2)}) collective-permute-start(bf16[384,1536]{1,0:T(8,128)(2,1)} %get-tuple-element.128), channel_id=1, source_target_pairs={{0,4},{4,0},{8,12},{12,8},{16,20},{20,16},{24,28},{28,24},{1,5},{5... | collective-permute-start | bytes 3538952 | tf_op jit(solution)/shard_map/ppermute | solution.py:730
  247.4 13.4 %collective-permute-start.50 = (bf16[256,384]{1,0:T(8,128)(2,1)S(1)}, bf16[256,384]{1,0:T(8,128)(2,1)S(1)}, u32[]{:S(2)}, u32[]{:S(2)}) collective-permute-start(bf16[256,384]{1,0:T(8,128)(2,1)S(1)} %get-tuple-element.137), channel_id=1, source_target_pairs={{0,3},{1,2},{2,1},{3,0},{4,7},{5,6},{6,5},{7,4},{8,11},{9,10},{10,... | collective-permute-start | bytes 589832 | tf_op jit(solution)/shard_map/ppermute | solution.py:730
  249.7 13.1 %collective-permute-start.49 = (bf16[256,384]{1,0:T(8,128)(2,1)}, bf16[256,384]{1,0:T(8,128)(2,1)S(1)}, u32[]{:S(2)}, u32[]{:S(2)}) collective-permute-start(bf16[256,384]{1,0:T(8,128)(2,1)} %get-tuple-element.138), channel_id=1, source_target_pairs={{0,2},{1,3},{2,0},{3,1},{4,6},{5,7},{6,4},{7,5},{8,10},{9,11},{10,... | collective-permute-start | bytes 589832 | tf_op jit(solution)/shard_map/ppermute | solution.py:730
  250.5 77.9 %copy-start.68 = (f32[21392]{0:T(1024)}, f32[21392]{0:T(1024)S(1)}, u32[]{:S(2)}) copy-start(f32[21392]{0:T(1024)S(1)} %concatenate.44) | copy-start | bytes 256708
  250.5 13.0 %collective-permute-start.48 = (bf16[256,384]{1,0:T(8,128)(2,1)}, bf16[256,384]{1,0:T(8,128)(2,1)S(1)}, u32[]{:S(2)}, u32[]{:S(2)}) collective-permute-start(bf16[256,384]{1,0:T(8,128)(2,1)} %get-tuple-element.139), channel_id=1, source_target_pairs={{0,1},{1,0},{2,3},{3,2},{4,5},{5,4},{6,7},{7,6},{8,9},{9,8},{10,11... | collective-permute-start | bytes 589832 | tf_op jit(solution)/shard_map/ppermute | solution.py:730
  252.6 13.0 %collective-permute-start.32 = (bf16[320,384]{1,0:T(8,128)(2,1)S(1)}, bf16[320,384]{1,0:T(8,128)(2,1)S(1)}, u32[]{:S(2)}, u32[]{:S(2)}) collective-permute-start(bf16[320,384]{1,0:T(8,128)(2,1)S(1)} %get-tuple-element.135), channel_id=1, source_target_pairs={{0,1},{1,0},{2,3},{3,2},{4,5},{5,4},{6,7},{7,6},{8,9},{9,8},{10,11... | collective-permute-start | bytes 737288 | tf_op jit(solution)/shard_map/ppermute | solution.py:730
  255.8 31.4 %collective-permute-start.56 = (bf16[384,1536]{1,0:T(8,128)(2,1)S(1)}, bf16[384,1536]{1,0:T(8,128)(2,1)S(1)}, u32[]{:S(2)}, u32[]{:S(2)}) collective-permute-start(bf16[384,1536]{1,0:T(8,128)(2,1)S(1)} %add_convert_fusion.2), channel_id=1, source_target_pairs={{0,8},{4,12},{24,16},{28,20},{1,9},{5,13},{25,17},{29,21},{2,10},{... | collective-permute-start | bytes 3538952 | tf_op jit(solution)/shard_map/ppermute | solution.py:750
  260.8 11.2 %collective-permute-start.42 = (bf16[384,384]{1,0:T(8,128)(2,1)S(1)}, bf16[384,384]{1,0:T(8,128)(2,1)S(1)}, u32[]{:S(2)}, u32[]{:S(2)}) collective-permute-start(bf16[384,384]{1,0:T(8,128)(2,1)S(1)} %get-tuple-element.130), channel_id=1, source_target_pairs={{0,3},{1,2},{2,1},{3,0},{4,7},{5,6},{6,5},{7,4},{8,11},{9,10},{10,... | collective-permute-start | bytes 884744 | tf_op jit(solution)/shard_map/ppermute | solution.py:730
  262.8 15.6 %collective-permute-start.41 = (bf16[384,384]{1,0:T(8,128)(2,1)S(1)}, bf16[384,384]{1,0:T(8,128)(2,1)S(1)}, u32[]{:S(2)}, u32[]{:S(2)}) collective-permute-start(bf16[384,384]{1,0:T(8,128)(2,1)S(1)} %get-tuple-element.131), channel_id=1, source_target_pairs={{0,2},{1,3},{2,0},{3,1},{4,6},{5,7},{6,4},{7,5},{8,10},{9,11},{10,... | collective-permute-start | bytes 884744 | tf_op jit(solution)/shard_map/ppermute | solution.py:730
  263.4 16.8 %collective-permute-start.40 = (bf16[384,384]{1,0:T(8,128)(2,1)S(1)}, bf16[384,384]{1,0:T(8,128)(2,1)S(1)}, u32[]{:S(2)}, u32[]{:S(2)}) collective-permute-start(bf16[384,384]{1,0:T(8,128)(2,1)S(1)} %get-tuple-element.132), channel_id=1, source_target_pairs={{0,1},{1,0},{2,3},{3,2},{4,5},{5,4},{6,7},{7,6},{8,9},{9,8},{10,11... | collective-permute-start | bytes 884744 | tf_op jit(solution)/shard_map/ppermute | solution.py:730
  265.7 21.4 %collective-permute-start.33 = (bf16[320,384]{1,0:T(8,128)(2,1)S(1)}, bf16[320,384]{1,0:T(8,128)(2,1)S(1)}, u32[]{:S(2)}, u32[]{:S(2)}) collective-permute-start(bf16[320,384]{1,0:T(8,128)(2,1)S(1)} %get-tuple-element.134), channel_id=1, source_target_pairs={{0,2},{1,3},{2,0},{3,1},{4,6},{5,7},{6,4},{7,5},{8,10},{9,11},{10,... | collective-permute-start | bytes 737288 | tf_op jit(solution)/shard_map/ppermute | solution.py:730
  272.0 15.1 %collective-permute-start.34 = (bf16[320,384]{1,0:T(8,128)(2,1)S(1)}, bf16[320,384]{1,0:T(8,128)(2,1)S(1)}, u32[]{:S(2)}, u32[]{:S(2)}) collective-permute-start(bf16[320,384]{1,0:T(8,128)(2,1)S(1)} %get-tuple-element.133), channel_id=1, source_target_pairs={{0,3},{1,2},{2,1},{3,0},{4,7},{5,6},{6,5},{7,4},{8,11},{9,10},{10,... | collective-permute-start | bytes 737288 | tf_op jit(solution)/shard_map/ppermute | solution.py:730
  278.4 51.4 %collective-permute-start.51 = (bf16[1024,384]{1,0:T(8,128)(2,1)S(1)}, bf16[1024,384]{1,0:T(8,128)(2,1)S(1)}, u32[]{:S(2)}, u32[]{:S(2)}) collective-permute-start(bf16[1024,384]{1,0:T(8,128)(2,1)S(1)} %pad_maximum_fusion.1), channel_id=1, source_target_pairs={{0,8},{4,12},{24,16},{28,20},{1,9},{5,13},{25,17},{29,21},{2,10},{... | collective-permute-start | bytes 2359304 | tf_op jit(solution)/shard_map/ppermute | solution.py:750
  280.3 46.9 %collective-permute-start.43 = (bf16[1536,384]{1,0:T(8,128)(2,1)S(1)}, bf16[1536,384]{1,0:T(8,128)(2,1)S(1)}, u32[]{:S(2)}, u32[]{:S(2)}) collective-permute-start(bf16[1536,384]{1,0:T(8,128)(2,1)S(1)} %pad_maximum_fusion), channel_id=1, source_target_pairs={{0,8},{4,12},{24,16},{28,20},{1,9},{5,13},{25,17},{29,21},{2,10},{... | collective-permute-start | bytes 3538952 | tf_op jit(solution)/shard_map/ppermute | solution.py:750
  287.5 50.9 %collective-permute-start.57 = (bf16[384,1536]{1,0:T(8,128)(2,1)S(1)}, bf16[384,1536]{1,0:T(8,128)(2,1)S(1)}, u32[]{:S(2)}, u32[]{:S(2)}) collective-permute-start(bf16[384,1536]{1,0:T(8,128)(2,1)S(1)} %add_convert_fusion.1), channel_id=1, source_target_pairs={{8,16},{12,20},{16,8},{20,12},{9,17},{13,21},{17,9},{21,13},{10,18... | collective-permute-start | bytes 3538952 | tf_op jit(solution)/shard_map/ppermute | solution.py:752
  288.3 48.5 %collective-permute-start.35 = (bf16[704,384]{1,0:T(8,128)(2,1)S(1)}, bf16[704,384]{1,0:T(8,128)(2,1)S(1)}, u32[]{:S(2)}, u32[]{:S(2)}) collective-permute-start(bf16[704,384]{1,0:T(8,128)(2,1)S(1)} %fusion), channel_id=1, source_target_pairs={{0,8},{4,12},{24,16},{28,20},{1,9},{5,13},{25,17},{29,21},{2,10},{... | collective-permute-start | bytes 1622024 | tf_op jit(solution)/shard_map/ppermute | solution.py:750
  327.6 12.7 %collective-permute-start.44 = (bf16[1536,384]{1,0:T(8,128)(2,1)S(1)}, bf16[1536,384]{1,0:T(8,128)(2,1)S(1)}, u32[]{:S(2)}, u32[]{:S(2)}) collective-permute-start(bf16[1536,384]{1,0:T(8,128)(2,1)S(1)} %add_convert_fusion.4), channel_id=1, source_target_pairs={{8,16},{12,20},{16,8},{20,12},{9,17},{13,21},{17,9},{21,13},{10,18... | collective-permute-start | bytes 3538952 | tf_op jit(solution)/shard_map/ppermute | solution.py:752
  328.4 11.0 %collective-permute-start.25 = (f32[168,128]{1,0:T(8,128)S(1)}, f32[168,128]{1,0:T(8,128)S(1)}, u32[]{:S(2)}, u32[]{:S(2)}) collective-permute-start(f32[168,128]{1,0:T(8,128)S(1)} %pad_bitcast_fusion), channel_id=1, source_target_pairs={{0,2},{1,3},{2,0},{3,1},{4,6},{5,7},{6,4},{7,5},{8,10},{9,11},{10,... | collective-permute-start | bytes 258056 | tf_op jit(solution)/shard_map/ppermute | solution.py:730
  329.8 12.1 %collective-permute-start.26 = (f32[168,128]{1,0:T(8,128)S(1)}, f32[168,128]{1,0:T(8,128)S(1)}, u32[]{:S(2)}, u32[]{:S(2)}) collective-permute-start(f32[168,128]{1,0:T(8,128)S(1)} %pad_bitcast_fusion), channel_id=1, source_target_pairs={{0,3},{1,2},{2,1},{3,0},{4,7},{5,6},{6,5},{7,4},{8,11},{9,10},{10,... | collective-permute-start | bytes 258056 | tf_op jit(solution)/shard_map/ppermute | solution.py:730
  336.8 6.4 %collective-permute-start.24 = (f32[168,128]{1,0:T(8,128)S(1)}, f32[168,128]{1,0:T(8,128)S(1)}, u32[]{:S(2)}, u32[]{:S(2)}) collective-permute-start(f32[168,128]{1,0:T(8,128)S(1)} %pad_bitcast_fusion), channel_id=1, source_target_pairs={{0,1},{1,0},{2,3},{3,2},{4,5},{5,4},{6,7},{7,6},{8,9},{9,8},{10,11... | collective-permute-start | bytes 258056 | tf_op jit(solution)/shard_map/ppermute | solution.py:730
  338.4 25.6 %collective-permute-start.36 = (bf16[704,384]{1,0:T(8,128)(2,1)S(1)}, bf16[704,384]{1,0:T(8,128)(2,1)S(1)}, u32[]{:S(2)}, u32[]{:S(2)}) collective-permute-start(bf16[704,384]{1,0:T(8,128)(2,1)S(1)} %add_convert_fusion.11), channel_id=1, source_target_pairs={{8,16},{12,20},{16,8},{20,12},{9,17},{13,21},{17,9},{21,13},{10,18... | collective-permute-start | bytes 1622024 | tf_op jit(solution)/shard_map/ppermute | solution.py:752
  339.4 24.8 %collective-permute-start.52 = (bf16[1024,384]{1,0:T(8,128)(2,1)S(1)}, bf16[1024,384]{1,0:T(8,128)(2,1)S(1)}, u32[]{:S(2)}, u32[]{:S(2)}) collective-permute-start(bf16[1024,384]{1,0:T(8,128)(2,1)S(1)} %add_convert_fusion.8), channel_id=1, source_target_pairs={{8,16},{12,20},{16,8},{20,12},{9,17},{13,21},{17,9},{21,13},{10,18... | collective-permute-start | bytes 2359304 | tf_op jit(solution)/shard_map/ppermute | solution.py:752
  340.2 48.6 %collective-permute-start.58 = (bf16[384,1536]{1,0:T(8,128)(2,1)S(1)}, bf16[384,1536]{1,0:T(8,128)(2,1)S(1)}, u32[]{:S(2)}, u32[]{:S(2)}) collective-permute-start(bf16[384,1536]{1,0:T(8,128)(2,1)S(1)} %add_convert_fusion), channel_id=1, source_target_pairs={{8,0},{12,4},{16,24},{20,28},{9,1},{13,5},{17,25},{21,29},{10,2},{... | collective-permute-start | bytes 3538952 | tf_op jit(solution)/shard_map/ppermute | solution.py:754
  341.9 72.3 %collective-permute-start.45 = (bf16[1536,384]{1,0:T(8,128)(2,1)S(1)}, bf16[1536,384]{1,0:T(8,128)(2,1)S(1)}, u32[]{:S(2)}, u32[]{:S(2)}) collective-permute-start(bf16[1536,384]{1,0:T(8,128)(2,1)S(1)} %add_convert_fusion.3), channel_id=1, source_target_pairs={{8,0},{12,4},{16,24},{20,28},{9,1},{13,5},{17,25},{21,29},{10,2},{... | collective-permute-start | bytes 3538952 | tf_op jit(solution)/shard_map/ppermute | solution.py:754
  343.2 93.3 %collective-permute-start.28 = (f32[168,128]{1,0:T(8,128)S(1)}, f32[168,128]{1,0:T(8,128)S(1)}, u32[]{:S(2)}, u32[]{:S(2)}) collective-permute-start(f32[168,128]{1,0:T(8,128)S(1)} %add_add_fusion.1), channel_id=1, source_target_pairs={{0,8},{4,12},{8,0},{12,4},{16,24},{20,28},{24,16},{28,20},{1,9},{5... | collective-permute-start | bytes 258056 | tf_op jit(solution)/shard_map/ppermute | solution.py:730
  364.0 74.1 %collective-permute-start.29 = (f32[168,128]{1,0:T(8,128)S(1)}, f32[168,128]{1,0:T(8,128)S(1)}, u32[]{:S(2)}, u32[]{:S(2)}) collective-permute-start(f32[168,128]{1,0:T(8,128)S(1)} %add_add_fusion.1), channel_id=1, source_target_pairs={{0,12},{4,8},{8,4},{12,0},{16,28},{20,24},{24,20},{28,16},{1,13},{... | collective-permute-start | bytes 258056 | tf_op jit(solution)/shard_map/ppermute | solution.py:730
  364.2 73.0 %collective-permute-start.37 = (bf16[704,384]{1,0:T(8,128)(2,1)S(1)}, bf16[704,384]{1,0:T(8,128)(2,1)S(1)}, u32[]{:S(2)}, u32[]{:S(2)}) collective-permute-start(bf16[704,384]{1,0:T(8,128)(2,1)S(1)} %add_convert_fusion.10), channel_id=1, source_target_pairs={{8,0},{12,4},{16,24},{20,28},{9,1},{13,5},{17,25},{21,29},{10,2},{... | collective-permute-start | bytes 1622024 | tf_op jit(solution)/shard_map/ppermute | solution.py:754
  388.9 47.6 %collective-permute-start.53 = (bf16[1024,384]{1,0:T(8,128)(2,1)S(1)}, bf16[1024,384]{1,0:T(8,128)(2,1)S(1)}, u32[]{:S(2)}, u32[]{:S(2)}) collective-permute-start(bf16[1024,384]{1,0:T(8,128)(2,1)S(1)} %add_convert_fusion.7), channel_id=1, source_target_pairs={{8,0},{12,4},{16,24},{20,28},{9,1},{13,5},{17,25},{21,29},{10,2},{... | collective-permute-start | bytes 2359304 | tf_op jit(solution)/shard_map/ppermute | solution.py:754
  414.2 35.8 %collective-permute-start.59 = (bf16[384,1536]{1,0:T(8,128)(2,1)S(1)}, bf16[384,1536]{1,0:T(8,128)(2,1)}, u32[]{:S(2)}, u32[]{:S(2)}) collective-permute-start(bf16[384,1536]{1,0:T(8,128)(2,1)S(1)} %broadcast_select_fusion.refs_1_), channel_id=1, source_target_pairs={{0,4},{4,0},{8,12},{12,8},{16,20},{20,16},{24,28},{28,24},{1,5},{5... | collective-permute-start | bytes 3538952 | tf_op jit(solution)/shard_map/ppermute | solution.py:730
  436.5 17.2 %collective-permute-start.46 = (bf16[1536,384]{1,0:T(8,128)(2,1)S(1)}, bf16[1536,384]{1,0:T(8,128)(2,1)}, u32[]{:S(2)}, u32[]{:S(2)}) collective-permute-start(bf16[1536,384]{1,0:T(8,128)(2,1)S(1)} %broadcast_select_fusion.1.refs_1_), channel_id=1, source_target_pairs={{0,4},{4,0},{8,12},{12,8},{16,20},{20,16},{24,28},{28,24},{1,5},{5... | collective-permute-start | bytes 3538952 | tf_op jit(solution)/shard_map/ppermute | solution.py:730
  436.6 2.9 collective-permute-start.27
  437.2 16.5 %collective-permute-start.54 = (bf16[1024,384]{1,0:T(8,128)(2,1)S(1)}, bf16[1024,384]{1,0:T(8,128)(2,1)}, u32[]{:S(2)}, u32[]{:S(2)}) collective-permute-start(bf16[1024,384]{1,0:T(8,128)(2,1)S(1)} %broadcast_select_fusion.2.refs_3_), channel_id=1, source_target_pairs={{0,4},{4,0},{8,12},{12,8},{16,20},{20,16},{24,28},{28,24},{1,5},{5... | collective-permute-start | bytes 2359304 | tf_op jit(solution)/shard_map/ppermute | solution.py:730
  438.1 20.6 %collective-permute-start.38 = (bf16[704,384]{1,0:T(8,128)(2,1)}, bf16[704,384]{1,0:T(8,128)(2,1)}, u32[]{:S(2)}, u32[]{:S(2)}) collective-permute-start(bf16[704,384]{1,0:T(8,128)(2,1)} %broadcast_select_fusion.3.refs_1_), channel_id=1, source_target_pairs={{0,4},{4,0},{8,12},{12,8},{16,20},{20,16},{24,28},{28,24},{1,5},{5... | collective-permute-start | bytes 1622024 | tf_op jit(solution)/shard_map/ppermute | solution.py:730
  439.5 7.1 %collective-permute-start.30 = (f32[168,128]{1,0:T(8,128)S(1)}, f32[168,128]{1,0:T(8,128)S(1)}, u32[]{:S(2)}, u32[]{:S(2)}) collective-permute-start(f32[168,128]{1,0:T(8,128)S(1)} %add_add_fusion), channel_id=1, source_target_pairs={{0,16},{4,20},{8,24},{12,28},{16,0},{20,4},{24,8},{28,12},{1,17},{... | collective-permute-start | bytes 258056 | tf_op jit(solution)/shard_map/ppermute | solution.py:730
  (83 other events, 794.4 us)
